TPU v7x, 32 devices: a whole 2x2x4 slice. The times are simulated.
32 devices in a mesh: tm: 4 (over y, x), row: 4 (over z), col: 2 (over core).
Axes of the slice: x: 2, y: 2, z: 4, core: 2. Of those that a mesh axis runs over, the one named last changes fastest.
Arguments:
- features: bfloat16 [8, 16, 20, 384], P('tm', 'row', 'col'), may hold values from -6 to 6
- reward_grad: bfloat16 [8, 16, 20, 384], P('tm', 'row', 'col'), may hold values from -6 to 6
- first_kernel: bfloat16 [3, 3, 3, 384, 384], P(None, None, None, 'tm'), may hold values from -0.0625 to 0.0625
- second_kernel: bfloat16 [3, 3, 3, 384, 384], P(None, None, None, 'tm'), may hold values from -0.0625 to 0.0625
- first_gain: float32 [384], replicated, may hold values from 0.25 to 1.75
- second_gain: float32 [384], replicated, may hold values from 0.25 to 1.75
- first_bias: float32 [384], replicated, may hold values from -3 to 3
Outputs:
- input_grad: bfloat16 [8, 16, 20, 384], P('tm', 'row', 'col')
All inputs are finite; a program needn't handle non-finite values.
Results may differ from a plain program's by a relative error of at most 0.0037.
Values may be sent and summed in bfloat16 or wider, within the bound.
No kernel may reach another device: no remote copies, remote signals or barrier semaphores. Data moves between devices by JAX's collectives and lax.ppermute only.
A program may use at most 128 MiB of HBM per device.

v0:
```python
import jax
import jax.numpy as jnp
from jax import lax
from jax.sharding import PartitionSpec as P

epsilon = 1e-06


def passed_along(value, axis, steps):
    count = lax.axis_size(axis)
    initial, last = (max(0, -steps), min(count, count - steps))
    return lax.ppermute(value, axis, [(source, source + steps) for source in range(initial, last)])


def padded(cells, sides, width):
    for axis, dim in sides:
        count = lax.axis_size(axis)
        ends = count - 1
        head = lax.slice_in_dim(cells, 0, width, axis=dim)
        tail = lax.slice_in_dim(cells, cells.shape[dim] - width, cells.shape[dim], axis=dim)
        cells = jnp.concatenate(
            [
                lax.ppermute(tail, axis, [(i, (i + 1) % count) for i in range(ends)]),
                cells,
                lax.ppermute(head, axis, [((i + 1) % count, i) for i in range(ends)]),
            ],
            axis=dim,
        )
    return cells


def rms_parts(values, gain):
    inv_rms = lax.rsqrt(jnp.mean(values * values, axis=-1, keepdims=True) + epsilon)
    normed = values * inv_rms
    return (inv_rms, normed, normed * gain)


def silu_slope(values):
    sigmoid_val = jax.nn.sigmoid(values)
    return sigmoid_val * (1.0 + values * (1.0 - sigmoid_val))


def rms_back(cotangent, inv_rms, normed, gain):
    scaled_grad = cotangent * gain
    return inv_rms * (scaled_grad - normed * jnp.mean(normed * scaled_grad, axis=-1, keepdims=True))


def conv_causal(plane, kernel, frame_count, row_count, col_count):
    channels = plane.shape[3]
    summed = jnp.zeros((frame_count * row_count * col_count, kernel.shape[4]), jnp.float32)
    for step_t in range(3):
        for step_h in range(3):
            for step_w in range(3):
                window = plane[
                    step_t : step_t + frame_count,
                    step_h : step_h + row_count,
                    step_w : step_w + col_count,
                ]
                summed = summed + jnp.dot(
                    window.reshape(-1, channels),
                    kernel[step_t, step_h, step_w],
                    preferred_element_type=jnp.float32,
                )
    return summed


def conv_transposed(plane, kernel, frame_count, row_count, col_count):
    channels = plane.shape[3]
    summed = jnp.zeros((frame_count * row_count * col_count, kernel.shape[3]), jnp.float32)
    for step_t in range(3):
        for step_h in range(3):
            for step_w in range(3):
                window = plane[
                    2 - step_t : 2 - step_t + frame_count,
                    2 - step_h : 2 - step_h + row_count,
                    2 - step_w : 2 - step_w + col_count,
                ]
                summed = summed + jnp.dot(
                    window.reshape(-1, channels),
                    kernel[step_t, step_h, step_w].T,
                    preferred_element_type=jnp.float32,
                )
    return summed


def later_frames(block):
    return passed_along(block, "tm", -1)


def plane_edges(stacked):
    return padded(stacked, (("row", 2), ("col", 3)), 1)


def on_device(
    features, reward_grad, first_kernel, second_kernel, first_gain, second_gain, first_bias
):
    frame_count, row_count, col_count, channels = features.shape
    earlier = passed_along(features, "tm", 1)
    input_ext = jnp.concatenate([earlier, features], axis=0)
    reward_ext = jnp.concatenate([reward_grad, later_frames(reward_grad)], axis=0)
    planes = plane_edges(jnp.stack([input_ext, reward_ext]))
    input_plane = planes[0]
    reward_plane = planes[1]
    inv_plane, normed_plane, act_plane = rms_parts(input_plane.astype(jnp.float32), first_gain)
    silu_plane = jax.nn.silu(act_plane).astype(jnp.bfloat16)
    inv_one = inv_plane[2:, 1:-1, 1:-1].reshape(-1, 1)
    normed_one = normed_plane[2:, 1:-1, 1:-1].reshape(-1, channels)
    act_one = act_plane[2:, 1:-1, 1:-1].reshape(-1, channels)
    kernel_one = lax.all_gather(first_kernel, "tm", axis=3, tiled=True)
    second_back = conv_transposed(
        reward_plane,
        lax.all_gather(second_kernel, "tm", axis=3, tiled=True),
        frame_count,
        row_count,
        col_count,
    )
    hidden = conv_causal(silu_plane, kernel_one, frame_count, row_count, col_count) + first_bias
    inv_two, normed_two, act_two = rms_parts(hidden, second_gain)
    hidden_grad = rms_back(
        second_back * silu_slope(act_two), inv_two, normed_two, second_gain
    ).astype(jnp.bfloat16)
    hidden_grad = hidden_grad.reshape(frame_count, row_count, col_count, channels)
    hidden_ext = jnp.concatenate([hidden_grad, later_frames(hidden_grad)], axis=0)
    hidden_plane = plane_edges(hidden_ext[None])[0]
    first_back = conv_transposed(hidden_plane, kernel_one, frame_count, row_count, col_count)
    result = rms_back(first_back * silu_slope(act_one), inv_one, normed_one, first_gain)
    result = result + reward_grad.reshape(-1, channels).astype(jnp.float32)
    return result.astype(jnp.bfloat16).reshape(frame_count, row_count, col_count, channels)


def solution(mesh):
    in_specs = (
        P("tm", "row", "col", None),
        P("tm", "row", "col", None),
        P(None, None, None, "tm", None),
        P(None, None, None, "tm", None),
        P(),
        P(),
        P(),
    )
    out_specs = P("tm", "row", "col", None)
    return jax.shard_map(
        on_device, mesh=mesh, in_specs=in_specs, out_specs=out_specs, check_vma=False
    )
```

profile of v0, /device:TPU:8, one launch (start us, length us, event | category | flops | bytes accessed | tf_op | source)
XLA Modules:
  0.0 275.7 jit_solution(18031163939670144844)
XLA Ops:
  8.0 3.4 %collective-permute-start = (bf16[2,4,10,384]{3,1,2,0:T(4,128)(2,1)}, bf16[2,4,10,384]{3,1,2,0:T(4,128)(2,1)S(1)}, u32[]{:S(2)}, u32[]{:S(2)}) collective-permute-start(bf16[2,4,10,384]{3,1,2,0:T(4,128)(2,1)} %param.7), channel_id=1, source_target_pairs={{0,8},{8,16},{16,24},{1,9},{9,17},{17,25},{2,10},{10,18},{18,26},{... | collective-permute-start | bytes 184328 | tf_op jit(solution)/shard_map/ppermute | solution.py:12
  11.4 1.3 collective-permute-start.1
  14.5 3.2 %collective-permute-done.1 = bf16[2,4,10,384]{3,1,2,0:T(4,128)(2,1)S(1)} collective-permute-done((bf16[2,4,10,384]{3,1,2,0:T(4,128)(2,1)}, bf16[2,4,10,384]{3,1,2,0:T(4,128)(2,1)S(1)}, u32[]{:S(2)}, u32[]{:S(2)}) %collective-permute-start.1) | collective-permute-done | bytes 61472 | tf_op jit(solution)/shard_map/ppermute | solution.py:12
  18.9 2.4 collective-permute-start.3
  21.2 3.5 %collective-permute-start.2 = (bf16[2,4,1,10,384]{4,2,3,1,0:T(2,128)(2,1)S(1)}, bf16[2,4,1,10,384]{4,2,3,1,0:T(2,128)(2,1)S(1)}, u32[]{:S(2)}, u32[]{:S(2)}) collective-permute-start(bf16[2,4,1,10,384]{4,2,3,1,0:T(2,128)(2,1)S(1)} %get-tuple-element.93), channel_id=1, source_target_pairs={{0,2},{2,4},{4,6},{1,3},{3,5},{5,7},{8,10},{10,12},{12,14},{9,11},... | collective-permute-start | bytes 184328 | tf_op jit(solution)/shard_map/ppermute | solution.py:23
  25.7 2.4 collective-permute-done.2
  28.1 1.3 collective-permute-start.5
  29.4 3.0 %collective-permute-start.4 = (bf16[2,4,6,1,384]{4,2,3,1,0:T(8,128)(2,1)S(1)}, bf16[2,4,6,1,384]{4,2,3,1,0:T(8,128)(2,1)S(1)}, u32[]{:S(2)}, u32[]{:S(2)}) collective-permute-start(bf16[2,4,6,1,384]{4,2,3,1,0:T(8,128)(2,1)S(1)} %get-tuple-element.8), channel_id=1, source_target_pairs={{0,1},{2,3},{4,5},{6,7},{8,9},{10,11},{12,13},{14,15},{16,17},{18,... | collective-permute-start | bytes 110600 | tf_op jit(solution)/shard_map/ppermute | solution.py:23
  44.3 1.2 fusion.15
  69.9 24.4 %all-gather.3.cloned.1.call-done = bf16[3,3,3,384,384]{4,3,2,1,0:T(8,128)(2,1)} async-done(((bf16[3,3,3,96,384]{4,3,2,1,0:T(8,128)(2,1)}), bf16[3,3,3,384,384]{4,3,2,1,0:T(8,128)(2,1)}) %all-gather.3.cloned.1.call-update) | async-done | bytes 7962640 | tf_op jit(solution)/shard_map/all_gather | solution.py:109
  103.7 1.2 convolution_add_fusion.70
  107.3 1.3 convolution_add_fusion.67
  125.4 1.3 multiply_reduce_fusion.2
  126.7 53.4 %all-gather.5.cloned.1.call-done = bf16[3,3,3,384,384]{4,3,2,1,0:T(8,128)(2,1)} async-done(((bf16[3,3,3,96,384]{4,3,2,1,0:T(8,128)(2,1)}), bf16[3,3,3,384,384]{4,3,2,1,0:T(8,128)(2,1)}) %all-gather.5.cloned.1.call-update) | async-done | bytes 7962640 | tf_op jit(solution)/shard_map/all_gather | solution.py:112
  181.3 1.2 convolution_add_fusion.51
  183.7 1.2 convolution_add_fusion.49
  185.0 1.2 convolution_add_fusion.48
  188.6 1.2 convolution_add_fusion.45
  189.9 1.2 convolution_add_fusion.44
  194.7 1.2 convolution_add_fusion.40
  197.2 1.2 convolution_add_fusion.38
  198.4 1.2 convolution_add_fusion.37
  203.3 1.2 convolution_add_fusion.33
  207.0 1.2 convolution_add_fusion.30
  209.4 1.2 convolution_add_fusion.28
  211.9 1.3 multiply_reduce_fusion.1
  213.4 1.3 collective-permute-start.6
  214.7 5.2 %collective-permute-done.6 = bf16[2,4,10,384]{3,2,1,0:T(8,128)(2,1)S(1)} collective-permute-done((bf16[2,4,10,384]{3,2,1,0:T(8,128)(2,1)S(1)}, bf16[2,4,10,384]{3,2,1,0:T(8,128)(2,1)S(1)}, u32[]{:S(2)}, u32[]{:S(2)}) %collective-permute-start.6) | collective-permute-done | bytes 61472 | tf_op jit(solution)/shard_map/ppermute | solution.py:12
  219.9 2.5 collective-permute-start.8
  222.4 3.4 %collective-permute-start.7 = (bf16[1,4,1,10,384]{4,3,2,1,0:T(8,128)(2,1)S(1)}, bf16[1,4,1,10,384]{4,3,2,1,0:T(8,128)(2,1)S(1)}, u32[]{:S(2)}, u32[]{:S(2)}) collective-permute-start(bf16[1,4,1,10,384]{4,3,2,1,0:T(8,128)(2,1)S(1)} %get-tuple-element.95), channel_id=1, source_target_pairs={{0,2},{2,4},{4,6},{1,3},{3,5},{5,7},{8,10},{10,12},{12,14},{9,11},... | collective-permute-start | bytes 92168 | tf_op jit(solution)/shard_map/ppermute | solution.py:23
  225.9 2.5 collective-permute-done.7
  228.4 1.3 collective-permute-start.10
  229.7 3.2 %collective-permute-start.9 = (bf16[1,4,6,1,384]{4,3,2,1,0:T(2,128)(2,1)S(1)}, bf16[1,4,6,1,384]{4,3,2,1,0:T(2,128)(2,1)S(1)}, u32[]{:S(2)}, u32[]{:S(2)}) collective-permute-start(bf16[1,4,6,1,384]{4,3,2,1,0:T(2,128)(2,1)S(1)} %get-tuple-element.37), channel_id=1, source_target_pairs={{0,1},{2,3},{4,5},{6,7},{8,9},{10,11},{12,13},{14,15},{16,17},{18,... | collective-permute-start | bytes 55304 | tf_op jit(solution)/shard_map/ppermute | solution.py:23
  237.6 1.2 convolution_add_fusion.24
  238.8 1.2 convolution_add_fusion.23
  241.2 1.2 convolution_add_fusion.21
  242.4 1.2 convolution_add_fusion.20
  244.9 1.2 convolution_add_fusion.18
  246.1 1.2 convolution_add_fusion.17
  248.5 1.2 convolution_add_fusion.15
  249.7 1.2 convolution_add_fusion.14
  252.1 1.2 convolution_add_fusion.12
  253.4 1.2 convolution_add_fusion.11
  255.8 1.2 convolution_add_fusion.9
  261.9 1.2 convolution_add_fusion.4
  264.3 1.2 convolution_add_fusion.2
  265.5 1.2 convolution_add_fusion.1
  266.7 1.3 multiply_reduce_fusion
  (280 shorter events, 104.8 us)
Async XLA Ops:
  6.5 87.8 %all-gather.3.cloned.1.call-start = ((), (), s32[]{:S(2)}) async-start(), calls=%async_computation | async-start | bytes 9953280 | tf_op jit(solution)/shard_map/all_gather | solution.py:109
  7.3 172.9 %all-gather.5.cloned.1.call-start = ((), (), s32[]{:S(2)}) async-start(), calls=%async_computation.1 | async-start | bytes 9953280 | tf_op jit(solution)/shard_map/all_gather | solution.py:112
  8.0 5.6 %collective-permute-start = (bf16[2,4,10,384]{3,1,2,0:T(4,128)(2,1)}, bf16[2,4,10,384]{3,1,2,0:T(4,128)(2,1)S(1)}, u32[]{:S(2)}, u32[]{:S(2)}) collective-permute-start(bf16[2,4,10,384]{3,1,2,0:T(4,128)(2,1)} %param.7), channel_id=1, source_target_pairs={{0,8},{8,16},{16,24},{1,9},{9,17},{17,25},{2,10},{10,18},{18,26},{... | collective-permute-start | bytes 184328 | tf_op jit(solution)/shard_map/ppermute | solution.py:12
  11.4 6.3 %collective-permute-start.1 = (bf16[2,4,10,384]{3,1,2,0:T(4,128)(2,1)}, bf16[2,4,10,384]{3,1,2,0:T(4,128)(2,1)S(1)}, u32[]{:S(2)}, u32[]{:S(2)}) collective-permute-start(bf16[2,4,10,384]{3,1,2,0:T(4,128)(2,1)} %param.8), channel_id=1, source_target_pairs={{8,0},{16,8},{24,16},{9,1},{17,9},{25,17},{10,2},{18,10},{26,18},{... | collective-permute-start | bytes 184328 | tf_op jit(solution)/shard_map/ppermute | solution.py:12
  18.9 6.8 %collective-permute-start.3 = (bf16[2,4,1,10,384]{4,2,3,1,0:T(2,128)(2,1)S(1)}, bf16[2,4,1,10,384]{4,2,3,1,0:T(2,128)(2,1)S(1)}, u32[]{:S(2)}, u32[]{:S(2)}) collective-permute-start(bf16[2,4,1,10,384]{4,2,3,1,0:T(2,128)(2,1)S(1)} %get-tuple-element.94), channel_id=1, source_target_pairs={{2,0},{4,2},{6,4},{3,1},{5,3},{7,5},{10,8},{12,10},{14,12},{11,9},... | collective-permute-start | bytes 184328 | tf_op jit(solution)/shard_map/ppermute | solution.py:25
  21.2 6.8 %collective-permute-start.2 = (bf16[2,4,1,10,384]{4,2,3,1,0:T(2,128)(2,1)S(1)}, bf16[2,4,1,10,384]{4,2,3,1,0:T(2,128)(2,1)S(1)}, u32[]{:S(2)}, u32[]{:S(2)}) collective-permute-start(bf16[2,4,1,10,384]{4,2,3,1,0:T(2,128)(2,1)S(1)} %get-tuple-element.93), channel_id=1, source_target_pairs={{0,2},{2,4},{4,6},{1,3},{3,5},{5,7},{8,10},{10,12},{12,14},{9,11},... | collective-permute-start | bytes 184328 | tf_op jit(solution)/shard_map/ppermute | solution.py:23
  28.1 4.3 %collective-permute-start.5 = (bf16[2,4,6,1,384]{4,2,3,1,0:T(8,128)(2,1)S(1)}, bf16[2,4,6,1,384]{4,2,3,1,0:T(8,128)(2,1)S(1)}, u32[]{:S(2)}, u32[]{:S(2)}) collective-permute-start(bf16[2,4,6,1,384]{4,2,3,1,0:T(8,128)(2,1)S(1)} %get-tuple-element.9), channel_id=1, source_target_pairs={{1,0},{3,2},{5,4},{7,6},{9,8},{11,10},{13,12},{15,14},{17,16},{19,... | collective-permute-start | bytes 110600 | tf_op jit(solution)/shard_map/ppermute | solution.py:25
  29.4 3.9 %collective-permute-start.4 = (bf16[2,4,6,1,384]{4,2,3,1,0:T(8,128)(2,1)S(1)}, bf16[2,4,6,1,384]{4,2,3,1,0:T(8,128)(2,1)S(1)}, u32[]{:S(2)}, u32[]{:S(2)}) collective-permute-start(bf16[2,4,6,1,384]{4,2,3,1,0:T(8,128)(2,1)S(1)} %get-tuple-element.8), channel_id=1, source_target_pairs={{0,1},{2,3},{4,5},{6,7},{8,9},{10,11},{12,13},{14,15},{16,17},{18,... | collective-permute-start | bytes 110600 | tf_op jit(solution)/shard_map/ppermute | solution.py:23
  63.8 59.1 %copy-start = (bf16[80,384]{1,0:T(8,128)(2,1)S(1)}, bf16[80,384]{1,0:T(8,128)(2,1)}, u32[]{:S(2)}) copy-start(bf16[80,384]{1,0:T(8,128)(2,1)} %reshape.327) | copy-start | bytes 184324
  66.8 57.3 %copy-start.1 = (bf16[80,384]{1,0:T(8,128)(2,1)S(1)}, bf16[80,384]{1,0:T(8,128)(2,1)}, u32[]{:S(2)}) copy-start(bf16[80,384]{1,0:T(8,128)(2,1)} %reshape.328) | copy-start | bytes 184324
  69.8 55.5 %copy-start.20 = (f32[384]{0:T(512)S(1)}, f32[384]{0:T(512)}, u32[]{:S(2)}) copy-start(f32[384]{0:T(512)} %param.13) | copy-start | bytes 4612
  69.9 110.2 %copy-start.18 = (bf16[80,384]{1,0:T(8,128)(2,1)S(1)}, bf16[80,384]{1,0:T(8,128)(2,1)}, u32[]{:S(2)}) copy-start(bf16[80,384]{1,0:T(8,128)(2,1)} %reshape.330) | copy-start | bytes 184324
  107.3 86.2 %copy-start.2 = (bf16[80,384]{1,0:T(8,128)(2,1)S(1)}, bf16[80,384]{1,0:T(8,128)(2,1)}, u32[]{:S(2)}) copy-start(bf16[80,384]{1,0:T(8,128)(2,1)} %reshape.341) | copy-start | bytes 184324
  108.6 86.1 %copy-start.3 = (bf16[80,384]{1,0:T(8,128)(2,1)S(1)}, bf16[80,384]{1,0:T(8,128)(2,1)}, u32[]{:S(2)}) copy-start(bf16[80,384]{1,0:T(8,128)(2,1)} %reshape.342) | copy-start | bytes 184324
  109.8 86.2 %copy-start.4 = (bf16[80,384]{1,0:T(8,128)(2,1)S(1)}, bf16[80,384]{1,0:T(8,128)(2,1)}, u32[]{:S(2)}) copy-start(bf16[80,384]{1,0:T(8,128)(2,1)} %reshape.343) | copy-start | bytes 184324
  111.0 86.2 %copy-start.5 = (bf16[80,384]{1,0:T(8,128)(2,1)S(1)}, bf16[80,384]{1,0:T(8,128)(2,1)}, u32[]{:S(2)}) copy-start(bf16[80,384]{1,0:T(8,128)(2,1)} %reshape.344) | copy-start | bytes 184324
  112.2 86.2 %copy-start.6 = (bf16[80,384]{1,0:T(8,128)(2,1)S(1)}, bf16[80,384]{1,0:T(8,128)(2,1)}, u32[]{:S(2)}) copy-start(bf16[80,384]{1,0:T(8,128)(2,1)} %reshape.345) | copy-start | bytes 184324
  113.4 86.3 %copy-start.7 = (bf16[80,384]{1,0:T(8,128)(2,1)S(1)}, bf16[80,384]{1,0:T(8,128)(2,1)}, u32[]{:S(2)}) copy-start(bf16[80,384]{1,0:T(8,128)(2,1)} %reshape.346) | copy-start | bytes 184324
  114.6 86.3 %copy-start.8 = (bf16[80,384]{1,0:T(8,128)(2,1)S(1)}, bf16[80,384]{1,0:T(8,128)(2,1)}, u32[]{:S(2)}) copy-start(bf16[80,384]{1,0:T(8,128)(2,1)} %reshape.347) | copy-start | bytes 184324
  115.8 86.3 %copy-start.9 = (bf16[80,384]{1,0:T(8,128)(2,1)S(1)}, bf16[80,384]{1,0:T(8,128)(2,1)}, u32[]{:S(2)}) copy-start(bf16[80,384]{1,0:T(8,128)(2,1)} %reshape.348) | copy-start | bytes 184324
  117.0 86.3 %copy-start.10 = (bf16[80,384]{1,0:T(8,128)(2,1)S(1)}, bf16[80,384]{1,0:T(8,128)(2,1)}, u32[]{:S(2)}) copy-start(bf16[80,384]{1,0:T(8,128)(2,1)} %reshape.349) | copy-start | bytes 184324
  118.2 86.4 %copy-start.11 = (bf16[80,384]{1,0:T(8,128)(2,1)S(1)}, bf16[80,384]{1,0:T(8,128)(2,1)}, u32[]{:S(2)}) copy-start(bf16[80,384]{1,0:T(8,128)(2,1)} %reshape.350) | copy-start | bytes 184324
  119.3 86.4 %copy-start.12 = (bf16[80,384]{1,0:T(8,128)(2,1)S(1)}, bf16[80,384]{1,0:T(8,128)(2,1)}, u32[]{:S(2)}) copy-start(bf16[80,384]{1,0:T(8,128)(2,1)} %reshape.351) | copy-start | bytes 184324
  120.5 86.4 %copy-start.13 = (bf16[80,384]{1,0:T(8,128)(2,1)S(1)}, bf16[80,384]{1,0:T(8,128)(2,1)}, u32[]{:S(2)}) copy-start(bf16[80,384]{1,0:T(8,128)(2,1)} %reshape.352) | copy-start | bytes 184324
  121.7 86.5 %copy-start.14 = (bf16[80,384]{1,0:T(8,128)(2,1)S(1)}, bf16[80,384]{1,0:T(8,128)(2,1)}, u32[]{:S(2)}) copy-start(bf16[80,384]{1,0:T(8,128)(2,1)} %reshape.353) | copy-start | bytes 184324
  122.9 86.5 %copy-start.15 = (bf16[80,384]{1,0:T(8,128)(2,1)S(1)}, bf16[80,384]{1,0:T(8,128)(2,1)}, u32[]{:S(2)}) copy-start(bf16[80,384]{1,0:T(8,128)(2,1)} %reshape.354) | copy-start | bytes 184324
  124.1 86.5 %copy-start.16 = (bf16[80,384]{1,0:T(8,128)(2,1)S(1)}, bf16[80,384]{1,0:T(8,128)(2,1)}, u32[]{:S(2)}) copy-start(bf16[80,384]{1,0:T(8,128)(2,1)} %reshape.355) | copy-start | bytes 184324
  125.4 86.5 %copy-start.22 = (f32[384]{0:T(512)S(1)}, f32[384]{0:T(512)}, u32[]{:S(2)}) copy-start(f32[384]{0:T(512)} %param.12) | copy-start | bytes 4612
  185.0 48.0 %copy-start.17 = (bf16[2,4,10,384]{3,1,2,0:T(4,128)(2,1)S(1)}, bf16[2,4,10,384]{3,1,2,0:T(4,128)(2,1)}, u32[]{:S(2)}) copy-start(bf16[2,4,10,384]{3,1,2,0:T(4,128)(2,1)} %param.8) | copy-start | bytes 184324
  189.9 43.4 %copy-start.19 = (f32[4,6,12,1]{1,2,0,3:T(8,128)S(1)}, f32[4,6,12,1]{1,2,0,3:T(8,128)}, u32[]{:S(2)}) copy-start(f32[4,6,12,1]{1,2,0,3:T(8,128)} %get-tuple-element.97) | copy-start | bytes 3460
  213.4 6.5 %collective-permute-start.6 = (bf16[2,4,10,384]{3,2,1,0:T(8,128)(2,1)S(1)}, bf16[2,4,10,384]{3,2,1,0:T(8,128)(2,1)S(1)}, u32[]{:S(2)}, u32[]{:S(2)}) collective-permute-start(bf16[2,4,10,384]{3,2,1,0:T(8,128)(2,1)S(1)} %reshape.357), channel_id=1, source_target_pairs={{8,0},{16,8},{24,16},{9,1},{17,9},{25,17},{10,2},{18,10},{26,18},{... | collective-permute-start | bytes 184328 | tf_op jit(solution)/shard_map/ppermute | solution.py:12
  219.9 6.0 %collective-permute-start.8 = (bf16[1,4,1,10,384]{4,3,2,1,0:T(8,128)(2,1)S(1)}, bf16[1,4,1,10,384]{4,3,2,1,0:T(8,128)(2,1)S(1)}, u32[]{:S(2)}, u32[]{:S(2)}) collective-permute-start(bf16[1,4,1,10,384]{4,3,2,1,0:T(8,128)(2,1)S(1)} %get-tuple-element.96), channel_id=1, source_target_pairs={{2,0},{4,2},{6,4},{3,1},{5,3},{7,5},{10,8},{12,10},{14,12},{11,9},... | collective-permute-start | bytes 92168 | tf_op jit(solution)/shard_map/ppermute | solution.py:25
  222.4 6.0 %collective-permute-start.7 = (bf16[1,4,1,10,384]{4,3,2,1,0:T(8,128)(2,1)S(1)}, bf16[1,4,1,10,384]{4,3,2,1,0:T(8,128)(2,1)S(1)}, u32[]{:S(2)}, u32[]{:S(2)}) collective-permute-start(bf16[1,4,1,10,384]{4,3,2,1,0:T(8,128)(2,1)S(1)} %get-tuple-element.95), channel_id=1, source_target_pairs={{0,2},{2,4},{4,6},{1,3},{3,5},{5,7},{8,10},{10,12},{12,14},{9,11},... | collective-permute-start | bytes 92168 | tf_op jit(solution)/shard_map/ppermute | solution.py:23
  228.4 5.0 %collective-permute-start.10 = (bf16[1,4,6,1,384]{4,3,2,1,0:T(2,128)(2,1)S(1)}, bf16[1,4,6,1,384]{4,3,2,1,0:T(2,128)(2,1)S(1)}, u32[]{:S(2)}, u32[]{:S(2)}) collective-permute-start(bf16[1,4,6,1,384]{4,3,2,1,0:T(2,128)(2,1)S(1)} %get-tuple-element.38), channel_id=1, source_target_pairs={{1,0},{3,2},{5,4},{7,6},{9,8},{11,10},{13,12},{15,14},{17,16},{19,... | collective-permute-start | bytes 55304 | tf_op jit(solution)/shard_map/ppermute | solution.py:25
  229.7 3.9 %collective-permute-start.9 = (bf16[1,4,6,1,384]{4,3,2,1,0:T(2,128)(2,1)S(1)}, bf16[1,4,6,1,384]{4,3,2,1,0:T(2,128)(2,1)S(1)}, u32[]{:S(2)}, u32[]{:S(2)}) collective-permute-start(bf16[1,4,6,1,384]{4,3,2,1,0:T(2,128)(2,1)S(1)} %get-tuple-element.37), channel_id=1, source_target_pairs={{0,1},{2,3},{4,5},{6,7},{8,9},{10,11},{12,13},{14,15},{16,17},{18,... | collective-permute-start | bytes 55304 | tf_op jit(solution)/shard_map/ppermute | solution.py:23
  235.1 31.7 %copy-start.21 = (f32[384]{0:T(512)S(1)}, f32[384]{0:T(512)}, u32[]{:S(2)}) copy-start(f32[384]{0:T(512)} %param.11) | copy-start | bytes 4612
Sparse Core Ops, SparseCore 0:
  9.2 85.0 all-gather.2
  96.1 83.9 all-gather.4
where the time goes:
time: 281 us; the launch traced here: 276 us
  matrix products  97.4 us (35%)
  waiting for transfers between devices  95.4 us (34%)
  local copies, waits for them, and re-layouts  36.2 us (13%)
  starting transfers between devices  26.5 us (9%)
  between operations  15.4 us (5%)
  other arithmetic  4.76 us (2%)
    dot_general x54, matrix products, conv_transposed(): jnp.dot(window.reshape(-1, channels), kernel[step_t, step_h, step_w].T, p...  65.4 us
    all_gather x1, waiting for transfers between devices, on_device(): lax.all_gather(second_kernel, 'tm', axis=3, tiled=True)  53.4 us
    dot_general x27, matrix products, conv_causal(): jnp.dot(window.reshape(-1, channels), kernel[step_t, step_h, step_w], pre...  32 us
    all_gather x1, waiting for transfers between devices, on_device(): kernel_one = lax.all_gather(first_kernel, 'tm', axis=3, tiled=True)  24.4 us
    slice x31, local copies, waits for them, and re-layouts, conv_transposed(): plane[2 - step_t:2 - step_t + frame_count, 2 - step_h:2 - step_h + row_co...  16.2 us
    ppermute x4, starting transfers between devices, padded(): lax.ppermute(tail, axis, [(i, (i + 1) % count) for i in range(ends)])  13.1 us
    reshape x54, local copies, waits for them, and re-layouts, conv_transposed(): window.reshape(-1, channels)  11.5 us
    ppermute x3, waiting for transfers between devices, passed_along(): lax.ppermute(value, axis, [(source, source + steps) for source in range(i...  9.32 us
  transfers between devices with their start and end apart: 13, of which 11 were waited for; matrix products, arithmetic and copies ran while one was open for 26% of the time, Pallas kernels for 0%

commit v1 on v0

v1 whole, which is shorter than its diff:
```python
import functools

import jax
import jax.numpy as jnp
from jax import lax
from jax.experimental import pallas as pl
from jax.experimental.pallas import tpu as pltpu
from jax.sharding import PartitionSpec as P

epsilon = 1e-06
f32 = jnp.float32
bf16 = jnp.bfloat16
lanes = 128


def is_power(count):
    return count & (count - 1) == 0


def sent_to(index, step, count):
    return index ^ step if is_power(count) else lax.rem(index + step, count)


def got_from(index, step, count):
    return index ^ step if is_power(count) else lax.rem(index + count - step, count)


def tm_exchange(blocks):
    count = len(blocks)
    got = [blocks[0]]
    for step in range(1, count):
        pairs = [
            (i, i ^ step if is_power(count) else (i + step) % count) for i in range(count)
        ]
        got.append(lax.ppermute(blocks[step], "tm", pairs))
    return got


def halo_pair(low_edge, high_edge, axis):
    count = lax.axis_size(axis)
    if count == 1:
        return jnp.zeros_like(high_edge), jnp.zeros_like(low_edge)
    even = lax.axis_index(axis) % 2 == 0
    first = [(i, i + 1) for i in range(0, count - 1, 2)]
    second = [(i, i + 1) for i in range(1, count - 1, 2)]
    swap = lambda pairs: [(a, b) for a, b in pairs] + [(b, a) for a, b in pairs]
    in_first = lax.ppermute(jnp.where(even, high_edge, low_edge), axis, swap(first))
    if second:
        in_second = lax.ppermute(jnp.where(even, low_edge, high_edge), axis, swap(second))
    else:
        in_second = jnp.zeros_like(in_first)
    return jnp.where(even, in_second, in_first), jnp.where(even, in_first, in_second)


def with_halo(cells):
    row_dim, col_dim = cells.ndim - 3, cells.ndim - 2
    for axis, dim in (("col", col_dim), ("row", row_dim)):
        size = cells.shape[dim]
        low, high = halo_pair(
            lax.slice_in_dim(cells, 0, 1, axis=dim),
            lax.slice_in_dim(cells, size - 1, size, axis=dim),
            axis,
        )
        cells = jnp.concatenate([low, cells, high], axis=dim)
    return cells.reshape(cells.shape[:row_dim] + (-1, cells.shape[-1]))


def rms_parts(values, gain):
    inv_rms = lax.rsqrt(jnp.mean(values * values, axis=-1, keepdims=True) + epsilon)
    normed = values * inv_rms
    return inv_rms, normed, normed * gain


def silu_slope(values):
    sigmoid_val = jax.nn.sigmoid(values)
    return sigmoid_val * (1.0 + values * (1.0 - sigmoid_val))


def rms_back(cotangent, inv_rms, normed, gain):
    scaled_grad = cotangent * gain
    return inv_rms * (scaled_grad - normed * jnp.mean(normed * scaled_grad, axis=-1, keepdims=True))


def slot_matrix(slot, width, channels, wide):
    row = lax.broadcasted_iota(jnp.int32, (channels, wide), 0)
    col = lax.broadcasted_iota(jnp.int32, (channels, wide), 1)
    hit = (row == col + slot * width) & (col < width)
    return jnp.where(hit, 1.0, 0.0).astype(bf16)


def spread_matrix(slot, width, channels, wide):
    row = lax.broadcasted_iota(jnp.int32, (wide, channels), 0)
    col = lax.broadcasted_iota(jnp.int32, (wide, channels), 1)
    hit = (col == row + slot * width) & (row < width)
    return jnp.where(hit, 1.0, 0.0).astype(bf16)


def pack_kernel(peers, width, feat_ref, reward_ref, gain_ref, *out_refs):
    me = lax.axis_index("tm")
    frames, _, channels = feat_ref.shape
    wide = out_refs[0].shape[2] - channels
    for frame in range(frames):
        values = feat_ref[frame].astype(f32)
        act = rms_parts(values, gain_ref[...])[2]
        silu = (act * jax.nn.sigmoid(act)).astype(bf16)
        for step in range(peers):
            slot = sent_to(me, step, peers)
            piece = jnp.dot(
                silu, slot_matrix(slot, width, channels, wide), preferred_element_type=f32
            )
            out_refs[step][frame, :, :channels] = reward_ref[frame]
            out_refs[step][frame, :, channels:] = piece.astype(bf16)


def lay_frames(peers, frames, block_refs, cells_ref):
    me = lax.axis_index("tm")
    total = peers * frames
    for step in range(peers):
        source = got_from(me, step, peers)
        for frame in range(frames):
            for tile in range(cells_ref.shape[0]):
                piece = block_refs[step][frame, :, tile * lanes : (tile + 1) * lanes]
                place = pl.ds(source * frames + frame, piece.shape[0], stride=total)
                cells_ref[tile, place, :] = piece.astype(f32)


def shifted(values, ahead):
    total = values.shape[1]
    if ahead == 0:
        return values
    frame = lax.broadcasted_iota(jnp.int32, values.shape, 1)
    moved = pltpu.roll(values, (-ahead) % total, 1)
    keep = frame < total - ahead if ahead > 0 else frame >= -ahead
    return jnp.where(keep, moved, 0.0)


def lay_taps(cells_ref, taps_ref, first, count, total, aheads):
    plane_rows = taps_ref.shape[0]
    cols = taps_ref.shape[1] // total
    span = (cols + 2) * total

    @pl.loop(0, plane_rows)
    def _(row):
        base = pl.multiple_of(row * span, total)
        for tile in range(count):
            values = cells_ref[first + tile, pl.ds(base, span), :]
            values = values.reshape(cols + 2, total, lanes)
            for at, ahead in enumerate(aheads):
                moved = shifted(values, ahead)
                for step_w in range(3):
                    k = ((at * 3 + step_w) * count + tile) * lanes
                    taps_ref[row, :, k : k + lanes] = (
                        moved[step_w : step_w + cols].reshape(cols * total, lanes).astype(bf16)
                    )


def conv_rows(taps_ref, weight_ref, rows):
    summed = None
    for step_h in range(3):
        left = taps_ref[step_h : step_h + rows].reshape(-1, taps_ref.shape[2])
        part = jnp.dot(left, weight_ref[step_h], preferred_element_type=f32)
        summed = part if summed is None else summed + part
    return summed


def hand_out(peers, frames, total, sum_ref, out_refs, start):
    me = lax.axis_index("tm")
    for step in range(peers):
        target = sent_to(me, step, peers)
        for frame in range(frames):
            place = pl.ds(target * frames + frame, out_refs[step].shape[1], stride=total)
            for tile in range(sum_ref.shape[0]):
                at = start + tile * lanes
                out_refs[step][frame, :, at : at + lanes] = sum_ref[tile, place, :].astype(bf16)


def put(sum_ref, values):
    for tile in range(sum_ref.shape[0]):
        sum_ref[tile] = values[:, tile * lanes : (tile + 1) * lanes]


def both_kernel(peers, frames, rows, channels, *refs):
    blocks = refs[:peers]
    weight_one, weight_two = refs[peers : peers + 2]
    outs = refs[peers + 2 : 2 * peers + 2]
    cells, taps_silu, taps_reward, sum_one, sum_two = refs[2 * peers + 2 :]
    total = peers * frames
    lay_frames(peers, frames, blocks, cells)
    tiles = channels // lanes
    lay_taps(cells, taps_silu, tiles, cells.shape[0] - tiles, total, (-2, -1, 0))
    put(sum_one, conv_rows(taps_silu, weight_one, rows))
    hand_out(peers, frames, total, sum_one, outs, 0)
    lay_taps(cells, taps_reward, 0, tiles, total, (0, 1, 2))
    put(sum_two, conv_rows(taps_reward, weight_two, rows))
    hand_out(peers, frames, total, sum_two, outs, channels)


def back_kernel(peers, frames, rows, *refs):
    blocks = refs[:peers]
    weight = refs[peers]
    outs = refs[peers + 1 : 2 * peers + 1]
    cells, taps, sums = refs[2 * peers + 1 :]
    total = peers * frames
    lay_frames(peers, frames, blocks, cells)
    lay_taps(cells, taps, 0, cells.shape[0], total, (0, 1, 2))
    put(sums, conv_rows(taps, weight, rows))
    hand_out(peers, frames, total, sums, outs, 0)


def gathered(peers, frame, block_refs, start, width, channels):
    me = lax.axis_index("tm")
    wide = block_refs[0].shape[2] - start
    summed = None
    for step in range(peers):
        spread = spread_matrix(got_from(me, step, peers), width, channels, wide)
        part = jnp.dot(
            block_refs[step][frame, :, start:], spread, preferred_element_type=f32
        )
        summed = part if summed is None else summed + part
    return summed


def middle_kernel(peers, width, *refs):
    blocks = refs[:peers]
    gain_ref, bias_ref, out_ref = refs[peers:]
    frames, _, channels = out_ref.shape
    for frame in range(frames):
        hidden = blocks[0][frame, :, :channels].astype(f32)
        for step in range(1, peers):
            hidden = hidden + blocks[step][frame, :, :channels].astype(f32)
        hidden = hidden + bias_ref[...]
        back = gathered(peers, frame, blocks, channels, width, channels)
        inv, normed, act = rms_parts(hidden, gain_ref[...])
        out_ref[frame] = rms_back(back * silu_slope(act), inv, normed, gain_ref[...]).astype(bf16)


def final_kernel(peers, width, *refs):
    blocks = refs[:peers]
    feat_ref, reward_ref, gain_ref, out_ref = refs[peers:]
    frames, _, channels = out_ref.shape
    for frame in range(frames):
        back = gathered(peers, frame, blocks, 0, width, channels)
        inv, normed, act = rms_parts(feat_ref[frame].astype(f32), gain_ref[...])
        result = rms_back(back * silu_slope(act), inv, normed, gain_ref[...])
        out_ref[frame] = (result + reward_ref[frame].astype(f32)).astype(bf16)


def call(kernel, outs, scratch=(), flops=0, name=None):
    moved = sum(s.size * s.dtype.itemsize for s in outs)
    return pl.pallas_call(
        kernel,
        out_shape=outs,
        scratch_shapes=list(scratch),
        cost_estimate=pl.CostEstimate(flops=flops, bytes_accessed=moved, transcendentals=0),
        name=name,
    )


def on_device(
    features, reward_grad, first_kernel, second_kernel, first_gain, second_gain, first_bias
):
    peers = lax.axis_size("tm")
    frames, rows, cols, channels = features.shape
    width = first_kernel.shape[3]
    wide = -(-width // lanes) * lanes
    total = peers * frames
    plane = (rows + 2) * (cols + 2)
    count = rows * cols
    struct = jax.ShapeDtypeStruct
    gain_one, gain_two = first_gain[None], second_gain[None]

    def turned(kernel):
        kernel = kernel[::-1, ::-1, ::-1].transpose(1, 0, 2, 4, 3)
        kernel = jnp.pad(kernel, ((0, 0),) * 4 + ((0, wide - width),))
        return kernel.reshape(3, 9 * channels, wide)

    weight_one = jnp.pad(
        first_kernel.transpose(1, 0, 2, 3, 4), ((0, 0),) * 3 + ((0, wide - width), (0, 0))
    ).reshape(3, 9 * wide, channels)
    weight_two = turned(second_kernel)
    weight_back = turned(first_kernel)

    planes = with_halo(jnp.stack([features, reward_grad]))
    packed = call(
        functools.partial(pack_kernel, peers, width),
        [struct((frames, plane, channels + wide), bf16)] * peers,
        name="pack",
    )(planes[0], planes[1], gain_one)
    got = tm_exchange(packed)
    flops = 2 * 27 * width * channels * total * count
    sums = call(
        functools.partial(both_kernel, peers, frames, rows, channels),
        [struct((frames, count, channels + wide), bf16)] * peers,
        [
            pltpu.VMEM(((channels + wide) // lanes, plane * total, lanes), f32),
            pltpu.VMEM((rows + 2, cols * total, 9 * wide), bf16),
            pltpu.VMEM((rows + 2, cols * total, 9 * channels), bf16),
            pltpu.VMEM((channels // lanes, count * total, lanes), f32),
            pltpu.VMEM((wide // lanes, count * total, lanes), f32),
        ],
        2 * flops,
        name="both",
    )(*got, weight_one, weight_two)
    got = tm_exchange(sums)
    hidden_grad = call(
        functools.partial(middle_kernel, peers, width),
        [struct((frames, count, channels), bf16)],
        name="middle",
    )(*got, gain_two, first_bias[None])[0]
    hidden_plane = with_halo(hidden_grad.reshape(features.shape))
    got = tm_exchange([hidden_plane] * peers)
    backs = call(
        functools.partial(back_kernel, peers, frames, rows),
        [struct((frames, count, wide), bf16)] * peers,
        [
            pltpu.VMEM((channels // lanes, plane * total, lanes), f32),
            pltpu.VMEM((rows + 2, cols * total, 9 * channels), bf16),
            pltpu.VMEM((wide // lanes, count * total, lanes), f32),
        ],
        flops,
        name="back",
    )(*got, weight_back)
    got = tm_exchange(backs)
    flat = (frames, count, channels)
    result = call(
        functools.partial(final_kernel, peers, width), [struct(flat, bf16)], name="final"
    )(*got, features.reshape(flat), reward_grad.reshape(flat), gain_one)[0]
    return result.reshape(features.shape)


def solution(mesh):
    in_specs = (
        P("tm", "row", "col", None),
        P("tm", "row", "col", None),
        P(None, None, None, "tm", None),
        P(None, None, None, "tm", None),
        P(),
        P(),
        P(),
    )
    out_specs = P("tm", "row", "col", None)
    return jax.shard_map(
        on_device, mesh=mesh, in_specs=in_specs, out_specs=out_specs, check_vma=False
    )
```

time: 281 us -> 86.3 us (0.31); the launches traced: 276 us -> 85.6 us
  matrix products: 97.4 us -> 0 us
  waiting for transfers between devices: 95.4 us -> 13.5 us
  Pallas kernels: 0 us -> 20.3 us
  between operations: 15.4 us -> 0.32 us
  local copies, waits for them, and re-layouts: 36.2 us -> 27.6 us
  starting transfers between devices: 26.5 us -> 20.3 us
    dot_general x81 -> x0, matrix products: 97.4 us -> none  [the longest x54 65.4 us: conv_transposed(): jnp.dot(window.reshape(-1, channels), kernel[step_t, step_h, step_w].T, p...]
    all_gather x2 -> x0, waiting for transfers between devices: 77.8 us -> none  [the longest x1 53.4 us: on_device(): lax.all_gather(second_kernel, 'tm', axis=3, tiled=True)]
    pallas_call x0 -> x5, Pallas kernels: none -> 20.3 us  [the longest x1 8.97 us: on_device(): call(functools.partial(both_kernel, peers, frames, rows, channels), [stru...]
    slice x67 -> x3, local copies, waits for them, and re-layouts: 20.4 us -> 0.21 us  [the longest x2 0.12 us: on_device(): planes[1]]
    reshape x86 -> x4, local copies, waits for them, and re-layouts: 15.5 us -> 1.92 us  [the longest x1 0.65 us: on_device(): return result.reshape(features.shape)]
    unnamed x46 -> x43, local copies, waits for them, and re-layouts: 0.1 us -> 10.7 us
    pad x0 -> x3, local copies, waits for them, and re-layouts: none -> 6.3 us  [the longest x2 4.33 us: turned(): kernel = jnp.pad(kernel, ((0, 0),) * 4 + ((0, wide - width),))]
    ppermute x11 -> x18, starting transfers between devices: 26.5 us -> 20.3 us  [the longest x12 14 us: tm_exchange(): got.append(lax.ppermute(blocks[step], 'tm', pairs))]
  transfers between devices with their start and end apart: 13 -> 18, of which waited for: 11 -> 10; matrix products, arithmetic and copies ran while one was open for 26% -> 25% of each run, Pallas kernels for 0% -> 0%
where the time goes in v1:
time: 86.3 us; the launch traced here: 85.6 us
  local copies, waits for them, and re-layouts  27.6 us (32%)
  starting transfers between devices  20.3 us (24%)
  Pallas kernels  20.3 us (24%)
  waiting for transfers between devices  13.5 us (16%)
  other arithmetic  3.66 us (4%)
    ppermute x12, starting transfers between devices, tm_exchange(): got.append(lax.ppermute(blocks[step], 'tm', pairs))  14 us
    unnamed x43, local copies, waits for them, and re-layouts  10.7 us
    pallas_call x1, Pallas kernels, on_device(): call(functools.partial(both_kernel, peers, frames, rows, channels), [stru...  8.97 us
    ppermute x2, starting transfers between devices, halo_pair(): lax.ppermute(jnp.where(even, low_edge, high_edge), axis, swap(second))  6.02 us
    pallas_call x1, Pallas kernels, on_device(): call(functools.partial(back_kernel, peers, frames, rows), [struct((frames...  5.19 us
    ppermute x4, waiting for transfers between devices, halo_pair(): lax.ppermute(jnp.where(even, high_edge, low_edge), axis, swap(first))  5.17 us
    ppermute x12, waiting for transfers between devices, tm_exchange(): got.append(lax.ppermute(blocks[step], 'tm', pairs))  4.96 us
    pad x2, local copies, waits for them, and re-layouts, turned(): kernel = jnp.pad(kernel, ((0, 0),) * 4 + ((0, wide - width),))  4.33 us
  transfers between devices with their start and end apart: 18, of which 10 were waited for; matrix products, arithmetic and copies ran while one was open for 25% of the time, Pallas kernels for 0%

profile of v1, /device:TPU:8, one launch (start us, length us, event | category | flops | bytes accessed | tf_op | source)
XLA Modules:
  0.0 85.6 jit_solution(17165838728866694521)
XLA Ops:
  0.0 0.9 %fusion = bf16[2,2,4,1,384]{4,2,3,1,0:T(4,128)(2,1)S(1)} fusion(bf16[1,2,4,10,384]{4,2,3,1,0:T(4,128)(2,1)} %bitcast.31, bf16[1,2,4,10,384]{4,2,3,1,0:T(4,128)(2,1)} %bitcast.28, pred[]{:T(512)S(6)} %eq.14), kind=kLoop, calls=%fused_computation.17 | loop fusion | flops 18432 | bytes 135169 | tf_op jit(solution)/shard_map/jit(_where)/select_n | solution.py:47
  1.0 1.2 %collective-permute-done = bf16[2,2,4,1,384]{4,2,3,1,0:T(4,128)(2,1)S(1)} collective-permute-done((bf16[2,2,4,1,384]{4,2,3,1,0:T(4,128)(2,1)S(1)}, bf16[2,2,4,1,384]{4,2,3,1,0:T(4,128)(2,1)S(1)}, u32[]{:S(2)}, u32[]{:S(2)}) %collective-permute-start) | collective-permute-done | bytes 12320 | tf_op jit(solution)/shard_map/ppermute | solution.py:47
  2.2 1.0 %pad_maximum_fusion.1 = bf16[2,2,4,12,384]{4,2,3,1,0:T(4,128)(2,1)S(1)} fusion(bf16[2,2,4,1,384]{4,2,3,1,0:T(4,128)(2,1)S(1)} %get-tuple-element.41, bf16[1,2,4,10,384]{4,2,3,1,0:T(4,128)(2,1)} %bitcast.32, bf16[1,2,4,10,384]{4,2,3,1,0:T(4,128)(2,1)} %bitcast.29, bf16[2,2,4,1,384]{4,2,3,1,0:T(4,128)(2,1)S(1)} %get-tuple-element.40), kind=kLoop, calls=%fused_computation.3 | loop fusion | flops 221184 | bytes 294912 | tf_op jit(solution)/shard_map/concatenate | solution.py:64
  3.3 3.5 %collective-permute-start.1 = (bf16[2,2,1,12,384]{4,2,3,1,0:T(2,128)(2,1)S(1)}, bf16[2,2,1,12,384]{4,2,3,1,0:T(2,128)(2,1)S(1)}, u32[]{:S(2)}, u32[]{:S(2)}) collective-permute-start(bf16[2,2,1,12,384]{4,2,3,1,0:T(2,128)(2,1)S(1)} %get-tuple-element.36), channel_id=1, source_target_pairs={{2,4},{4,2},{3,5},{5,3},{10,12},{12,10},{11,13},{13,11},{18,20},{2... | collective-permute-start | bytes 110600 | tf_op jit(solution)/shard_map/ppermute | solution.py:49
  6.9 1.3 %broadcast_in_dim.17.gain_ref.refs_6_ = f32[1,384]{1,0:T(1,128)} reshape(f32[384]{0:T(512)} %param.11) | data formatting | bytes 3072 | tf_op jit(solution)/shard_map/broadcast_in_dim | solution.py:270
  8.2 1.4 %collective-permute-done.1 = bf16[2,2,1,12,384]{4,2,3,1,0:T(2,128)(2,1)S(1)} collective-permute-done((bf16[2,2,1,12,384]{4,2,3,1,0:T(2,128)(2,1)S(1)}, bf16[2,2,1,12,384]{4,2,3,1,0:T(2,128)(2,1)S(1)}, u32[]{:S(2)}, u32[]{:S(2)}) %collective-permute-start.1) | collective-permute-done | bytes 36896 | tf_op jit(solution)/shard_map/ppermute | solution.py:49
  9.6 1.7 %collective-permute-done.2 = bf16[2,2,1,12,384]{4,2,3,1,0:T(2,128)(2,1)S(1)} collective-permute-done((bf16[2,2,1,12,384]{4,2,3,1,0:T(2,128)(2,1)S(1)}, bf16[2,2,1,12,384]{4,2,3,1,0:T(2,128)(2,1)S(1)}, u32[]{:S(2)}, u32[]{:S(2)}) %collective-permute-start.2) | collective-permute-done | bytes 36896 | tf_op jit(solution)/shard_map/ppermute | solution.py:47
  11.4 1.1 %pad_maximum_fusion = bf16[2,2,6,12,384]{4,2,3,1,0:T(8,128)(2,1)S(1)} fusion(bf16[2,2,1,12,384]{4,2,3,1,0:T(2,128)(2,1)S(1)} %get-tuple-element.35, bf16[2,2,4,1,384]{4,2,3,1,0:T(4,128)(2,1)S(1)} %get-tuple-element.41, bf16[1,2,4,10,384]{4,2,3,1,0:T(4,128)(2,1)} %bitcast.33, bf16[1,2,4,10,384]{4,2,3,1,0:T(4,128)(2,1)} %bitcast.30, ...), kind=kLoop, calls=%fused_computation.2 | loop fusion | flops 1327104 | bytes 442368 | tf_op jit(solution)/shard_map/concatenate | solution.py:64
  12.7 0.7 copy.18.feat_ref
  13.4 0.7 copy.19.reward_ref
  14.1 2.1 %pack.1 = (bf16[2,72,512]{2,1,0:T(8,128)(2,1)}, bf16[2,72,512]{2,1,0:T(8,128)(2,1)}, bf16[2,72,512]{2,1,0:T(8,128)(2,1)}, bf16[2,72,512]{2,1,0:T(8,128)(2,1)}) custom-call(bf16[2,72,384]{2,1,0:T(8,128)(2,1)} %copy.18.feat_ref, bf16[2,72,384]{2,1,0:T(8,128)(2,1)} %copy.19.reward_ref, f32[1,384]{1,0:T(1,128)} %broadcast_in_dim.17.gain_ref.refs_6_), custom_call_target="tpu_custom_call" | custom-call | bytes 589824 | tf_op jit(solution)/shard_map/pack/pallas_call | solution.py:284
  16.2 1.5 %collective-permute-start.3 = (bf16[2,72,512]{2,1,0:T(8,128)(2,1)}, bf16[2,72,512]{2,1,0:T(8,128)(2,1)S(1)}, u32[]{:S(2)}, u32[]{:S(2)}) collective-permute-start(bf16[2,72,512]{2,1,0:T(8,128)(2,1)} %get-tuple-element.18), channel_id=1, source_target_pairs={{0,8},{8,0},{16,24},{24,16},{1,9},{9,1},{17,25},{25,17},{2,10},{10... | collective-permute-start | bytes 442376 | tf_op jit(solution)/shard_map/ppermute | solution.py:35
  17.7 1.5 %collective-permute-start.4 = (bf16[2,72,512]{2,1,0:T(8,128)(2,1)}, bf16[2,72,512]{2,1,0:T(8,128)(2,1)S(1)}, u32[]{:S(2)}, u32[]{:S(2)}) collective-permute-start(bf16[2,72,512]{2,1,0:T(8,128)(2,1)} %get-tuple-element.19), channel_id=1, source_target_pairs={{0,16},{8,24},{16,0},{24,8},{1,17},{9,25},{17,1},{25,9},{2,18},{10... | collective-permute-start | bytes 442376 | tf_op jit(solution)/shard_map/ppermute | solution.py:35
  19.7 1.5 %reverse_bitcast_fusion.1 = bf16[3,3,3,384,96]{3,4,2,0,1:T(8,128)(2,1)} fusion(bf16[3,3,3,96,384]{4,3,2,1,0:T(8,128)(2,1)S(1)} %copy-done.1), kind=kLoop, calls=%fused_computation.1 | loop fusion | bytes 3981312 | tf_op jit(solution)/shard_map/transpose | solution.py:273
  21.2 3.1 %copy.35 = bf16[3,3,3,384,96]{4,3,2,1,0:T(8,128)(2,1)S(1)} copy(bf16[3,3,3,384,96]{3,4,2,0,1:T(8,128)(2,1)} %reverse_bitcast_fusion.1) | data formatting | bytes 3981312
  24.3 1.8 %copy.34 = bf16[3,3,3,96,384]{4,3,2,1,0:T(8,128)(2,1)S(1)} copy(bf16[3,3,3,96,384]{4,3,2,0,1:T(8,128)(2,1)} %bitcast.27) | data formatting | bytes 3981312
  26.1 2.2 %pad.12.clone = bf16[3,3,3,384,128]{4,3,2,1,0:T(8,128)(2,1)} pad(bf16[3,3,3,384,96]{4,3,2,1,0:T(8,128)(2,1)S(1)} %copy.35, bf16[]{:T(256)} %constant.33.clone.1), padding=0_0x0_0x0_0x0_0x0_32 | pad | bytes 4644866 | tf_op jit(solution)/shard_map/jit(_pad)/pad | solution.py:274
  28.2 2.0 %pad.11.clone = bf16[3,3,3,128,384]{4,3,2,1,0:T(8,128)(2,1)} pad(bf16[3,3,3,96,384]{4,3,2,1,0:T(8,128)(2,1)S(1)} %copy.34, bf16[]{:T(256)} %constant.33.clone.1), padding=0_0x0_0x0_0x0_32x0_0 | pad | bytes 4644866 | tf_op jit(solution)/shard_map/jit(_pad)/pad | solution.py:277
  30.2 0.6 copy-done.5
  31.0 9.0 %both.1 = (bf16[2,40,512]{2,1,0:T(8,128)(2,1)}, bf16[2,40,512]{2,1,0:T(8,128)(2,1)}, bf16[2,40,512]{2,1,0:T(8,128)(2,1)}, bf16[2,40,512]{2,1,0:T(8,128)(2,1)}) custom-call(bf16[2,72,512]{2,1,0:T(8,128)(2,1)} %get-tuple-element.17.refs_0_, bf16[2,72,512]{2,1,0:T(8,128)(2,1)} %copy-done.5, bf16[2,72,512]{2,1,0:T(8,128)(2,1)} %copy-done.6, ...), custom_call_target="tpu_custom_call" | custom-call | flops 1274019840 | bytes 327680 | tf_op jit(solution)/shard_map/both/pallas_call | solution.py:291
  39.9 1.5 %collective-permute-start.6 = (bf16[2,40,512]{2,1,0:T(8,128)(2,1)}, bf16[2,40,512]{2,1,0:T(8,128)(2,1)S(1)}, u32[]{:S(2)}, u32[]{:S(2)}) collective-permute-start(bf16[2,40,512]{2,1,0:T(8,128)(2,1)} %get-tuple-element.22), channel_id=1, source_target_pairs={{0,8},{8,0},{16,24},{24,16},{1,9},{9,1},{17,25},{25,17},{2,10},{10... | collective-permute-start | bytes 245768 | tf_op jit(solution)/shard_map/ppermute | solution.py:35
  41.4 1.5 %collective-permute-start.7 = (bf16[2,40,512]{2,1,0:T(8,128)(2,1)}, bf16[2,40,512]{2,1,0:T(8,128)(2,1)S(1)}, u32[]{:S(2)}, u32[]{:S(2)}) collective-permute-start(bf16[2,40,512]{2,1,0:T(8,128)(2,1)} %get-tuple-element.23), channel_id=1, source_target_pairs={{0,16},{8,24},{16,0},{24,8},{1,17},{9,25},{17,1},{25,9},{2,18},{10... | collective-permute-start | bytes 245768 | tf_op jit(solution)/shard_map/ppermute | solution.py:35
  43.4 0.6 broadcast_in_dim.18.refs_4_
  44.0 0.6 broadcast_in_dim.19.refs_5_
  44.8 1.3 %collective-permute-done.7.refs_2_ = bf16[2,40,512]{2,1,0:T(8,128)(2,1)S(1)} collective-permute-done((bf16[2,40,512]{2,1,0:T(8,128)(2,1)}, bf16[2,40,512]{2,1,0:T(8,128)(2,1)S(1)}, u32[]{:S(2)}, u32[]{:S(2)}) %collective-permute-start.7) | collective-permute-done | bytes 81952 | tf_op jit(solution)/shard_map/ppermute | solution.py:35
  46.1 2.4 %collective-permute-done.8.refs_3_ = bf16[2,40,512]{2,1,0:T(8,128)(2,1)S(1)} collective-permute-done((bf16[2,40,512]{2,1,0:T(8,128)(2,1)}, bf16[2,40,512]{2,1,0:T(8,128)(2,1)S(1)}, u32[]{:S(2)}, u32[]{:S(2)}) %collective-permute-start.8) | collective-permute-done | bytes 81952 | tf_op jit(solution)/shard_map/ppermute | solution.py:35
  48.5 0.6 copy-done.13
  49.1 2.0 %middle.1 = bf16[2,40,384]{2,1,0:T(8,128)(2,1)} custom-call(bf16[2,40,512]{2,1,0:T(8,128)(2,1)} %get-tuple-element.21.refs_0_, bf16[2,40,512]{2,1,0:T(8,128)(2,1)} %copy-done.11, bf16[2,40,512]{2,1,0:T(8,128)(2,1)} %copy-done.12, bf16[2,40,512]{2,1,0:T(8,128)(2,1)} %copy-done.13, f32[1,384]{1,0:T(1,128)} %broadcast_in_dim.18.refs_4_, ...), custom_call_target="tpu_custom_call" | custom-call | bytes 61440 | tf_op jit(solution)/shard_map/middle/pallas_call | solution.py:305
  51.2 0.9 %copy.22 = bf16[2,40,384]{2,0,1:T(2,128)(2,1)S(1)} copy(bf16[2,40,384]{2,1,0:T(8,128)(2,1)} %middle.1) | data formatting | bytes 122880 | tf_op jit(solution)/shard_map/middle/pallas_call | solution.py:305
  52.2 1.2 %collective-permute-done.9 = bf16[2,4,1,384]{3,0,2,1:T(2,128)(2,1)S(1)} collective-permute-done((bf16[2,4,1,384]{3,0,2,1:T(2,128)(2,1)S(1)}, bf16[2,4,1,384]{3,0,2,1:T(2,128)(2,1)S(1)}, u32[]{:S(2)}, u32[]{:S(2)}) %collective-permute-start.9) | collective-permute-done | bytes 6176 | tf_op jit(solution)/shard_map/ppermute | solution.py:47
  53.5 2.5 %collective-permute-start.10 = (bf16[2,1,12,384]{3,0,2,1:T(2,128)(2,1)S(1)}, bf16[2,1,12,384]{3,0,2,1:T(2,128)(2,1)S(1)}, u32[]{:S(2)}, u32[]{:S(2)}) collective-permute-start(bf16[2,1,12,384]{3,0,2,1:T(2,128)(2,1)S(1)} %get-tuple-element.29), channel_id=1, source_target_pairs={{2,4},{4,2},{3,5},{5,3},{10,12},{12,10},{11,13},{13,11},{18,20},{2... | collective-permute-start | bytes 55304 | tf_op jit(solution)/shard_map/ppermute | solution.py:49
  56.0 1.2 %collective-permute-done.11 = bf16[2,1,12,384]{3,0,2,1:T(2,128)(2,1)S(1)} collective-permute-done((bf16[2,1,12,384]{3,0,2,1:T(2,128)(2,1)S(1)}, bf16[2,1,12,384]{3,0,2,1:T(2,128)(2,1)S(1)}, u32[]{:S(2)}, u32[]{:S(2)}) %collective-permute-start.11) | collective-permute-done | bytes 18464 | tf_op jit(solution)/shard_map/ppermute | solution.py:47
  57.3 1.9 %collective-permute-done.10 = bf16[2,1,12,384]{3,0,2,1:T(2,128)(2,1)S(1)} collective-permute-done((bf16[2,1,12,384]{3,0,2,1:T(2,128)(2,1)S(1)}, bf16[2,1,12,384]{3,0,2,1:T(2,128)(2,1)S(1)}, u32[]{:S(2)}, u32[]{:S(2)}) %collective-permute-start.10) | collective-permute-done | bytes 18464 | tf_op jit(solution)/shard_map/ppermute | solution.py:49
  59.4 0.6 collective-permute-start.12
  60.5 2.4 %collective-permute-start.14 = (bf16[2,72,384]{2,1,0:T(8,128)(2,1)S(1)}, bf16[2,72,384]{2,1,0:T(8,128)(2,1)S(1)}, u32[]{:S(2)}, u32[]{:S(2)}) collective-permute-start(bf16[2,72,384]{2,1,0:T(8,128)(2,1)S(1)} %copy.27.refs_0_), channel_id=1, source_target_pairs={{0,24},{8,16},{16,8},{24,0},{1,25},{9,17},{17,9},{25,1},{2,26},{10... | collective-permute-start | bytes 331784 | tf_op jit(solution)/shard_map/ppermute | solution.py:35
  63.0 1.5 %reverse_bitcast_fusion = bf16[3,3,3,384,96]{3,4,2,0,1:T(8,128)(2,1)} fusion(bf16[3,3,3,96,384]{4,3,2,1,0:T(8,128)(2,1)S(1)} %copy-done), kind=kLoop, calls=%fused_computation | loop fusion | bytes 3981312 | tf_op jit(solution)/shard_map/transpose | solution.py:273
  64.5 3.1 %copy.36 = bf16[3,3,3,384,96]{4,3,2,1,0:T(8,128)(2,1)S(1)} copy(bf16[3,3,3,384,96]{3,4,2,0,1:T(8,128)(2,1)} %reverse_bitcast_fusion) | data formatting | bytes 3981312
  67.6 2.2 %pad.13.clone = bf16[3,3,3,384,128]{4,3,2,1,0:T(8,128)(2,1)} pad(bf16[3,3,3,384,96]{4,3,2,1,0:T(8,128)(2,1)S(1)} %copy.36, bf16[]{:T(256)} %constant.33.clone.1), padding=0_0x0_0x0_0x0_0x0_32 | pad | bytes 4644866 | tf_op jit(solution)/shard_map/jit(_pad)/pad | solution.py:274
  69.8 0.6 copy-done.8
  70.5 5.2 %back.1 = (bf16[2,40,128]{2,1,0:T(8,128)(2,1)}, bf16[2,40,128]{2,1,0:T(8,128)(2,1)}, bf16[2,40,128]{2,1,0:T(8,128)(2,1)}, bf16[2,40,128]{2,1,0:T(8,128)(2,1)}) custom-call(bf16[2,72,384]{2,1,0:T(8,128)(2,1)} %copy-done.4, bf16[2,72,384]{2,1,0:T(8,128)(2,1)} %copy-done.8, bf16[2,72,384]{2,1,0:T(8,128)(2,1)} %copy-done.9, bf16[2,72,384]{2,1,0:T(8,128)(2,1)} %copy-done.10, ...), custom_call_target="tpu_custom_call" | custom-call | flops 637009920 | bytes 81920 | tf_op jit(solution)/shard_map/back/pallas_call | solution.py:312
  76.7 2.4 %collective-permute-start.17 = (bf16[2,40,128]{2,1,0:T(8,128)(2,1)}, bf16[2,40,128]{2,1,0:T(8,128)(2,1)S(1)}, u32[]{:S(2)}, u32[]{:S(2)}) collective-permute-start(bf16[2,40,128]{2,1,0:T(8,128)(2,1)} %get-tuple-element.28), channel_id=1, source_target_pairs={{0,24},{8,16},{16,8},{24,0},{1,25},{9,17},{17,9},{25,1},{2,26},{10... | collective-permute-start | bytes 61448 | tf_op jit(solution)/shard_map/ppermute | solution.py:35
  79.3 0.6 copy.30.refs_4_
  79.9 0.6 copy.31.refs_5_
  80.5 1.0 %collective-permute-done.17.refs_3_ = bf16[2,40,128]{2,1,0:T(8,128)(2,1)S(1)} collective-permute-done((bf16[2,40,128]{2,1,0:T(8,128)(2,1)}, bf16[2,40,128]{2,1,0:T(8,128)(2,1)S(1)}, u32[]{:S(2)}, u32[]{:S(2)}) %collective-permute-start.17) | collective-permute-done | bytes 20512 | tf_op jit(solution)/shard_map/ppermute | solution.py:35
  81.6 0.6 copy-done.16
  82.2 1.9 %final.1 = bf16[2,40,384]{2,1,0:T(8,128)(2,1)} custom-call(bf16[2,40,128]{2,1,0:T(8,128)(2,1)} %get-tuple-element.25.refs_0_, bf16[2,40,128]{2,1,0:T(8,128)(2,1)} %copy-done.14, bf16[2,40,128]{2,1,0:T(8,128)(2,1)} %copy-done.15, bf16[2,40,128]{2,1,0:T(8,128)(2,1)} %copy-done.16, bf16[2,40,384]{2,1,0:T(8,128)(2,1)} %copy.30.refs_4_, ...), custom_call_target="tpu_custom_call" | custom-call | bytes 61440 | tf_op jit(solution)/shard_map/final/pallas_call | solution.py:325
  84.1 0.9 %copy.32 = bf16[2,40,384]{2,0,1:T(2,128)(2,1)S(1)} copy(bf16[2,40,384]{2,1,0:T(8,128)(2,1)} %final.1) | data formatting | bytes 122880 | tf_op jit(solution)/shard_map/final/pallas_call | solution.py:325
  85.0 0.6 copy.33
  (67 shorter events, 4.2 us)
Async XLA Ops:
  0.0 19.7 %copy-start.1 = (bf16[3,3,3,96,384]{4,3,2,1,0:T(8,128)(2,1)S(1)}, bf16[3,3,3,96,384]{4,3,2,1,0:T(8,128)(2,1)}, u32[]{:S(2)}) copy-start(bf16[3,3,3,96,384]{4,3,2,1,0:T(8,128)(2,1)} %param.10) | copy-start | bytes 5971972
  0.9 1.2 %collective-permute-start = (bf16[2,2,4,1,384]{4,2,3,1,0:T(4,128)(2,1)S(1)}, bf16[2,2,4,1,384]{4,2,3,1,0:T(4,128)(2,1)S(1)}, u32[]{:S(2)}, u32[]{:S(2)}) collective-permute-start(bf16[2,2,4,1,384]{4,2,3,1,0:T(4,128)(2,1)S(1)} %fusion), channel_id=1, source_target_pairs={{0,1},{1,0},{2,3},{3,2},{4,5},{5,4},{6,7},{7,6},{8,9},{9,8},{10,11... | collective-permute-start | bytes 36872 | tf_op jit(solution)/shard_map/ppermute | solution.py:47
  3.3 6.2 %collective-permute-start.1 = (bf16[2,2,1,12,384]{4,2,3,1,0:T(2,128)(2,1)S(1)}, bf16[2,2,1,12,384]{4,2,3,1,0:T(2,128)(2,1)S(1)}, u32[]{:S(2)}, u32[]{:S(2)}) collective-permute-start(bf16[2,2,1,12,384]{4,2,3,1,0:T(2,128)(2,1)S(1)} %get-tuple-element.36), channel_id=1, source_target_pairs={{2,4},{4,2},{3,5},{5,3},{10,12},{12,10},{11,13},{13,11},{18,20},{2... | collective-permute-start | bytes 110600 | tf_op jit(solution)/shard_map/ppermute | solution.py:49
  6.8 4.4 %collective-permute-start.2 = (bf16[2,2,1,12,384]{4,2,3,1,0:T(2,128)(2,1)S(1)}, bf16[2,2,1,12,384]{4,2,3,1,0:T(2,128)(2,1)S(1)}, u32[]{:S(2)}, u32[]{:S(2)}) collective-permute-start(bf16[2,2,1,12,384]{4,2,3,1,0:T(2,128)(2,1)S(1)} %get-tuple-element.37), channel_id=1, source_target_pairs={{0,2},{4,6},{2,0},{6,4},{1,3},{5,7},{3,1},{7,5},{8,10},{12,14},{10... | collective-permute-start | bytes 110600 | tf_op jit(solution)/shard_map/ppermute | solution.py:47
  16.2 14.0 %collective-permute-start.3 = (bf16[2,72,512]{2,1,0:T(8,128)(2,1)}, bf16[2,72,512]{2,1,0:T(8,128)(2,1)S(1)}, u32[]{:S(2)}, u32[]{:S(2)}) collective-permute-start(bf16[2,72,512]{2,1,0:T(8,128)(2,1)} %get-tuple-element.18), channel_id=1, source_target_pairs={{0,8},{8,0},{16,24},{24,16},{1,9},{9,1},{17,25},{25,17},{2,10},{10... | collective-permute-start | bytes 442376 | tf_op jit(solution)/shard_map/ppermute | solution.py:35
  17.7 12.5 %collective-permute-start.4 = (bf16[2,72,512]{2,1,0:T(8,128)(2,1)}, bf16[2,72,512]{2,1,0:T(8,128)(2,1)S(1)}, u32[]{:S(2)}, u32[]{:S(2)}) collective-permute-start(bf16[2,72,512]{2,1,0:T(8,128)(2,1)} %get-tuple-element.19), channel_id=1, source_target_pairs={{0,16},{8,24},{16,0},{24,8},{1,17},{9,25},{17,1},{25,9},{2,18},{10... | collective-permute-start | bytes 442376 | tf_op jit(solution)/shard_map/ppermute | solution.py:35
  19.2 11.0 %collective-permute-start.5 = (bf16[2,72,512]{2,1,0:T(8,128)(2,1)}, bf16[2,72,512]{2,1,0:T(8,128)(2,1)S(1)}, u32[]{:S(2)}, u32[]{:S(2)}) collective-permute-start(bf16[2,72,512]{2,1,0:T(8,128)(2,1)} %get-tuple-element.20), channel_id=1, source_target_pairs={{0,24},{8,16},{16,8},{24,0},{1,25},{9,17},{17,9},{25,1},{2,26},{10... | collective-permute-start | bytes 442376 | tf_op jit(solution)/shard_map/ppermute | solution.py:35
  30.2 0.7 copy-start.5
  30.2 0.7 copy-start.6
  30.2 0.7 copy-start.7
  31.0 12.5 %copy-start.17 = (f32[384]{0:T(512)S(1)}, f32[384]{0:T(512)}, u32[]{:S(2)}) copy-start(f32[384]{0:T(512)} %param.12) | copy-start | bytes 4612
  31.0 13.1 %copy-start.18 = (f32[384]{0:T(512)S(1)}, f32[384]{0:T(512)}, u32[]{:S(2)}) copy-start(f32[384]{0:T(512)} %param.13) | copy-start | bytes 4612
  31.0 32.0 %copy-start = (bf16[3,3,3,96,384]{4,3,2,1,0:T(8,128)(2,1)S(1)}, bf16[3,3,3,96,384]{4,3,2,1,0:T(8,128)(2,1)}, u32[]{:S(2)}) copy-start(bf16[3,3,3,96,384]{4,3,2,1,0:T(8,128)(2,1)} %param.9) | copy-start | bytes 5971972
  39.9 4.8 %collective-permute-start.6 = (bf16[2,40,512]{2,1,0:T(8,128)(2,1)}, bf16[2,40,512]{2,1,0:T(8,128)(2,1)S(1)}, u32[]{:S(2)}, u32[]{:S(2)}) collective-permute-start(bf16[2,40,512]{2,1,0:T(8,128)(2,1)} %get-tuple-element.22), channel_id=1, source_target_pairs={{0,8},{8,0},{16,24},{24,16},{1,9},{9,1},{17,25},{25,17},{2,10},{10... | collective-permute-start | bytes 245768 | tf_op jit(solution)/shard_map/ppermute | solution.py:35
  41.4 4.7 %collective-permute-start.7 = (bf16[2,40,512]{2,1,0:T(8,128)(2,1)}, bf16[2,40,512]{2,1,0:T(8,128)(2,1)S(1)}, u32[]{:S(2)}, u32[]{:S(2)}) collective-permute-start(bf16[2,40,512]{2,1,0:T(8,128)(2,1)} %get-tuple-element.23), channel_id=1, source_target_pairs={{0,16},{8,24},{16,0},{24,8},{1,17},{9,25},{17,1},{25,9},{2,18},{10... | collective-permute-start | bytes 245768 | tf_op jit(solution)/shard_map/ppermute | solution.py:35
  43.0 5.6 %collective-permute-start.8 = (bf16[2,40,512]{2,1,0:T(8,128)(2,1)}, bf16[2,40,512]{2,1,0:T(8,128)(2,1)S(1)}, u32[]{:S(2)}, u32[]{:S(2)}) collective-permute-start(bf16[2,40,512]{2,1,0:T(8,128)(2,1)} %get-tuple-element.24), channel_id=1, source_target_pairs={{0,24},{8,16},{16,8},{24,0},{1,25},{9,17},{17,9},{25,1},{2,26},{10... | collective-permute-start | bytes 245768 | tf_op jit(solution)/shard_map/ppermute | solution.py:35
  44.8 3.7 %copy-start.11 = (bf16[2,40,512]{2,1,0:T(8,128)(2,1)}, bf16[2,40,512]{2,1,0:T(8,128)(2,1)S(1)}, u32[]{:S(2)}) copy-start(bf16[2,40,512]{2,1,0:T(8,128)(2,1)S(1)} %collective-permute-done.6.refs_1_) | copy-start | bytes 245764
  46.1 2.4 %copy-start.12 = (bf16[2,40,512]{2,1,0:T(8,128)(2,1)}, bf16[2,40,512]{2,1,0:T(8,128)(2,1)S(1)}, u32[]{:S(2)}) copy-start(bf16[2,40,512]{2,1,0:T(8,128)(2,1)S(1)} %collective-permute-done.7.refs_2_) | copy-start | bytes 245764
  48.5 0.6 copy-start.13
  52.1 1.2 %collective-permute-start.9 = (bf16[2,4,1,384]{3,0,2,1:T(2,128)(2,1)S(1)}, bf16[2,4,1,384]{3,0,2,1:T(2,128)(2,1)S(1)}, u32[]{:S(2)}, u32[]{:S(2)}) collective-permute-start(bf16[2,4,1,384]{3,0,2,1:T(2,128)(2,1)S(1)} %broadcast_select_fusion.12), channel_id=1, source_target_pairs={{0,1},{1,0},{2,3},{3,2},{4,5},{5,4},{6,7},{7,6},{8,9},{9,8},{10,11... | collective-permute-start | bytes 18440 | tf_op jit(solution)/shard_map/ppermute | solution.py:47
  53.4 3.8 %collective-permute-start.11 = (bf16[2,1,12,384]{3,0,2,1:T(2,128)(2,1)S(1)}, bf16[2,1,12,384]{3,0,2,1:T(2,128)(2,1)S(1)}, u32[]{:S(2)}, u32[]{:S(2)}) collective-permute-start(bf16[2,1,12,384]{3,0,2,1:T(2,128)(2,1)S(1)} %bitcast.47), channel_id=1, source_target_pairs={{0,2},{4,6},{2,0},{6,4},{1,3},{5,7},{3,1},{7,5},{8,10},{12,14},{10... | collective-permute-start | bytes 55304 | tf_op jit(solution)/shard_map/ppermute | solution.py:47
  53.5 5.7 %collective-permute-start.10 = (bf16[2,1,12,384]{3,0,2,1:T(2,128)(2,1)S(1)}, bf16[2,1,12,384]{3,0,2,1:T(2,128)(2,1)S(1)}, u32[]{:S(2)}, u32[]{:S(2)}) collective-permute-start(bf16[2,1,12,384]{3,0,2,1:T(2,128)(2,1)S(1)} %get-tuple-element.29), channel_id=1, source_target_pairs={{2,4},{4,2},{3,5},{5,3},{10,12},{12,10},{11,13},{13,11},{18,20},{2... | collective-permute-start | bytes 55304 | tf_op jit(solution)/shard_map/ppermute | solution.py:49
  59.4 8.2 %copy-start.4 = (bf16[2,72,384]{2,1,0:T(8,128)(2,1)}, bf16[2,72,384]{2,1,0:T(8,128)(2,1)S(1)}, u32[]{:S(2)}) copy-start(bf16[2,72,384]{2,1,0:T(8,128)(2,1)S(1)} %copy.27.refs_0_) | copy-start | bytes 331780
  59.4 10.3 %collective-permute-start.12 = (bf16[2,72,384]{2,1,0:T(8,128)(2,1)S(1)}, bf16[2,72,384]{2,1,0:T(8,128)(2,1)S(1)}, u32[]{:S(2)}, u32[]{:S(2)}) collective-permute-start(bf16[2,72,384]{2,1,0:T(8,128)(2,1)S(1)} %copy.27.refs_0_), channel_id=1, source_target_pairs={{0,8},{8,0},{16,24},{24,16},{1,9},{9,1},{17,25},{25,17},{2,10},{10... | collective-permute-start | bytes 331784 | tf_op jit(solution)/shard_map/ppermute | solution.py:35
  60.0 9.7 %collective-permute-start.13 = (bf16[2,72,384]{2,1,0:T(8,128)(2,1)S(1)}, bf16[2,72,384]{2,1,0:T(8,128)(2,1)S(1)}, u32[]{:S(2)}, u32[]{:S(2)}) collective-permute-start(bf16[2,72,384]{2,1,0:T(8,128)(2,1)S(1)} %copy.27.refs_0_), channel_id=1, source_target_pairs={{0,16},{8,24},{16,0},{24,8},{1,17},{9,25},{17,1},{25,9},{2,18},{10... | collective-permute-start | bytes 331784 | tf_op jit(solution)/shard_map/ppermute | solution.py:35
  60.5 9.2 %collective-permute-start.14 = (bf16[2,72,384]{2,1,0:T(8,128)(2,1)S(1)}, bf16[2,72,384]{2,1,0:T(8,128)(2,1)S(1)}, u32[]{:S(2)}, u32[]{:S(2)}) collective-permute-start(bf16[2,72,384]{2,1,0:T(8,128)(2,1)S(1)} %copy.27.refs_0_), channel_id=1, source_target_pairs={{0,24},{8,16},{16,8},{24,0},{1,25},{9,17},{17,9},{25,1},{2,26},{10... | collective-permute-start | bytes 331784 | tf_op jit(solution)/shard_map/ppermute | solution.py:35
  69.7 9.4 %copy-start.2 = (bf16[2,4,10,384]{3,1,2,0:T(4,128)(2,1)S(1)}, bf16[2,4,10,384]{3,1,2,0:T(4,128)(2,1)}, u32[]{:S(2)}) copy-start(bf16[2,4,10,384]{3,1,2,0:T(4,128)(2,1)} %param.7) | copy-start | bytes 184324
  69.7 9.5 %copy-start.3 = (bf16[2,4,10,384]{3,1,2,0:T(4,128)(2,1)S(1)}, bf16[2,4,10,384]{3,1,2,0:T(4,128)(2,1)}, u32[]{:S(2)}) copy-start(bf16[2,4,10,384]{3,1,2,0:T(4,128)(2,1)} %param.8) | copy-start | bytes 184324
  69.7 0.6 copy-start.8
  69.7 0.7 copy-start.9
  69.7 0.7 copy-start.10
  75.6 4.9 %collective-permute-start.15 = (bf16[2,40,128]{2,1,0:T(8,128)(2,1)}, bf16[2,40,128]{2,1,0:T(8,128)(2,1)S(1)}, u32[]{:S(2)}, u32[]{:S(2)}) collective-permute-start(bf16[2,40,128]{2,1,0:T(8,128)(2,1)} %get-tuple-element.26), channel_id=1, source_target_pairs={{0,8},{8,0},{16,24},{24,16},{1,9},{9,1},{17,25},{25,17},{2,10},{10... | collective-permute-start | bytes 61448 | tf_op jit(solution)/shard_map/ppermute | solution.py:35
  76.2 4.3 %collective-permute-start.16 = (bf16[2,40,128]{2,1,0:T(8,128)(2,1)}, bf16[2,40,128]{2,1,0:T(8,128)(2,1)S(1)}, u32[]{:S(2)}, u32[]{:S(2)}) collective-permute-start(bf16[2,40,128]{2,1,0:T(8,128)(2,1)} %get-tuple-element.27), channel_id=1, source_target_pairs={{0,16},{8,24},{16,0},{24,8},{1,17},{9,25},{17,1},{25,9},{2,18},{10... | collective-permute-start | bytes 61448 | tf_op jit(solution)/shard_map/ppermute | solution.py:35
  76.7 4.9 %collective-permute-start.17 = (bf16[2,40,128]{2,1,0:T(8,128)(2,1)}, bf16[2,40,128]{2,1,0:T(8,128)(2,1)S(1)}, u32[]{:S(2)}, u32[]{:S(2)}) collective-permute-start(bf16[2,40,128]{2,1,0:T(8,128)(2,1)} %get-tuple-element.28), channel_id=1, source_target_pairs={{0,24},{8,16},{16,8},{24,0},{1,25},{9,17},{17,9},{25,1},{2,26},{10... | collective-permute-start | bytes 61448 | tf_op jit(solution)/shard_map/ppermute | solution.py:35
  80.5 1.1 %copy-start.14 = (bf16[2,40,128]{2,1,0:T(8,128)(2,1)}, bf16[2,40,128]{2,1,0:T(8,128)(2,1)S(1)}, u32[]{:S(2)}) copy-start(bf16[2,40,128]{2,1,0:T(8,128)(2,1)S(1)} %collective-permute-done.15.refs_1_) | copy-start | bytes 61444
  80.5 1.1 %copy-start.15 = (bf16[2,40,128]{2,1,0:T(8,128)(2,1)}, bf16[2,40,128]{2,1,0:T(8,128)(2,1)S(1)}, u32[]{:S(2)}) copy-start(bf16[2,40,128]{2,1,0:T(8,128)(2,1)S(1)} %collective-permute-done.16.refs_2_) | copy-start | bytes 61444
  81.6 0.6 copy-start.16

commit v2 on v1

v2 whole, which is shorter than its diff:
```python
import functools
import math

import jax
import jax.numpy as jnp
from jax import lax
from jax.experimental import pallas as pl
from jax.experimental.pallas import tpu as pltpu
from jax.sharding import PartitionSpec as P

epsilon = 1e-06
f32 = jnp.float32
bf16 = jnp.bfloat16
lanes = 128


def is_power(count):
    return count & (count - 1) == 0


def sent_to(index, step, count):
    return index ^ step if is_power(count) else lax.rem(index + step, count)


def got_from(index, step, count):
    return index ^ step if is_power(count) else lax.rem(index + count - step, count)


def tm_exchange(blocks):
    count = len(blocks)
    got = [blocks[0]]
    for step in range(1, count):
        pairs = [
            (i, i ^ step if is_power(count) else (i + step) % count) for i in range(count)
        ]
        got.append(lax.ppermute(blocks[step], "tm", pairs))
    return got


def is_even(axis):
    return lax.rem(lax.axis_index(axis), 2) == 0


def halo_swaps(low_edge, high_edge, axis):
    count = lax.axis_size(axis)
    even = is_even(axis)
    got = []
    for start, value in ((0, (high_edge, low_edge)), (1, (low_edge, high_edge))):
        pairs = [(i, i + 1) for i in range(start, count - 1, 2)]
        if pairs:
            pairs = pairs + [(b, a) for a, b in pairs]
            got.append(lax.ppermute(jnp.where(even, *value), axis, pairs))
        else:
            got.append(None)
    return got


def low_and_high(axis, first, second):
    even = is_even(axis)
    if first is None:
        return None, None
    nothing = jnp.zeros_like(first)
    second = nothing if second is None else second
    return jnp.where(even, second, first), jnp.where(even, first, second)


def edges(cells, dim):
    size = cells.shape[dim]
    return (
        lax.slice_in_dim(cells, 0, 1, axis=dim),
        lax.slice_in_dim(cells, size - 1, size, axis=dim),
    )


def joined(low, cells, high, dim):
    if low is None:
        low = high = jnp.zeros_like(edges(cells, dim)[0])
    return jnp.concatenate([low, cells, high], axis=dim)


def with_halo(cells, axis, dim):
    got = halo_swaps(*edges(cells, dim), axis)
    low, high = low_and_high(axis, *got)
    return joined(low, cells, high, dim)


def rms_parts(values, gain):
    inv_rms = lax.rsqrt(jnp.mean(values * values, axis=-1, keepdims=True) + epsilon)
    normed = values * inv_rms
    return inv_rms, normed, normed * gain


def silu_slope(values):
    sigmoid_val = jax.nn.sigmoid(values)
    return sigmoid_val * (1.0 + values * (1.0 - sigmoid_val))


def rms_back(cotangent, inv_rms, normed, gain):
    scaled_grad = cotangent * gain
    return inv_rms * (scaled_grad - normed * jnp.mean(normed * scaled_grad, axis=-1, keepdims=True))


def slot_matrix(slot, width, channels, wide):
    row = lax.broadcasted_iota(jnp.int32, (channels, wide), 0)
    col = lax.broadcasted_iota(jnp.int32, (channels, wide), 1)
    hit = (row == col + slot * width) & (col < width)
    return jnp.where(hit, 1.0, 0.0).astype(bf16)


def spread_matrix(slot, width, channels, wide):
    row = lax.broadcasted_iota(jnp.int32, (wide, channels), 0)
    col = lax.broadcasted_iota(jnp.int32, (wide, channels), 1)
    hit = (col == row + slot * width) & (row < width)
    return jnp.where(hit, 1.0, 0.0).astype(bf16)


def pack_kernel(peers, width, *refs):
    strips_ref, *edge_refs = refs[: -peers - 2]
    gain_ref, *out_refs = refs[-peers - 2 : -1]
    plane_ref = refs[-1]
    me = lax.axis_index("tm")
    _, frames, rows, span, channels = strips_ref.shape
    wide = out_refs[0].shape[2] - channels
    for frame in range(frames):
        for array in range(2):
            got = [ref[array, frame, 0].astype(f32) for ref in edge_refs] + [None, None]
            low, high = low_and_high("row", got[0], got[1])
            if low is None:
                low = high = jnp.zeros((span, channels), f32)
            strips = [strips_ref[array, frame, row].astype(f32) for row in range(rows)]
            for row, strip in enumerate([low, *strips, high]):
                plane_ref[array, row * span : (row + 1) * span, :] = strip
        act = rms_parts(plane_ref[0], gain_ref[...])[2]
        silu = (act * jax.nn.sigmoid(act)).astype(bf16)
        reward = plane_ref[1].astype(bf16)
        for step in range(peers):
            slot = sent_to(me, step, peers)
            piece = jnp.dot(
                silu, slot_matrix(slot, width, channels, wide), preferred_element_type=f32
            )
            out_refs[step][frame, :, :channels] = reward
            out_refs[step][frame, :, channels:] = piece.astype(bf16)


def lay_frames(peers, frames, block_refs, cells_ref):
    me = lax.axis_index("tm")
    total = peers * frames
    for step in range(peers):
        source = got_from(me, step, peers)
        for frame in range(frames):
            for tile in range(cells_ref.shape[0]):
                piece = block_refs[step][frame, :, tile * lanes : (tile + 1) * lanes]
                place = pl.ds(source * frames + frame, piece.shape[0], stride=total)
                cells_ref[tile, place, :] = piece.astype(f32)


def shifted(values, ahead):
    total = values.shape[1]
    if ahead == 0:
        return values
    frame = lax.broadcasted_iota(jnp.int32, values.shape, 1)
    moved = pltpu.roll(values, (-ahead) % total, 1)
    keep = frame < total - ahead if ahead > 0 else frame >= -ahead
    return jnp.where(keep, moved, 0.0)


def chunk_rows(rows, total):
    return max(r for r in range(1, rows + 1) if rows % r == 0 and (r == 1 or r * total <= 32))


def stacked_weights(kernel_ref, wide, order):
    width, channels = kernel_ref.shape[3:]
    pad = jnp.zeros((wide - width, channels), bf16)

    def block(a, b, c):
        value = kernel_ref[a, b, c]
        return jnp.concatenate([value, pad], axis=0) if wide > width else value

    return jnp.concatenate(
        [jnp.concatenate([block(*tap) for tap in column], axis=0) for column in order], axis=1
    )


def conv_ahead(
    cells_ref, first, kernel_ref, plane_ref, parts_ref, sum_ref, rows, total, cols_first=False
):
    plane_rows, span, channels = plane_ref.shape
    cols = span // total - 2
    wide = sum_ref.shape[0] * lanes
    wide_tiles = wide // lanes

    @pl.loop(0, plane_rows)
    def _(row):
        base = pl.multiple_of(row * span, total)
        for tile in range(channels // lanes):
            plane_ref[row, :, tile * lanes : (tile + 1) * lanes] = cells_ref[
                first + tile, pl.ds(base, span), :
            ].astype(bf16)

    weights = stacked_weights(
        kernel_ref,
        wide,
        [[(2 - s, 2 - b, 2 - c) for s in range(3) for c in range(3)] for b in range(3)],
    )
    step = chunk_rows(rows, total)

    def chunk(start):
        left = jnp.concatenate(
            [plane_ref[pl.ds(start + b, step)].reshape(-1, channels) for b in range(3)], axis=1
        )
        parts = lax.dot_general(left, weights, (((1,), (1,)), ((), ())), preferred_element_type=f32)
        for tile in range(parts_ref.shape[0]):
            parts_ref[tile] = parts[:, tile * lanes : (tile + 1) * lanes]
        for row in range(step):
            for tile in range(wide_tiles):
                summed = None
                for s in range(3):
                    part = None
                    for c in range(3):
                        at = (row * (cols + 2) + c) * total
                        piece = parts_ref[(s * 3 + c) * wide_tiles + tile, at : at + cols * total, :]
                        part = piece if part is None else part + piece
                    part = shifted(part.reshape(cols, total, lanes), s)
                    summed = part if summed is None else summed + part
                if cols_first:
                    for col in range(cols):
                        place = pl.ds((col * rows + start + row) * total, total)
                        sum_ref[tile, place, :] = summed[col]
                else:
                    place = pl.ds((start + row) * cols * total, cols * total)
                    sum_ref[tile, place, :] = summed.reshape(cols * total, lanes)

    run_chunks(rows, step, chunk)


def run_chunks(rows, step, chunk):
    if step == rows:
        chunk(0)
    else:
        pl.loop(0, rows, step=step)(chunk)


def conv_behind(cells_ref, first, kernel_ref, taps_ref, sum_ref, rows, total):
    plane_rows, cols = taps_ref.shape[0], taps_ref.shape[1] // total
    channels = sum_ref.shape[0] * lanes
    wide_tiles = taps_ref.shape[2] // (3 * lanes)
    span = (cols + 2) * total

    @pl.loop(0, plane_rows)
    def _(row):
        base = pl.multiple_of(row * span, total)
        for tile in range(wide_tiles):
            for c in range(3):
                at = (c * wide_tiles + tile) * lanes
                taps_ref[row, :, at : at + lanes] = cells_ref[
                    first + tile, pl.ds(base + c * total, cols * total), :
                ].astype(bf16)

    weights = stacked_weights(
        kernel_ref,
        wide_tiles * lanes,
        [[(a, b, c) for b in range(3) for c in range(3)] for a in range(3)],
    )
    step = chunk_rows(rows, total)

    def chunk(start):
        left = jnp.concatenate(
            [
                taps_ref[pl.ds(start + b, step)].reshape(-1, taps_ref.shape[2])
                for b in range(3)
            ],
            axis=1,
        )
        parts = jnp.dot(left, weights, preferred_element_type=f32)
        place = pl.ds(start * cols * total, step * cols * total)
        for tile in range(channels // lanes):
            summed = None
            for a in range(3):
                at = a * channels + tile * lanes
                part = parts[:, at : at + lanes].reshape(step * cols, total, lanes)
                part = shifted(part, a - 2)
                summed = part if summed is None else summed + part
            sum_ref[tile, place, :] = summed.reshape(-1, lanes)

    run_chunks(rows, step, chunk)


def hand_out(peers, frames, total, sum_ref, out_refs, start):
    me = lax.axis_index("tm")
    for step in range(peers):
        target = sent_to(me, step, peers)
        for frame in range(frames):
            place = pl.ds(target * frames + frame, out_refs[step].shape[1], stride=total)
            for tile in range(sum_ref.shape[0]):
                at = start + tile * lanes
                out_refs[step][frame, :, at : at + lanes] = sum_ref[tile, place, :].astype(bf16)


def both_kernel(peers, frames, rows, channels, *refs):
    blocks = refs[:peers]
    kernel_one, kernel_two = refs[peers : peers + 2]
    outs = refs[peers + 2 : 2 * peers + 2]
    cells, taps, plane, parts, sum_one, sum_two = refs[2 * peers + 2 :]
    total = peers * frames
    tiles = channels // lanes
    lay_frames(peers, frames, blocks, cells)
    conv_behind(cells, tiles, kernel_one, taps, sum_one, rows, total)
    hand_out(peers, frames, total, sum_one, outs, 0)
    conv_ahead(cells, 0, kernel_two, plane, parts, sum_two, rows, total)
    hand_out(peers, frames, total, sum_two, outs, channels)


def back_kernel(peers, frames, rows, *refs):
    blocks = refs[:peers]
    kernel = refs[peers]
    outs = refs[peers + 1 : 2 * peers + 1]
    cells, plane, parts, sums = refs[2 * peers + 1 :]
    total = peers * frames
    lay_frames(peers, frames, blocks, cells)
    conv_ahead(cells, 0, kernel, plane, parts, sums, rows, total, cols_first=True)
    hand_out(peers, frames, total, sums, outs, 0)


def gathered(peers, frame, block_refs, start, width, channels):
    me = lax.axis_index("tm")
    wide = block_refs[0].shape[2] - start
    summed = None
    for step in range(peers):
        spread = spread_matrix(got_from(me, step, peers), width, channels, wide)
        part = jnp.dot(
            block_refs[step][frame, :, start:], spread, preferred_element_type=f32
        )
        summed = part if summed is None else summed + part
    return summed


def split_rows(flat_ref, values, out_ref, frame):
    flat_ref[...] = values
    cols = out_ref.shape[2]
    for row in range(out_ref.shape[1]):
        out_ref[frame, row] = flat_ref[row * cols : (row + 1) * cols, :].astype(bf16)


def join_rows(flat_ref, in_ref, frame):
    cols = in_ref.shape[2]
    for row in range(in_ref.shape[1]):
        flat_ref[row * cols : (row + 1) * cols, :] = in_ref[frame, row].astype(f32)
    return flat_ref[...]


def middle_kernel(peers, width, *refs):
    blocks = refs[:peers]
    gain_ref, bias_ref, out_ref, flat_ref = refs[peers:]
    frames, channels = out_ref.shape[0], out_ref.shape[3]
    for frame in range(frames):
        hidden = blocks[0][frame, :, :channels].astype(f32)
        for step in range(1, peers):
            hidden = hidden + blocks[step][frame, :, :channels].astype(f32)
        hidden = hidden + bias_ref[...]
        back = gathered(peers, frame, blocks, channels, width, channels)
        inv, normed, act = rms_parts(hidden, gain_ref[...])
        grad = rms_back(back * silu_slope(act), inv, normed, gain_ref[...])
        split_rows(flat_ref.at[frame], grad, out_ref, frame)


def final_kernel(peers, width, *refs):
    blocks = refs[:peers]
    feat_ref, reward_ref, gain_ref, out_ref, flat_ref = refs[peers:]
    frames, channels = out_ref.shape[0], out_ref.shape[3]
    for frame in range(frames):
        back = gathered(peers, frame, blocks, 0, width, channels)
        cells = join_rows(flat_ref.at[frame, 0], feat_ref, frame)
        reward = join_rows(flat_ref.at[frame, 1], reward_ref, frame)
        inv, normed, act = rms_parts(cells, gain_ref[...])
        result = rms_back(back * silu_slope(act), inv, normed, gain_ref[...])
        split_rows(flat_ref.at[frame, 2], result + reward, out_ref, frame)


def size_of(structs):
    return sum(math.prod(s.shape) * s.dtype.itemsize for s in structs)


def call(kernel, outs, scratch=(), flops=0, spare=2, name=None):
    def run(*operands):
        held = size_of(outs) + size_of(operands)
        grant = 2 * held + size_of(scratch) + spare * 2**20
        return pl.pallas_call(
            kernel,
            out_shape=outs,
            scratch_shapes=list(scratch),
            cost_estimate=pl.CostEstimate(
                flops=flops, bytes_accessed=held, transcendentals=0
            ),
            compiler_params=pltpu.CompilerParams(vmem_limit_bytes=min(grant, 60 * 2**20)),
            name=name,
        )(*operands)

    return run


def on_device(
    features, reward_grad, first_kernel, second_kernel, first_gain, second_gain, first_bias
):
    peers = lax.axis_size("tm")
    frames, rows, cols, channels = features.shape
    width = first_kernel.shape[3]
    wide = -(-width // lanes) * lanes
    total = peers * frames
    plane = (rows + 2) * (cols + 2)
    count = rows * cols
    struct = jax.ShapeDtypeStruct
    gain_one, gain_two = first_gain[None], second_gain[None]

    strips = with_halo(jnp.stack([features, reward_grad]), "col", 3)
    row_edges = [got for got in halo_swaps(*edges(strips, 2), "row") if got is not None]
    packed = call(
        functools.partial(pack_kernel, peers, width),
        [struct((frames, plane, channels + wide), bf16)] * peers,
        [pltpu.VMEM((2, plane, channels), f32)],
        name="pack",
    )(strips, *row_edges, gain_one)
    got = tm_exchange(packed)
    ahead_scratch = [
        pltpu.VMEM((rows + 2, (cols + 2) * total, channels), bf16),
        pltpu.VMEM((9 * wide // lanes, chunk_rows(rows, total) * (cols + 2) * total, lanes), f32),
    ]
    flops = 2 * 27 * width * channels * total * count
    sums = call(
        functools.partial(both_kernel, peers, frames, rows, channels),
        [struct((frames, count, channels + wide), bf16)] * peers,
        [
            pltpu.VMEM(((channels + wide) // lanes, plane * total, lanes), f32),
            pltpu.VMEM((rows + 2, cols * total, 3 * wide), bf16),
            *ahead_scratch,
            pltpu.VMEM((channels // lanes, count * total, lanes), f32),
            pltpu.VMEM((wide // lanes, count * total, lanes), f32),
        ],
        2 * flops,
        spare=8,
        name="both",
    )(*got, first_kernel, second_kernel)
    got = tm_exchange(sums)
    hidden_grad = call(
        functools.partial(middle_kernel, peers, width),
        [struct(features.shape, bf16)],
        [pltpu.VMEM((frames, count, channels), f32)],
        name="middle",
    )(*got, gain_two, first_bias[None])[0]
    hidden_plane = with_halo(with_halo(hidden_grad, "col", 2), "row", 1)
    got = tm_exchange([hidden_plane.reshape(frames, plane, channels)] * peers)
    backs = call(
        functools.partial(back_kernel, peers, frames, rows),
        [struct((frames, count, wide), bf16)] * peers,
        [
            pltpu.VMEM((channels // lanes, plane * total, lanes), f32),
            *ahead_scratch,
            pltpu.VMEM((wide // lanes, count * total, lanes), f32),
        ],
        flops,
        spare=8,
        name="back",
    )(*got, first_kernel)
    got = tm_exchange(backs)
    by_col = (0, 2, 1, 3)
    held = features.transpose(by_col), reward_grad.transpose(by_col)
    result = call(
        functools.partial(final_kernel, peers, width),
        [struct(held[0].shape, bf16)],
        [pltpu.VMEM((frames, 3, count, channels), f32)],
        name="final",
    )(*got, *held, gain_one)[0]
    return result.transpose(by_col)


def solution(mesh):
    in_specs = (
        P("tm", "row", "col", None),
        P("tm", "row", "col", None),
        P(None, None, None, "tm", None),
        P(None, None, None, "tm", None),
        P(),
        P(),
        P(),
    )
    out_specs = P("tm", "row", "col", None)
    return jax.shard_map(
        on_device, mesh=mesh, in_specs=in_specs, out_specs=out_specs, check_vma=False
    )
```

time: 86.3 us -> 59.4 us (0.69)
  local copies, waits for them, and re-layouts: 27.6 us -> 4.8 us
  Pallas kernels: 20.3 us -> 7.28 us
  waiting for transfers between devices: 13.5 us -> 22.7 us
  other arithmetic: 3.66 us -> 0.41 us
  starting transfers between devices: 20.3 us -> 23.2 us
    pallas_call x5, Pallas kernels: 20.3 us -> 7.28 us  [run(): pl.pallas_call(kernel, out_shape=outs, scratch_shapes=list(scratch), cost...]
    ppermute x12, waiting for transfers between devices: 4.96 us -> 16.9 us  [tm_exchange(): got.append(lax.ppermute(blocks[step], 'tm', pairs))]
    unnamed x43 -> x12, local copies, waits for them, and re-layouts: 10.7 us -> 3.12 us
    pad x3 -> x0, local copies, waits for them, and re-layouts: 6.3 us -> none  [the longest x2 4.33 us: turned(): kernel = jnp.pad(kernel, ((0, 0),) * 4 + ((0, wide - width),))]
    transpose x2 -> x0, local copies, waits for them, and re-layouts: 3.06 us -> none  [turned(): kernel = kernel[::-1, ::-1, ::-1].transpose(1, 0, 2, 4, 3)]
    ppermute x6, waiting for transfers between devices: 8.5 us -> 5.77 us  [halo_swaps(): got.append(lax.ppermute(jnp.where(even, *value), axis, pairs))]
    ppermute x6, starting transfers between devices: 6.31 us -> 8.97 us  [halo_swaps(): got.append(lax.ppermute(jnp.where(even, *value), axis, pairs))]
    concatenate x3 -> x2, other arithmetic: 2.28 us -> 0.18 us  [joined(): return jnp.concatenate([low, cells, high], axis=dim)]
  transfers between devices with their start and end apart: 18 -> 18, of which waited for: 10 -> 15; matrix products, arithmetic and copies ran while one was open for 25% -> 1% of each run, Pallas kernels for 0% -> 0%
where the time goes in v2:
time: 59.4 us; the launch traced here: 58.6 us
  starting transfers between devices  23.2 us (39%)
  waiting for transfers between devices  22.7 us (38%)
  Pallas kernels  7.28 us (12%)
  local copies, waits for them, and re-layouts  4.8 us (8%)
    ppermute x12, waiting for transfers between devices, tm_exchange(): got.append(lax.ppermute(blocks[step], 'tm', pairs))  16.9 us
    ppermute x12, starting transfers between devices, tm_exchange(): got.append(lax.ppermute(blocks[step], 'tm', pairs))  14.2 us
    ppermute x6, starting transfers between devices, halo_swaps(): got.append(lax.ppermute(jnp.where(even, *value), axis, pairs))  8.97 us
    pallas_call x5, Pallas kernels, run(): pl.pallas_call(kernel, out_shape=outs, scratch_shapes=list(scratch), cost...  7.28 us
    ppermute x6, waiting for transfers between devices, halo_swaps(): got.append(lax.ppermute(jnp.where(even, *value), axis, pairs))  5.77 us
    unnamed x12, local copies, waits for them, and re-layouts  3.12 us
  transfers between devices with their start and end apart: 18, of which 15 were waited for; matrix products, arithmetic and copies ran while one was open for 1% of the time, Pallas kernels for 0%

profile of v2, /device:TPU:8, one launch (start us, length us, event | category | flops | bytes accessed | tf_op | source)
XLA Modules:
  0.0 58.6 jit_solution(2297034931857640341)
XLA Ops:
  0.0 0.9 %copy_bitcast_fusion = (bf16[1,2,4,10,384]{4,3,2,1,0:T(8,128)(2,1)S(1)}, bf16[1,2,4,10,384]{4,3,2,1,0:T(8,128)(2,1)S(1)}) fusion(bf16[2,4,10,384]{3,1,2,0:T(4,128)(2,1)} %param.8, bf16[2,4,10,384]{3,1,2,0:T(4,128)(2,1)} %param.7), kind=kLoop, calls=%fused_computation.2 | loop fusion | bytes 245760 | tf_op jit(solution)/shard_map/stack | solution.py:414
  0.9 0.1 broadcast_select_fusion.4
  0.9 0.1 collective-permute-start
  1.0 1.2 %collective-permute-done = bf16[2,2,4,1,384]{4,3,2,1,0:T(2,128)(2,1)S(1)} collective-permute-done((bf16[2,2,4,1,384]{4,3,2,1,0:T(2,128)(2,1)S(1)}, bf16[2,2,4,1,384]{4,3,2,1,0:T(2,128)(2,1)S(1)}, u32[]{:S(2)}, u32[]{:S(2)}) %collective-permute-start) | collective-permute-done | bytes 12320 | tf_op jit(solution)/shard_map/ppermute | solution.py:52
  2.3 0.1 pad_maximum_fusion.refs_0_
  2.4 0.1 collective-permute-start.1
  2.5 5.0 %collective-permute-start.2 = (bf16[2,2,1,12,384]{4,3,2,1,0:T(8,128)(2,1)S(1)}, bf16[2,2,1,12,384]{4,3,2,1,0:T(8,128)(2,1)S(1)}, u32[]{:S(2)}, u32[]{:S(2)}) collective-permute-start(bf16[2,2,1,12,384]{4,3,2,1,0:T(8,128)(2,1)S(1)} %get-tuple-element.32), channel_id=1, source_target_pairs={{2,4},{4,2},{3,5},{5,3},{10,12},{12,10},{11,13},{13,11},{18,20},{2... | collective-permute-start | bytes 110600 | tf_op jit(solution)/shard_map/ppermute | solution.py:52
  7.5 0.7 %broadcast_in_dim.17.refs_3_.refs_6_ = f32[1,384]{1,0:T(1,128)S(1)} reshape(f32[384]{0:T(512)} %param.11) | data formatting | bytes 3072 | tf_op jit(solution)/shard_map/broadcast_in_dim | solution.py:412
  8.2 0.0 collective-permute-done.1.refs_1_
  8.2 1.4 %collective-permute-done.2.refs_2_ = bf16[2,2,1,12,384]{4,3,2,1,0:T(8,128)(2,1)S(1)} collective-permute-done((bf16[2,2,1,12,384]{4,3,2,1,0:T(8,128)(2,1)S(1)}, bf16[2,2,1,12,384]{4,3,2,1,0:T(8,128)(2,1)S(1)}, u32[]{:S(2)}, u32[]{:S(2)}) %collective-permute-start.2) | collective-permute-done | bytes 36896 | tf_op jit(solution)/shard_map/ppermute | solution.py:52
  9.6 0.5 pack.1
  10.1 1.6 %collective-permute-start.3 = (bf16[2,72,512]{2,1,0:T(8,128)(2,1)S(1)}, bf16[2,72,512]{2,1,0:T(8,128)(2,1)S(1)}, u32[]{:S(2)}, u32[]{:S(2)}) collective-permute-start(bf16[2,72,512]{2,1,0:T(8,128)(2,1)S(1)} %get-tuple-element.18), channel_id=1, source_target_pairs={{0,8},{8,0},{16,24},{24,16},{1,9},{9,1},{17,25},{25,17},{2,10},{10... | collective-permute-start | bytes 442376 | tf_op jit(solution)/shard_map/ppermute | solution.py:36
  11.6 1.5 %collective-permute-start.4 = (bf16[2,72,512]{2,1,0:T(8,128)(2,1)S(1)}, bf16[2,72,512]{2,1,0:T(8,128)(2,1)S(1)}, u32[]{:S(2)}, u32[]{:S(2)}) collective-permute-start(bf16[2,72,512]{2,1,0:T(8,128)(2,1)S(1)} %get-tuple-element.19), channel_id=1, source_target_pairs={{0,16},{8,24},{16,0},{24,8},{1,17},{9,25},{17,1},{25,9},{2,18},{10... | collective-permute-start | bytes 442376 | tf_op jit(solution)/shard_map/ppermute | solution.py:36
  13.1 0.5 collective-permute-start.5
  13.6 2.8 %collective-permute-done.3.refs_1_ = bf16[2,72,512]{2,1,0:T(8,128)(2,1)S(1)} collective-permute-done((bf16[2,72,512]{2,1,0:T(8,128)(2,1)S(1)}, bf16[2,72,512]{2,1,0:T(8,128)(2,1)S(1)}, u32[]{:S(2)}, u32[]{:S(2)}) %collective-permute-start.3) | collective-permute-done | bytes 147488 | tf_op jit(solution)/shard_map/ppermute | solution.py:36
  16.4 3.5 %collective-permute-done.4.refs_2_ = bf16[2,72,512]{2,1,0:T(8,128)(2,1)S(1)} collective-permute-done((bf16[2,72,512]{2,1,0:T(8,128)(2,1)S(1)}, bf16[2,72,512]{2,1,0:T(8,128)(2,1)S(1)}, u32[]{:S(2)}, u32[]{:S(2)}) %collective-permute-start.4) | collective-permute-done | bytes 147488 | tf_op jit(solution)/shard_map/ppermute | solution.py:36
  19.9 0.0 collective-permute-done.5.refs_3_
  19.9 1.6 %copy-done = bf16[3,3,3,96,384]{4,3,2,1,0:T(8,128)(2,1)S(1)} copy-done((bf16[3,3,3,96,384]{4,3,2,1,0:T(8,128)(2,1)S(1)}, bf16[3,3,3,96,384]{4,3,2,1,0:T(8,128)(2,1)}, u32[]{:S(2)}) %copy-start) | copy-done | bytes 1990680
  21.4 1.6 %copy-done.3 = bf16[3,3,3,96,384]{4,3,2,1,0:T(8,128)(2,1)S(1)} copy-done((bf16[3,3,3,96,384]{4,3,2,1,0:T(8,128)(2,1)S(1)}, bf16[3,3,3,96,384]{4,3,2,1,0:T(8,128)(2,1)}, u32[]{:S(2)}) %copy-start.3) | copy-done | bytes 1990680
  23.0 3.6 %both.1 = (bf16[2,40,512]{2,1,0:T(8,128)(2,1)S(1)}, bf16[2,40,512]{2,1,0:T(8,128)(2,1)S(1)}, bf16[2,40,512]{2,1,0:T(8,128)(2,1)S(1)}, bf16[2,40,512]{2,1,0:T(8,128)(2,1)S(1)}) custom-call(bf16[2,72,512]{2,1,0:T(8,128)(2,1)S(1)} %get-tuple-element.17.refs_0_, bf16[2,72,512]{2,1,0:T(8,128)(2,1)S(1)} %collective-permute-done.3.refs_1_, ...), custom_call_target="tpu_custom_call" | custom-call | flops 1274019840 | bytes 4898816 | tf_op jit(solution)/shard_map/both/pallas_call | solution.py:387
  26.6 0.7 %collective-permute-start.6 = (bf16[2,40,512]{2,1,0:T(8,128)(2,1)S(1)}, bf16[2,40,512]{2,1,0:T(8,128)(2,1)S(1)}, u32[]{:S(2)}, u32[]{:S(2)}) collective-permute-start(bf16[2,40,512]{2,1,0:T(8,128)(2,1)S(1)} %get-tuple-element.22), channel_id=1, source_target_pairs={{0,8},{8,0},{16,24},{24,16},{1,9},{9,1},{17,25},{25,17},{2,10},{10... | collective-permute-start | bytes 245768 | tf_op jit(solution)/shard_map/ppermute | solution.py:36
  27.3 0.8 %collective-permute-start.7 = (bf16[2,40,512]{2,1,0:T(8,128)(2,1)S(1)}, bf16[2,40,512]{2,1,0:T(8,128)(2,1)S(1)}, u32[]{:S(2)}, u32[]{:S(2)}) collective-permute-start(bf16[2,40,512]{2,1,0:T(8,128)(2,1)S(1)} %get-tuple-element.23), channel_id=1, source_target_pairs={{0,16},{8,24},{16,0},{24,8},{1,17},{9,25},{17,1},{25,9},{2,18},{10... | collective-permute-start | bytes 245768 | tf_op jit(solution)/shard_map/ppermute | solution.py:36
  28.1 2.0 %collective-permute-start.8 = (bf16[2,40,512]{2,1,0:T(8,128)(2,1)S(1)}, bf16[2,40,512]{2,1,0:T(8,128)(2,1)S(1)}, u32[]{:S(2)}, u32[]{:S(2)}) collective-permute-start(bf16[2,40,512]{2,1,0:T(8,128)(2,1)S(1)} %get-tuple-element.24), channel_id=1, source_target_pairs={{0,24},{8,16},{16,8},{24,0},{1,25},{9,17},{17,9},{25,1},{2,26},{10... | collective-permute-start | bytes 245768 | tf_op jit(solution)/shard_map/ppermute | solution.py:36
  30.1 0.9 %collective-permute-done.6.refs_1_ = bf16[2,40,512]{2,1,0:T(8,128)(2,1)S(1)} collective-permute-done((bf16[2,40,512]{2,1,0:T(8,128)(2,1)S(1)}, bf16[2,40,512]{2,1,0:T(8,128)(2,1)S(1)}, u32[]{:S(2)}, u32[]{:S(2)}) %collective-permute-start.6) | collective-permute-done | bytes 81952 | tf_op jit(solution)/shard_map/ppermute | solution.py:36
  31.1 0.6 %collective-permute-done.7.refs_2_ = bf16[2,40,512]{2,1,0:T(8,128)(2,1)S(1)} collective-permute-done((bf16[2,40,512]{2,1,0:T(8,128)(2,1)S(1)}, bf16[2,40,512]{2,1,0:T(8,128)(2,1)S(1)}, u32[]{:S(2)}, u32[]{:S(2)}) %collective-permute-start.7) | collective-permute-done | bytes 81952 | tf_op jit(solution)/shard_map/ppermute | solution.py:36
  31.7 1.7 %collective-permute-done.8.refs_3_ = bf16[2,40,512]{2,1,0:T(8,128)(2,1)S(1)} collective-permute-done((bf16[2,40,512]{2,1,0:T(8,128)(2,1)S(1)}, bf16[2,40,512]{2,1,0:T(8,128)(2,1)S(1)}, u32[]{:S(2)}, u32[]{:S(2)}) %collective-permute-start.8) | collective-permute-done | bytes 81952 | tf_op jit(solution)/shard_map/ppermute | solution.py:36
  33.4 0.4 middle.1
  33.9 0.1 collective-permute-start.9
  33.9 1.2 %collective-permute-done.9 = bf16[2,4,1,384]{3,2,1,0:T(2,128)(2,1)S(1)} collective-permute-done((bf16[2,4,1,384]{3,2,1,0:T(2,128)(2,1)S(1)}, bf16[2,4,1,384]{3,2,1,0:T(2,128)(2,1)S(1)}, u32[]{:S(2)}, u32[]{:S(2)}) %collective-permute-start.9) | collective-permute-done | bytes 6176 | tf_op jit(solution)/shard_map/ppermute | solution.py:52
  35.2 0.1 collective-permute-start.11
  35.3 3.6 %collective-permute-start.10 = (bf16[2,1,12,384]{3,2,1,0:T(8,128)(2,1)S(1)}, bf16[2,1,12,384]{3,2,1,0:T(8,128)(2,1)S(1)}, u32[]{:S(2)}, u32[]{:S(2)}) collective-permute-start(bf16[2,1,12,384]{3,2,1,0:T(8,128)(2,1)S(1)} %get-tuple-element.29), channel_id=1, source_target_pairs={{2,4},{4,2},{3,5},{5,3},{10,12},{12,10},{11,13},{13,11},{18,20},{2... | collective-permute-start | bytes 55304 | tf_op jit(solution)/shard_map/ppermute | solution.py:52
  38.9 0.2 collective-permute-done.11
  39.1 1.9 %collective-permute-done.10 = bf16[2,1,12,384]{3,2,1,0:T(8,128)(2,1)S(1)} collective-permute-done((bf16[2,1,12,384]{3,2,1,0:T(8,128)(2,1)S(1)}, bf16[2,1,12,384]{3,2,1,0:T(8,128)(2,1)S(1)}, u32[]{:S(2)}, u32[]{:S(2)}) %collective-permute-start.10) | collective-permute-done | bytes 18464 | tf_op jit(solution)/shard_map/ppermute | solution.py:52
  41.0 0.1 pad_maximum_fusion.1
  41.1 0.1 copy.12
  41.2 1.7 %collective-permute-start.12 = (bf16[2,72,384]{2,1,0:T(8,128)(2,1)S(1)}, bf16[2,72,384]{2,1,0:T(8,128)(2,1)S(1)}, u32[]{:S(2)}, u32[]{:S(2)}) collective-permute-start(bf16[2,72,384]{2,1,0:T(8,128)(2,1)S(1)} %copy.16.refs_0_), channel_id=1, source_target_pairs={{0,8},{8,0},{16,24},{24,16},{1,9},{9,1},{17,25},{25,17},{2,10},{10... | collective-permute-start | bytes 331784 | tf_op jit(solution)/shard_map/ppermute | solution.py:36
  42.9 1.0 %collective-permute-start.13 = (bf16[2,72,384]{2,1,0:T(8,128)(2,1)S(1)}, bf16[2,72,384]{2,1,0:T(8,128)(2,1)S(1)}, u32[]{:S(2)}, u32[]{:S(2)}) collective-permute-start(bf16[2,72,384]{2,1,0:T(8,128)(2,1)S(1)} %copy.16.refs_0_), channel_id=1, source_target_pairs={{0,16},{8,24},{16,0},{24,8},{1,17},{9,25},{17,1},{25,9},{2,18},{10... | collective-permute-start | bytes 331784 | tf_op jit(solution)/shard_map/ppermute | solution.py:36
  43.9 0.9 %collective-permute-start.14 = (bf16[2,72,384]{2,1,0:T(8,128)(2,1)S(1)}, bf16[2,72,384]{2,1,0:T(8,128)(2,1)S(1)}, u32[]{:S(2)}, u32[]{:S(2)}) collective-permute-start(bf16[2,72,384]{2,1,0:T(8,128)(2,1)S(1)} %copy.16.refs_0_), channel_id=1, source_target_pairs={{0,24},{8,16},{16,8},{24,0},{1,25},{9,17},{17,9},{25,1},{2,26},{10... | collective-permute-start | bytes 331784 | tf_op jit(solution)/shard_map/ppermute | solution.py:36
  44.8 1.8 %collective-permute-done.12.refs_1_ = bf16[2,72,384]{2,1,0:T(8,128)(2,1)S(1)} collective-permute-done((bf16[2,72,384]{2,1,0:T(8,128)(2,1)S(1)}, bf16[2,72,384]{2,1,0:T(8,128)(2,1)S(1)}, u32[]{:S(2)}, u32[]{:S(2)}) %collective-permute-start.12) | collective-permute-done | bytes 110624 | tf_op jit(solution)/shard_map/ppermute | solution.py:36
  46.5 3.2 %collective-permute-done.13.refs_2_ = bf16[2,72,384]{2,1,0:T(8,128)(2,1)S(1)} collective-permute-done((bf16[2,72,384]{2,1,0:T(8,128)(2,1)S(1)}, bf16[2,72,384]{2,1,0:T(8,128)(2,1)S(1)}, u32[]{:S(2)}, u32[]{:S(2)}) %collective-permute-start.13) | collective-permute-done | bytes 110624 | tf_op jit(solution)/shard_map/ppermute | solution.py:36
  49.8 1.8 %back.1 = (bf16[2,40,128]{2,1,0:T(8,128)(2,1)S(1)}, bf16[2,40,128]{2,1,0:T(8,128)(2,1)S(1)}, bf16[2,40,128]{2,1,0:T(8,128)(2,1)S(1)}, bf16[2,40,128]{2,1,0:T(8,128)(2,1)S(1)}) custom-call(bf16[2,72,384]{2,1,0:T(8,128)(2,1)S(1)} %copy.16.refs_0_, bf16[2,72,384]{2,1,0:T(8,128)(2,1)S(1)} %collective-permute-done.12.refs_1_, ...), custom_call_target="tpu_custom_call" | custom-call | flops 637009920 | bytes 2514944 | tf_op jit(solution)/shard_map/back/pallas_call | solution.py:387
  51.6 0.5 collective-permute-start.15
  52.0 0.8 %collective-permute-start.16 = (bf16[2,40,128]{2,1,0:T(8,128)(2,1)S(1)}, bf16[2,40,128]{2,1,0:T(8,128)(2,1)S(1)}, u32[]{:S(2)}, u32[]{:S(2)}) collective-permute-start(bf16[2,40,128]{2,1,0:T(8,128)(2,1)S(1)} %get-tuple-element.27), channel_id=1, source_target_pairs={{0,16},{8,24},{16,0},{24,8},{1,17},{9,25},{17,1},{25,9},{2,18},{10... | collective-permute-start | bytes 61448 | tf_op jit(solution)/shard_map/ppermute | solution.py:36
  52.8 2.3 %collective-permute-start.17 = (bf16[2,40,128]{2,1,0:T(8,128)(2,1)S(1)}, bf16[2,40,128]{2,1,0:T(8,128)(2,1)S(1)}, u32[]{:S(2)}, u32[]{:S(2)}) collective-permute-start(bf16[2,40,128]{2,1,0:T(8,128)(2,1)S(1)} %get-tuple-element.28), channel_id=1, source_target_pairs={{0,24},{8,16},{16,8},{24,0},{1,25},{9,17},{17,9},{25,1},{2,26},{10... | collective-permute-start | bytes 61448 | tf_op jit(solution)/shard_map/ppermute | solution.py:36
  55.1 0.3 collective-permute-done.15.refs_1_
  55.4 0.4 collective-permute-done.16.refs_2_
  55.8 1.7 %collective-permute-done.17.refs_3_ = bf16[2,40,128]{2,1,0:T(8,128)(2,1)S(1)} collective-permute-done((bf16[2,40,128]{2,1,0:T(8,128)(2,1)S(1)}, bf16[2,40,128]{2,1,0:T(8,128)(2,1)S(1)}, u32[]{:S(2)}, u32[]{:S(2)}) %collective-permute-start.17) | collective-permute-done | bytes 20512 | tf_op jit(solution)/shard_map/ppermute | solution.py:36
  57.5 1.0 %final.1 = bf16[2,10,4,384]{3,2,1,0:T(4,128)(2,1)} custom-call(bf16[2,40,128]{2,1,0:T(8,128)(2,1)S(1)} %get-tuple-element.25.refs_0_, bf16[2,40,128]{2,1,0:T(8,128)(2,1)S(1)} %collective-permute-done.15.refs_1_, bf16[2,40,128]{2,1,0:T(8,128)(2,1)S(1)} %collective-permute-done.16.refs_2_, bf16[2,40,128]{2,1,0:T(8,128)(2,1)S(1)} %collective-permute-done.17.refs_3_, ...), custom_call_target="tpu_custom_call" | custom-call | bytes 267776 | tf_op jit(solution)/shard_map/final/pallas_call | solution.py:387
  (21 shorter events, 0.2 us)
Async XLA Ops:
  0.9 1.3 %collective-permute-start = (bf16[2,2,4,1,384]{4,3,2,1,0:T(2,128)(2,1)S(1)}, bf16[2,2,4,1,384]{4,3,2,1,0:T(2,128)(2,1)S(1)}, u32[]{:S(2)}, u32[]{:S(2)}) collective-permute-start(bf16[2,2,4,1,384]{4,3,2,1,0:T(2,128)(2,1)S(1)} %broadcast_select_fusion.4), channel_id=1, source_target_pairs={{0,1},{1,0},{2,3},{3,2},{4,5},{5,4},{6,7},{7,6},{8,9},{9,8},{10,11... | collective-permute-start | bytes 36872 | tf_op jit(solution)/shard_map/ppermute | solution.py:52
  2.4 5.8 %collective-permute-start.1 = (bf16[2,2,1,12,384]{4,3,2,1,0:T(8,128)(2,1)S(1)}, bf16[2,2,1,12,384]{4,3,2,1,0:T(8,128)(2,1)S(1)}, u32[]{:S(2)}, u32[]{:S(2)}) collective-permute-start(bf16[2,2,1,12,384]{4,3,2,1,0:T(8,128)(2,1)S(1)} %get-tuple-element.33), channel_id=1, source_target_pairs={{0,2},{4,6},{2,0},{6,4},{1,3},{5,7},{3,1},{7,5},{8,10},{12,14},{10... | collective-permute-start | bytes 110600 | tf_op jit(solution)/shard_map/ppermute | solution.py:52
  2.5 7.1 %collective-permute-start.2 = (bf16[2,2,1,12,384]{4,3,2,1,0:T(8,128)(2,1)S(1)}, bf16[2,2,1,12,384]{4,3,2,1,0:T(8,128)(2,1)S(1)}, u32[]{:S(2)}, u32[]{:S(2)}) collective-permute-start(bf16[2,2,1,12,384]{4,3,2,1,0:T(8,128)(2,1)S(1)} %get-tuple-element.32), channel_id=1, source_target_pairs={{2,4},{4,2},{3,5},{5,3},{10,12},{12,10},{11,13},{13,11},{18,20},{2... | collective-permute-start | bytes 110600 | tf_op jit(solution)/shard_map/ppermute | solution.py:52
  10.1 6.3 %collective-permute-start.3 = (bf16[2,72,512]{2,1,0:T(8,128)(2,1)S(1)}, bf16[2,72,512]{2,1,0:T(8,128)(2,1)S(1)}, u32[]{:S(2)}, u32[]{:S(2)}) collective-permute-start(bf16[2,72,512]{2,1,0:T(8,128)(2,1)S(1)} %get-tuple-element.18), channel_id=1, source_target_pairs={{0,8},{8,0},{16,24},{24,16},{1,9},{9,1},{17,25},{25,17},{2,10},{10... | collective-permute-start | bytes 442376 | tf_op jit(solution)/shard_map/ppermute | solution.py:36
  11.6 8.3 %collective-permute-start.4 = (bf16[2,72,512]{2,1,0:T(8,128)(2,1)S(1)}, bf16[2,72,512]{2,1,0:T(8,128)(2,1)S(1)}, u32[]{:S(2)}, u32[]{:S(2)}) collective-permute-start(bf16[2,72,512]{2,1,0:T(8,128)(2,1)S(1)} %get-tuple-element.19), channel_id=1, source_target_pairs={{0,16},{8,24},{16,0},{24,8},{1,17},{9,25},{17,1},{25,9},{2,18},{10... | collective-permute-start | bytes 442376 | tf_op jit(solution)/shard_map/ppermute | solution.py:36
  13.1 6.7 %collective-permute-start.5 = (bf16[2,72,512]{2,1,0:T(8,128)(2,1)S(1)}, bf16[2,72,512]{2,1,0:T(8,128)(2,1)S(1)}, u32[]{:S(2)}, u32[]{:S(2)}) collective-permute-start(bf16[2,72,512]{2,1,0:T(8,128)(2,1)S(1)} %get-tuple-element.20), channel_id=1, source_target_pairs={{0,24},{8,16},{16,8},{24,0},{1,25},{9,17},{17,9},{25,1},{2,26},{10... | collective-permute-start | bytes 442376 | tf_op jit(solution)/shard_map/ppermute | solution.py:36
  19.9 1.6 %copy-start = (bf16[3,3,3,96,384]{4,3,2,1,0:T(8,128)(2,1)S(1)}, bf16[3,3,3,96,384]{4,3,2,1,0:T(8,128)(2,1)}, u32[]{:S(2)}) copy-start(bf16[3,3,3,96,384]{4,3,2,1,0:T(8,128)(2,1)} %refs_4_.3) | copy-start | bytes 5971972
  21.4 1.6 %copy-start.3 = (bf16[3,3,3,96,384]{4,3,2,1,0:T(8,128)(2,1)S(1)}, bf16[3,3,3,96,384]{4,3,2,1,0:T(8,128)(2,1)}, u32[]{:S(2)}) copy-start(bf16[3,3,3,96,384]{4,3,2,1,0:T(8,128)(2,1)} %refs_5_.1) | copy-start | bytes 5971972
  23.0 7.1 %copy-start.4 = (f32[384]{0:T(512)S(1)}, f32[384]{0:T(512)}, u32[]{:S(2)}) copy-start(f32[384]{0:T(512)} %param.12) | copy-start | bytes 4612
  23.0 7.1 %copy-start.5 = (f32[384]{0:T(512)S(1)}, f32[384]{0:T(512)}, u32[]{:S(2)}) copy-start(f32[384]{0:T(512)} %param.13) | copy-start | bytes 4612
  26.6 4.5 %collective-permute-start.6 = (bf16[2,40,512]{2,1,0:T(8,128)(2,1)S(1)}, bf16[2,40,512]{2,1,0:T(8,128)(2,1)S(1)}, u32[]{:S(2)}, u32[]{:S(2)}) collective-permute-start(bf16[2,40,512]{2,1,0:T(8,128)(2,1)S(1)} %get-tuple-element.22), channel_id=1, source_target_pairs={{0,8},{8,0},{16,24},{24,16},{1,9},{9,1},{17,25},{25,17},{2,10},{10... | collective-permute-start | bytes 245768 | tf_op jit(solution)/shard_map/ppermute | solution.py:36
  27.3 4.4 %collective-permute-start.7 = (bf16[2,40,512]{2,1,0:T(8,128)(2,1)S(1)}, bf16[2,40,512]{2,1,0:T(8,128)(2,1)S(1)}, u32[]{:S(2)}, u32[]{:S(2)}) collective-permute-start(bf16[2,40,512]{2,1,0:T(8,128)(2,1)S(1)} %get-tuple-element.23), channel_id=1, source_target_pairs={{0,16},{8,24},{16,0},{24,8},{1,17},{9,25},{17,1},{25,9},{2,18},{10... | collective-permute-start | bytes 245768 | tf_op jit(solution)/shard_map/ppermute | solution.py:36
  28.1 5.3 %collective-permute-start.8 = (bf16[2,40,512]{2,1,0:T(8,128)(2,1)S(1)}, bf16[2,40,512]{2,1,0:T(8,128)(2,1)S(1)}, u32[]{:S(2)}, u32[]{:S(2)}) collective-permute-start(bf16[2,40,512]{2,1,0:T(8,128)(2,1)S(1)} %get-tuple-element.24), channel_id=1, source_target_pairs={{0,24},{8,16},{16,8},{24,0},{1,25},{9,17},{17,9},{25,1},{2,26},{10... | collective-permute-start | bytes 245768 | tf_op jit(solution)/shard_map/ppermute | solution.py:36
  33.4 24.1 %copy-start.1 = (bf16[2,4,10,384]{3,1,2,0:T(4,128)(2,1)S(1)}, bf16[2,4,10,384]{3,1,2,0:T(4,128)(2,1)}, u32[]{:S(2)}) copy-start(bf16[2,4,10,384]{3,1,2,0:T(4,128)(2,1)} %param.8) | copy-start | bytes 184324
  33.4 24.1 %copy-start.2 = (bf16[2,4,10,384]{3,1,2,0:T(4,128)(2,1)S(1)}, bf16[2,4,10,384]{3,1,2,0:T(4,128)(2,1)}, u32[]{:S(2)}) copy-start(bf16[2,4,10,384]{3,1,2,0:T(4,128)(2,1)} %param.7) | copy-start | bytes 184324
  33.9 1.2 %collective-permute-start.9 = (bf16[2,4,1,384]{3,2,1,0:T(2,128)(2,1)S(1)}, bf16[2,4,1,384]{3,2,1,0:T(2,128)(2,1)S(1)}, u32[]{:S(2)}, u32[]{:S(2)}) collective-permute-start(bf16[2,4,1,384]{3,2,1,0:T(2,128)(2,1)S(1)} %broadcast_select_fusion.7), channel_id=1, source_target_pairs={{0,1},{1,0},{2,3},{3,2},{4,5},{5,4},{6,7},{7,6},{8,9},{9,8},{10,11... | collective-permute-start | bytes 18440 | tf_op jit(solution)/shard_map/ppermute | solution.py:52
  35.2 3.9 %collective-permute-start.11 = (bf16[2,1,12,384]{3,2,1,0:T(8,128)(2,1)S(1)}, bf16[2,1,12,384]{3,2,1,0:T(8,128)(2,1)S(1)}, u32[]{:S(2)}, u32[]{:S(2)}) collective-permute-start(bf16[2,1,12,384]{3,2,1,0:T(8,128)(2,1)S(1)} %broadcast_select_fusion.10), channel_id=1, source_target_pairs={{0,2},{4,6},{2,0},{6,4},{1,3},{5,7},{3,1},{7,5},{8,10},{12,14},{10... | collective-permute-start | bytes 55304 | tf_op jit(solution)/shard_map/ppermute | solution.py:52
  35.3 5.7 %collective-permute-start.10 = (bf16[2,1,12,384]{3,2,1,0:T(8,128)(2,1)S(1)}, bf16[2,1,12,384]{3,2,1,0:T(8,128)(2,1)S(1)}, u32[]{:S(2)}, u32[]{:S(2)}) collective-permute-start(bf16[2,1,12,384]{3,2,1,0:T(8,128)(2,1)S(1)} %get-tuple-element.29), channel_id=1, source_target_pairs={{2,4},{4,2},{3,5},{5,3},{10,12},{12,10},{11,13},{13,11},{18,20},{2... | collective-permute-start | bytes 55304 | tf_op jit(solution)/shard_map/ppermute | solution.py:52
  41.2 5.3 %collective-permute-start.12 = (bf16[2,72,384]{2,1,0:T(8,128)(2,1)S(1)}, bf16[2,72,384]{2,1,0:T(8,128)(2,1)S(1)}, u32[]{:S(2)}, u32[]{:S(2)}) collective-permute-start(bf16[2,72,384]{2,1,0:T(8,128)(2,1)S(1)} %copy.16.refs_0_), channel_id=1, source_target_pairs={{0,8},{8,0},{16,24},{24,16},{1,9},{9,1},{17,25},{25,17},{2,10},{10... | collective-permute-start | bytes 331784 | tf_op jit(solution)/shard_map/ppermute | solution.py:36
  42.9 6.9 %collective-permute-start.13 = (bf16[2,72,384]{2,1,0:T(8,128)(2,1)S(1)}, bf16[2,72,384]{2,1,0:T(8,128)(2,1)S(1)}, u32[]{:S(2)}, u32[]{:S(2)}) collective-permute-start(bf16[2,72,384]{2,1,0:T(8,128)(2,1)S(1)} %copy.16.refs_0_), channel_id=1, source_target_pairs={{0,16},{8,24},{16,0},{24,8},{1,17},{9,25},{17,1},{25,9},{2,18},{10... | collective-permute-start | bytes 331784 | tf_op jit(solution)/shard_map/ppermute | solution.py:36
  43.9 5.9 %collective-permute-start.14 = (bf16[2,72,384]{2,1,0:T(8,128)(2,1)S(1)}, bf16[2,72,384]{2,1,0:T(8,128)(2,1)S(1)}, u32[]{:S(2)}, u32[]{:S(2)}) collective-permute-start(bf16[2,72,384]{2,1,0:T(8,128)(2,1)S(1)} %copy.16.refs_0_), channel_id=1, source_target_pairs={{0,24},{8,16},{16,8},{24,0},{1,25},{9,17},{17,9},{25,1},{2,26},{10... | collective-permute-start | bytes 331784 | tf_op jit(solution)/shard_map/ppermute | solution.py:36
  51.6 3.8 %collective-permute-start.15 = (bf16[2,40,128]{2,1,0:T(8,128)(2,1)S(1)}, bf16[2,40,128]{2,1,0:T(8,128)(2,1)S(1)}, u32[]{:S(2)}, u32[]{:S(2)}) collective-permute-start(bf16[2,40,128]{2,1,0:T(8,128)(2,1)S(1)} %get-tuple-element.26), channel_id=1, source_target_pairs={{0,8},{8,0},{16,24},{24,16},{1,9},{9,1},{17,25},{25,17},{2,10},{10... | collective-permute-start | bytes 61448 | tf_op jit(solution)/shard_map/ppermute | solution.py:36
  52.0 3.8 %collective-permute-start.16 = (bf16[2,40,128]{2,1,0:T(8,128)(2,1)S(1)}, bf16[2,40,128]{2,1,0:T(8,128)(2,1)S(1)}, u32[]{:S(2)}, u32[]{:S(2)}) collective-permute-start(bf16[2,40,128]{2,1,0:T(8,128)(2,1)S(1)} %get-tuple-element.27), channel_id=1, source_target_pairs={{0,16},{8,24},{16,0},{24,8},{1,17},{9,25},{17,1},{25,9},{2,18},{10... | collective-permute-start | bytes 61448 | tf_op jit(solution)/shard_map/ppermute | solution.py:36
  52.8 4.7 %collective-permute-start.17 = (bf16[2,40,128]{2,1,0:T(8,128)(2,1)S(1)}, bf16[2,40,128]{2,1,0:T(8,128)(2,1)S(1)}, u32[]{:S(2)}, u32[]{:S(2)}) collective-permute-start(bf16[2,40,128]{2,1,0:T(8,128)(2,1)S(1)} %get-tuple-element.28), channel_id=1, source_target_pairs={{0,24},{8,16},{16,8},{24,0},{1,25},{9,17},{17,9},{25,1},{2,26},{10... | collective-permute-start | bytes 61448 | tf_op jit(solution)/shard_map/ppermute | solution.py:36

commit v3 on v2

--- a/solution.py
+++ b/solution.py
@@ -380,7 +380,7 @@
     return sum(math.prod(s.shape) * s.dtype.itemsize for s in structs)
 
 
-def call(kernel, outs, scratch=(), flops=0, spare=2, name=None):
+def call(kernel, outs, scratch=(), flops=0, spare=2, covered=0, name=None):
     def run(*operands):
         held = size_of(outs) + size_of(operands)
         grant = 2 * held + size_of(scratch) + spare * 2**20
@@ -389,7 +389,7 @@
             out_shape=outs,
             scratch_shapes=list(scratch),
             cost_estimate=pl.CostEstimate(
-                flops=flops, bytes_accessed=held, transcendentals=0
+                flops=flops + covered, bytes_accessed=held, transcendentals=0
             ),
             compiler_params=pltpu.CompilerParams(vmem_limit_bytes=min(grant, 60 * 2**20)),
             name=name,
@@ -417,6 +417,7 @@
         functools.partial(pack_kernel, peers, width),
         [struct((frames, plane, channels + wide), bf16)] * peers,
         [pltpu.VMEM((2, plane, channels), f32)],
+        covered=4 * 10**9,
         name="pack",
     )(strips, *row_edges, gain_one)
     got = tm_exchange(packed)

time: 59.4 us -> 56.2 us (0.946)
  local copies, waits for them, and re-layouts: 4.8 us -> 1.7 us
    unnamed x12, local copies, waits for them, and re-layouts: 3.12 us -> 0.03 us
where the time goes in v3:
time: 56.2 us; the launch traced here: 55.5 us
  starting transfers between devices  23.2 us (41%)
  waiting for transfers between devices  22.7 us (40%)
  Pallas kernels  7.28 us (13%)
  local copies, waits for them, and re-layouts  1.7 us (3%)
    ppermute x12, waiting for transfers between devices, tm_exchange(): got.append(lax.ppermute(blocks[step], 'tm', pairs))  16.9 us
    ppermute x12, starting transfers between devices, tm_exchange(): got.append(lax.ppermute(blocks[step], 'tm', pairs))  14.2 us
    ppermute x6, starting transfers between devices, halo_swaps(): got.append(lax.ppermute(jnp.where(even, *value), axis, pairs))  8.97 us
    pallas_call x5, Pallas kernels, run(): pl.pallas_call(kernel, out_shape=outs, scratch_shapes=list(scratch), cost...  7.28 us
    ppermute x6, waiting for transfers between devices, halo_swaps(): got.append(lax.ppermute(jnp.where(even, *value), axis, pairs))  5.77 us
  transfers between devices with their start and end apart: 18, of which 15 were waited for; matrix products, arithmetic and copies ran while one was open for 1% of the time, Pallas kernels for 0%

profile of v3, /device:TPU:8, one launch (start us, length us, event | category | flops | bytes accessed | tf_op | source)
XLA Modules:
  0.0 55.5 jit_solution(1955212316756992030)
XLA Ops:
  0.0 0.9 %copy_bitcast_fusion = (bf16[1,2,4,10,384]{4,3,2,1,0:T(8,128)(2,1)S(1)}, bf16[1,2,4,10,384]{4,3,2,1,0:T(8,128)(2,1)S(1)}) fusion(bf16[2,4,10,384]{3,1,2,0:T(4,128)(2,1)} %param.8, bf16[2,4,10,384]{3,1,2,0:T(4,128)(2,1)} %param.7), kind=kLoop, calls=%fused_computation.2 | loop fusion | bytes 245760 | tf_op jit(solution)/shard_map/stack | solution.py:414
  0.9 0.1 broadcast_select_fusion.4
  0.9 0.1 collective-permute-start
  1.0 1.2 %collective-permute-done = bf16[2,2,4,1,384]{4,3,2,1,0:T(2,128)(2,1)S(1)} collective-permute-done((bf16[2,2,4,1,384]{4,3,2,1,0:T(2,128)(2,1)S(1)}, bf16[2,2,4,1,384]{4,3,2,1,0:T(2,128)(2,1)S(1)}, u32[]{:S(2)}, u32[]{:S(2)}) %collective-permute-start) | collective-permute-done | bytes 12320 | tf_op jit(solution)/shard_map/ppermute | solution.py:52
  2.3 0.1 pad_maximum_fusion.refs_0_
  2.4 0.1 collective-permute-start.1
  2.5 5.0 %collective-permute-start.2 = (bf16[2,2,1,12,384]{4,3,2,1,0:T(8,128)(2,1)S(1)}, bf16[2,2,1,12,384]{4,3,2,1,0:T(8,128)(2,1)S(1)}, u32[]{:S(2)}, u32[]{:S(2)}) collective-permute-start(bf16[2,2,1,12,384]{4,3,2,1,0:T(8,128)(2,1)S(1)} %get-tuple-element.32), channel_id=1, source_target_pairs={{2,4},{4,2},{3,5},{5,3},{10,12},{12,10},{11,13},{13,11},{18,20},{2... | collective-permute-start | bytes 110600 | tf_op jit(solution)/shard_map/ppermute | solution.py:52
  7.5 0.7 %broadcast_in_dim.17.refs_3_.refs_6_ = f32[1,384]{1,0:T(1,128)S(1)} reshape(f32[384]{0:T(512)} %param.11) | data formatting | bytes 3072 | tf_op jit(solution)/shard_map/broadcast_in_dim | solution.py:412
  8.2 0.0 collective-permute-done.1.refs_1_
  8.2 1.4 %collective-permute-done.2.refs_2_ = bf16[2,2,1,12,384]{4,3,2,1,0:T(8,128)(2,1)S(1)} collective-permute-done((bf16[2,2,1,12,384]{4,3,2,1,0:T(8,128)(2,1)S(1)}, bf16[2,2,1,12,384]{4,3,2,1,0:T(8,128)(2,1)S(1)}, u32[]{:S(2)}, u32[]{:S(2)}) %collective-permute-start.2) | collective-permute-done | bytes 36896 | tf_op jit(solution)/shard_map/ppermute | solution.py:52
  9.6 0.5 pack.1
  10.1 1.6 %collective-permute-start.3 = (bf16[2,72,512]{2,1,0:T(8,128)(2,1)S(1)}, bf16[2,72,512]{2,1,0:T(8,128)(2,1)S(1)}, u32[]{:S(2)}, u32[]{:S(2)}) collective-permute-start(bf16[2,72,512]{2,1,0:T(8,128)(2,1)S(1)} %get-tuple-element.18), channel_id=1, source_target_pairs={{0,8},{8,0},{16,24},{24,16},{1,9},{9,1},{17,25},{25,17},{2,10},{10... | collective-permute-start | bytes 442376 | tf_op jit(solution)/shard_map/ppermute | solution.py:36
  11.6 1.5 %collective-permute-start.4 = (bf16[2,72,512]{2,1,0:T(8,128)(2,1)S(1)}, bf16[2,72,512]{2,1,0:T(8,128)(2,1)S(1)}, u32[]{:S(2)}, u32[]{:S(2)}) collective-permute-start(bf16[2,72,512]{2,1,0:T(8,128)(2,1)S(1)} %get-tuple-element.19), channel_id=1, source_target_pairs={{0,16},{8,24},{16,0},{24,8},{1,17},{9,25},{17,1},{25,9},{2,18},{10... | collective-permute-start | bytes 442376 | tf_op jit(solution)/shard_map/ppermute | solution.py:36
  13.1 0.5 collective-permute-start.5
  13.6 2.8 %collective-permute-done.3.refs_1_ = bf16[2,72,512]{2,1,0:T(8,128)(2,1)S(1)} collective-permute-done((bf16[2,72,512]{2,1,0:T(8,128)(2,1)S(1)}, bf16[2,72,512]{2,1,0:T(8,128)(2,1)S(1)}, u32[]{:S(2)}, u32[]{:S(2)}) %collective-permute-start.3) | collective-permute-done | bytes 147488 | tf_op jit(solution)/shard_map/ppermute | solution.py:36
  16.4 3.5 %collective-permute-done.4.refs_2_ = bf16[2,72,512]{2,1,0:T(8,128)(2,1)S(1)} collective-permute-done((bf16[2,72,512]{2,1,0:T(8,128)(2,1)S(1)}, bf16[2,72,512]{2,1,0:T(8,128)(2,1)S(1)}, u32[]{:S(2)}, u32[]{:S(2)}) %collective-permute-start.4) | collective-permute-done | bytes 147488 | tf_op jit(solution)/shard_map/ppermute | solution.py:36
  19.9 0.0 collective-permute-done.5.refs_3_
  19.9 0.0 copy-start.4
  19.9 0.0 copy-start.5
  19.9 3.6 %both.1 = (bf16[2,40,512]{2,1,0:T(8,128)(2,1)S(1)}, bf16[2,40,512]{2,1,0:T(8,128)(2,1)S(1)}, bf16[2,40,512]{2,1,0:T(8,128)(2,1)S(1)}, bf16[2,40,512]{2,1,0:T(8,128)(2,1)S(1)}) custom-call(bf16[2,72,512]{2,1,0:T(8,128)(2,1)S(1)} %get-tuple-element.17.refs_0_, bf16[2,72,512]{2,1,0:T(8,128)(2,1)S(1)} %collective-permute-done.3.refs_1_, ...), custom_call_target="tpu_custom_call" | custom-call | flops 1274019840 | bytes 4898816 | tf_op jit(solution)/shard_map/both/pallas_call | solution.py:387
  23.5 0.7 %collective-permute-start.6 = (bf16[2,40,512]{2,1,0:T(8,128)(2,1)S(1)}, bf16[2,40,512]{2,1,0:T(8,128)(2,1)S(1)}, u32[]{:S(2)}, u32[]{:S(2)}) collective-permute-start(bf16[2,40,512]{2,1,0:T(8,128)(2,1)S(1)} %get-tuple-element.22), channel_id=1, source_target_pairs={{0,8},{8,0},{16,24},{24,16},{1,9},{9,1},{17,25},{25,17},{2,10},{10... | collective-permute-start | bytes 245768 | tf_op jit(solution)/shard_map/ppermute | solution.py:36
  24.2 0.8 %collective-permute-start.7 = (bf16[2,40,512]{2,1,0:T(8,128)(2,1)S(1)}, bf16[2,40,512]{2,1,0:T(8,128)(2,1)S(1)}, u32[]{:S(2)}, u32[]{:S(2)}) collective-permute-start(bf16[2,40,512]{2,1,0:T(8,128)(2,1)S(1)} %get-tuple-element.23), channel_id=1, source_target_pairs={{0,16},{8,24},{16,0},{24,8},{1,17},{9,25},{17,1},{25,9},{2,18},{10... | collective-permute-start | bytes 245768 | tf_op jit(solution)/shard_map/ppermute | solution.py:36
  25.0 2.0 %collective-permute-start.8 = (bf16[2,40,512]{2,1,0:T(8,128)(2,1)S(1)}, bf16[2,40,512]{2,1,0:T(8,128)(2,1)S(1)}, u32[]{:S(2)}, u32[]{:S(2)}) collective-permute-start(bf16[2,40,512]{2,1,0:T(8,128)(2,1)S(1)} %get-tuple-element.24), channel_id=1, source_target_pairs={{0,24},{8,16},{16,8},{24,0},{1,25},{9,17},{17,9},{25,1},{2,26},{10... | collective-permute-start | bytes 245768 | tf_op jit(solution)/shard_map/ppermute | solution.py:36
  27.1 0.9 %collective-permute-done.6.refs_1_ = bf16[2,40,512]{2,1,0:T(8,128)(2,1)S(1)} collective-permute-done((bf16[2,40,512]{2,1,0:T(8,128)(2,1)S(1)}, bf16[2,40,512]{2,1,0:T(8,128)(2,1)S(1)}, u32[]{:S(2)}, u32[]{:S(2)}) %collective-permute-start.6) | collective-permute-done | bytes 81952 | tf_op jit(solution)/shard_map/ppermute | solution.py:36
  28.0 0.6 %collective-permute-done.7.refs_2_ = bf16[2,40,512]{2,1,0:T(8,128)(2,1)S(1)} collective-permute-done((bf16[2,40,512]{2,1,0:T(8,128)(2,1)S(1)}, bf16[2,40,512]{2,1,0:T(8,128)(2,1)S(1)}, u32[]{:S(2)}, u32[]{:S(2)}) %collective-permute-start.7) | collective-permute-done | bytes 81952 | tf_op jit(solution)/shard_map/ppermute | solution.py:36
  28.6 1.7 %collective-permute-done.8.refs_3_ = bf16[2,40,512]{2,1,0:T(8,128)(2,1)S(1)} collective-permute-done((bf16[2,40,512]{2,1,0:T(8,128)(2,1)S(1)}, bf16[2,40,512]{2,1,0:T(8,128)(2,1)S(1)}, u32[]{:S(2)}, u32[]{:S(2)}) %collective-permute-start.8) | collective-permute-done | bytes 81952 | tf_op jit(solution)/shard_map/ppermute | solution.py:36
  30.4 0.4 middle.1
  30.8 0.1 collective-permute-start.9
  30.9 1.2 %collective-permute-done.9 = bf16[2,4,1,384]{3,2,1,0:T(2,128)(2,1)S(1)} collective-permute-done((bf16[2,4,1,384]{3,2,1,0:T(2,128)(2,1)S(1)}, bf16[2,4,1,384]{3,2,1,0:T(2,128)(2,1)S(1)}, u32[]{:S(2)}, u32[]{:S(2)}) %collective-permute-start.9) | collective-permute-done | bytes 6176 | tf_op jit(solution)/shard_map/ppermute | solution.py:52
  32.1 0.1 collective-permute-start.11
  32.2 3.6 %collective-permute-start.10 = (bf16[2,1,12,384]{3,2,1,0:T(8,128)(2,1)S(1)}, bf16[2,1,12,384]{3,2,1,0:T(8,128)(2,1)S(1)}, u32[]{:S(2)}, u32[]{:S(2)}) collective-permute-start(bf16[2,1,12,384]{3,2,1,0:T(8,128)(2,1)S(1)} %get-tuple-element.29), channel_id=1, source_target_pairs={{2,4},{4,2},{3,5},{5,3},{10,12},{12,10},{11,13},{13,11},{18,20},{2... | collective-permute-start | bytes 55304 | tf_op jit(solution)/shard_map/ppermute | solution.py:52
  35.9 0.2 collective-permute-done.11
  36.0 1.9 %collective-permute-done.10 = bf16[2,1,12,384]{3,2,1,0:T(8,128)(2,1)S(1)} collective-permute-done((bf16[2,1,12,384]{3,2,1,0:T(8,128)(2,1)S(1)}, bf16[2,1,12,384]{3,2,1,0:T(8,128)(2,1)S(1)}, u32[]{:S(2)}, u32[]{:S(2)}) %collective-permute-start.10) | collective-permute-done | bytes 18464 | tf_op jit(solution)/shard_map/ppermute | solution.py:52
  37.9 0.1 pad_maximum_fusion.1
  38.0 0.1 copy.12
  38.1 1.7 %collective-permute-start.12 = (bf16[2,72,384]{2,1,0:T(8,128)(2,1)S(1)}, bf16[2,72,384]{2,1,0:T(8,128)(2,1)S(1)}, u32[]{:S(2)}, u32[]{:S(2)}) collective-permute-start(bf16[2,72,384]{2,1,0:T(8,128)(2,1)S(1)} %copy.16.refs_0_), channel_id=1, source_target_pairs={{0,8},{8,0},{16,24},{24,16},{1,9},{9,1},{17,25},{25,17},{2,10},{10... | collective-permute-start | bytes 331784 | tf_op jit(solution)/shard_map/ppermute | solution.py:36
  39.8 1.0 %collective-permute-start.13 = (bf16[2,72,384]{2,1,0:T(8,128)(2,1)S(1)}, bf16[2,72,384]{2,1,0:T(8,128)(2,1)S(1)}, u32[]{:S(2)}, u32[]{:S(2)}) collective-permute-start(bf16[2,72,384]{2,1,0:T(8,128)(2,1)S(1)} %copy.16.refs_0_), channel_id=1, source_target_pairs={{0,16},{8,24},{16,0},{24,8},{1,17},{9,25},{17,1},{25,9},{2,18},{10... | collective-permute-start | bytes 331784 | tf_op jit(solution)/shard_map/ppermute | solution.py:36
  40.8 0.9 %collective-permute-start.14 = (bf16[2,72,384]{2,1,0:T(8,128)(2,1)S(1)}, bf16[2,72,384]{2,1,0:T(8,128)(2,1)S(1)}, u32[]{:S(2)}, u32[]{:S(2)}) collective-permute-start(bf16[2,72,384]{2,1,0:T(8,128)(2,1)S(1)} %copy.16.refs_0_), channel_id=1, source_target_pairs={{0,24},{8,16},{16,8},{24,0},{1,25},{9,17},{17,9},{25,1},{2,26},{10... | collective-permute-start | bytes 331784 | tf_op jit(solution)/shard_map/ppermute | solution.py:36
  41.7 1.8 %collective-permute-done.12.refs_1_ = bf16[2,72,384]{2,1,0:T(8,128)(2,1)S(1)} collective-permute-done((bf16[2,72,384]{2,1,0:T(8,128)(2,1)S(1)}, bf16[2,72,384]{2,1,0:T(8,128)(2,1)S(1)}, u32[]{:S(2)}, u32[]{:S(2)}) %collective-permute-start.12) | collective-permute-done | bytes 110624 | tf_op jit(solution)/shard_map/ppermute | solution.py:36
  43.4 3.2 %collective-permute-done.13.refs_2_ = bf16[2,72,384]{2,1,0:T(8,128)(2,1)S(1)} collective-permute-done((bf16[2,72,384]{2,1,0:T(8,128)(2,1)S(1)}, bf16[2,72,384]{2,1,0:T(8,128)(2,1)S(1)}, u32[]{:S(2)}, u32[]{:S(2)}) %collective-permute-start.13) | collective-permute-done | bytes 110624 | tf_op jit(solution)/shard_map/ppermute | solution.py:36
  46.7 1.8 %back.1 = (bf16[2,40,128]{2,1,0:T(8,128)(2,1)S(1)}, bf16[2,40,128]{2,1,0:T(8,128)(2,1)S(1)}, bf16[2,40,128]{2,1,0:T(8,128)(2,1)S(1)}, bf16[2,40,128]{2,1,0:T(8,128)(2,1)S(1)}) custom-call(bf16[2,72,384]{2,1,0:T(8,128)(2,1)S(1)} %copy.16.refs_0_, bf16[2,72,384]{2,1,0:T(8,128)(2,1)S(1)} %collective-permute-done.12.refs_1_, ...), custom_call_target="tpu_custom_call" | custom-call | flops 637009920 | bytes 2514944 | tf_op jit(solution)/shard_map/back/pallas_call | solution.py:387
  48.5 0.4 collective-permute-start.15
  48.9 0.8 %collective-permute-start.16 = (bf16[2,40,128]{2,1,0:T(8,128)(2,1)S(1)}, bf16[2,40,128]{2,1,0:T(8,128)(2,1)S(1)}, u32[]{:S(2)}, u32[]{:S(2)}) collective-permute-start(bf16[2,40,128]{2,1,0:T(8,128)(2,1)S(1)} %get-tuple-element.27), channel_id=1, source_target_pairs={{0,16},{8,24},{16,0},{24,8},{1,17},{9,25},{17,1},{25,9},{2,18},{10... | collective-permute-start | bytes 61448 | tf_op jit(solution)/shard_map/ppermute | solution.py:36
  49.8 2.3 %collective-permute-start.17 = (bf16[2,40,128]{2,1,0:T(8,128)(2,1)S(1)}, bf16[2,40,128]{2,1,0:T(8,128)(2,1)S(1)}, u32[]{:S(2)}, u32[]{:S(2)}) collective-permute-start(bf16[2,40,128]{2,1,0:T(8,128)(2,1)S(1)} %get-tuple-element.28), channel_id=1, source_target_pairs={{0,24},{8,16},{16,8},{24,0},{1,25},{9,17},{17,9},{25,1},{2,26},{10... | collective-permute-start | bytes 61448 | tf_op jit(solution)/shard_map/ppermute | solution.py:36
  52.0 0.3 collective-permute-done.15.refs_1_
  52.3 0.4 collective-permute-done.16.refs_2_
  52.7 1.7 %collective-permute-done.17.refs_3_ = bf16[2,40,128]{2,1,0:T(8,128)(2,1)S(1)} collective-permute-done((bf16[2,40,128]{2,1,0:T(8,128)(2,1)S(1)}, bf16[2,40,128]{2,1,0:T(8,128)(2,1)S(1)}, u32[]{:S(2)}, u32[]{:S(2)}) %collective-permute-start.17) | collective-permute-done | bytes 20512 | tf_op jit(solution)/shard_map/ppermute | solution.py:36
  54.5 1.0 %final.1 = bf16[2,10,4,384]{3,2,1,0:T(4,128)(2,1)} custom-call(bf16[2,40,128]{2,1,0:T(8,128)(2,1)S(1)} %get-tuple-element.25.refs_0_, bf16[2,40,128]{2,1,0:T(8,128)(2,1)S(1)} %collective-permute-done.15.refs_1_, bf16[2,40,128]{2,1,0:T(8,128)(2,1)S(1)} %collective-permute-done.16.refs_2_, bf16[2,40,128]{2,1,0:T(8,128)(2,1)S(1)} %collective-permute-done.17.refs_3_, ...), custom_call_target="tpu_custom_call" | custom-call | bytes 267776 | tf_op jit(solution)/shard_map/final/pallas_call | solution.py:387
  (21 shorter events, 0.2 us)
Async XLA Ops:
  0.9 1.3 %collective-permute-start = (bf16[2,2,4,1,384]{4,3,2,1,0:T(2,128)(2,1)S(1)}, bf16[2,2,4,1,384]{4,3,2,1,0:T(2,128)(2,1)S(1)}, u32[]{:S(2)}, u32[]{:S(2)}) collective-permute-start(bf16[2,2,4,1,384]{4,3,2,1,0:T(2,128)(2,1)S(1)} %broadcast_select_fusion.4), channel_id=1, source_target_pairs={{0,1},{1,0},{2,3},{3,2},{4,5},{5,4},{6,7},{7,6},{8,9},{9,8},{10,11... | collective-permute-start | bytes 36872 | tf_op jit(solution)/shard_map/ppermute | solution.py:52
  2.4 5.8 %collective-permute-start.1 = (bf16[2,2,1,12,384]{4,3,2,1,0:T(8,128)(2,1)S(1)}, bf16[2,2,1,12,384]{4,3,2,1,0:T(8,128)(2,1)S(1)}, u32[]{:S(2)}, u32[]{:S(2)}) collective-permute-start(bf16[2,2,1,12,384]{4,3,2,1,0:T(8,128)(2,1)S(1)} %get-tuple-element.33), channel_id=1, source_target_pairs={{0,2},{4,6},{2,0},{6,4},{1,3},{5,7},{3,1},{7,5},{8,10},{12,14},{10... | collective-permute-start | bytes 110600 | tf_op jit(solution)/shard_map/ppermute | solution.py:52
  2.5 7.1 %collective-permute-start.2 = (bf16[2,2,1,12,384]{4,3,2,1,0:T(8,128)(2,1)S(1)}, bf16[2,2,1,12,384]{4,3,2,1,0:T(8,128)(2,1)S(1)}, u32[]{:S(2)}, u32[]{:S(2)}) collective-permute-start(bf16[2,2,1,12,384]{4,3,2,1,0:T(8,128)(2,1)S(1)} %get-tuple-element.32), channel_id=1, source_target_pairs={{2,4},{4,2},{3,5},{5,3},{10,12},{12,10},{11,13},{13,11},{18,20},{2... | collective-permute-start | bytes 110600 | tf_op jit(solution)/shard_map/ppermute | solution.py:52
  8.2 11.7 %copy-start = (bf16[3,3,3,96,384]{4,3,2,1,0:T(8,128)(2,1)S(1)}, bf16[3,3,3,96,384]{4,3,2,1,0:T(8,128)(2,1)}, u32[]{:S(2)}) copy-start(bf16[3,3,3,96,384]{4,3,2,1,0:T(8,128)(2,1)} %refs_4_.3) | copy-start | bytes 5971972
  8.2 11.7 %copy-start.3 = (bf16[3,3,3,96,384]{4,3,2,1,0:T(8,128)(2,1)S(1)}, bf16[3,3,3,96,384]{4,3,2,1,0:T(8,128)(2,1)}, u32[]{:S(2)}) copy-start(bf16[3,3,3,96,384]{4,3,2,1,0:T(8,128)(2,1)} %refs_5_.1) | copy-start | bytes 5971972
  10.1 6.3 %collective-permute-start.3 = (bf16[2,72,512]{2,1,0:T(8,128)(2,1)S(1)}, bf16[2,72,512]{2,1,0:T(8,128)(2,1)S(1)}, u32[]{:S(2)}, u32[]{:S(2)}) collective-permute-start(bf16[2,72,512]{2,1,0:T(8,128)(2,1)S(1)} %get-tuple-element.18), channel_id=1, source_target_pairs={{0,8},{8,0},{16,24},{24,16},{1,9},{9,1},{17,25},{25,17},{2,10},{10... | collective-permute-start | bytes 442376 | tf_op jit(solution)/shard_map/ppermute | solution.py:36
  11.6 8.3 %collective-permute-start.4 = (bf16[2,72,512]{2,1,0:T(8,128)(2,1)S(1)}, bf16[2,72,512]{2,1,0:T(8,128)(2,1)S(1)}, u32[]{:S(2)}, u32[]{:S(2)}) collective-permute-start(bf16[2,72,512]{2,1,0:T(8,128)(2,1)S(1)} %get-tuple-element.19), channel_id=1, source_target_pairs={{0,16},{8,24},{16,0},{24,8},{1,17},{9,25},{17,1},{25,9},{2,18},{10... | collective-permute-start | bytes 442376 | tf_op jit(solution)/shard_map/ppermute | solution.py:36
  13.1 6.7 %collective-permute-start.5 = (bf16[2,72,512]{2,1,0:T(8,128)(2,1)S(1)}, bf16[2,72,512]{2,1,0:T(8,128)(2,1)S(1)}, u32[]{:S(2)}, u32[]{:S(2)}) collective-permute-start(bf16[2,72,512]{2,1,0:T(8,128)(2,1)S(1)} %get-tuple-element.20), channel_id=1, source_target_pairs={{0,24},{8,16},{16,8},{24,0},{1,25},{9,17},{17,9},{25,1},{2,26},{10... | collective-permute-start | bytes 442376 | tf_op jit(solution)/shard_map/ppermute | solution.py:36
  19.9 7.2 %copy-start.4 = (f32[384]{0:T(512)S(1)}, f32[384]{0:T(512)}, u32[]{:S(2)}) copy-start(f32[384]{0:T(512)} %param.12) | copy-start | bytes 4612
  19.9 7.2 %copy-start.5 = (f32[384]{0:T(512)S(1)}, f32[384]{0:T(512)}, u32[]{:S(2)}) copy-start(f32[384]{0:T(512)} %param.13) | copy-start | bytes 4612
  23.5 4.5 %collective-permute-start.6 = (bf16[2,40,512]{2,1,0:T(8,128)(2,1)S(1)}, bf16[2,40,512]{2,1,0:T(8,128)(2,1)S(1)}, u32[]{:S(2)}, u32[]{:S(2)}) collective-permute-start(bf16[2,40,512]{2,1,0:T(8,128)(2,1)S(1)} %get-tuple-element.22), channel_id=1, source_target_pairs={{0,8},{8,0},{16,24},{24,16},{1,9},{9,1},{17,25},{25,17},{2,10},{10... | collective-permute-start | bytes 245768 | tf_op jit(solution)/shard_map/ppermute | solution.py:36
  24.2 4.4 %collective-permute-start.7 = (bf16[2,40,512]{2,1,0:T(8,128)(2,1)S(1)}, bf16[2,40,512]{2,1,0:T(8,128)(2,1)S(1)}, u32[]{:S(2)}, u32[]{:S(2)}) collective-permute-start(bf16[2,40,512]{2,1,0:T(8,128)(2,1)S(1)} %get-tuple-element.23), channel_id=1, source_target_pairs={{0,16},{8,24},{16,0},{24,8},{1,17},{9,25},{17,1},{25,9},{2,18},{10... | collective-permute-start | bytes 245768 | tf_op jit(solution)/shard_map/ppermute | solution.py:36
  25.0 5.3 %collective-permute-start.8 = (bf16[2,40,512]{2,1,0:T(8,128)(2,1)S(1)}, bf16[2,40,512]{2,1,0:T(8,128)(2,1)S(1)}, u32[]{:S(2)}, u32[]{:S(2)}) collective-permute-start(bf16[2,40,512]{2,1,0:T(8,128)(2,1)S(1)} %get-tuple-element.24), channel_id=1, source_target_pairs={{0,24},{8,16},{16,8},{24,0},{1,25},{9,17},{17,9},{25,1},{2,26},{10... | collective-permute-start | bytes 245768 | tf_op jit(solution)/shard_map/ppermute | solution.py:36
  30.4 24.1 %copy-start.1 = (bf16[2,4,10,384]{3,1,2,0:T(4,128)(2,1)S(1)}, bf16[2,4,10,384]{3,1,2,0:T(4,128)(2,1)}, u32[]{:S(2)}) copy-start(bf16[2,4,10,384]{3,1,2,0:T(4,128)(2,1)} %param.8) | copy-start | bytes 184324
  30.4 24.1 %copy-start.2 = (bf16[2,4,10,384]{3,1,2,0:T(4,128)(2,1)S(1)}, bf16[2,4,10,384]{3,1,2,0:T(4,128)(2,1)}, u32[]{:S(2)}) copy-start(bf16[2,4,10,384]{3,1,2,0:T(4,128)(2,1)} %param.7) | copy-start | bytes 184324
  30.8 1.2 %collective-permute-start.9 = (bf16[2,4,1,384]{3,2,1,0:T(2,128)(2,1)S(1)}, bf16[2,4,1,384]{3,2,1,0:T(2,128)(2,1)S(1)}, u32[]{:S(2)}, u32[]{:S(2)}) collective-permute-start(bf16[2,4,1,384]{3,2,1,0:T(2,128)(2,1)S(1)} %broadcast_select_fusion.7), channel_id=1, source_target_pairs={{0,1},{1,0},{2,3},{3,2},{4,5},{5,4},{6,7},{7,6},{8,9},{9,8},{10,11... | collective-permute-start | bytes 18440 | tf_op jit(solution)/shard_map/ppermute | solution.py:52
  32.1 3.9 %collective-permute-start.11 = (bf16[2,1,12,384]{3,2,1,0:T(8,128)(2,1)S(1)}, bf16[2,1,12,384]{3,2,1,0:T(8,128)(2,1)S(1)}, u32[]{:S(2)}, u32[]{:S(2)}) collective-permute-start(bf16[2,1,12,384]{3,2,1,0:T(8,128)(2,1)S(1)} %broadcast_select_fusion.10), channel_id=1, source_target_pairs={{0,2},{4,6},{2,0},{6,4},{1,3},{5,7},{3,1},{7,5},{8,10},{12,14},{10... | collective-permute-start | bytes 55304 | tf_op jit(solution)/shard_map/ppermute | solution.py:52
  32.2 5.7 %collective-permute-start.10 = (bf16[2,1,12,384]{3,2,1,0:T(8,128)(2,1)S(1)}, bf16[2,1,12,384]{3,2,1,0:T(8,128)(2,1)S(1)}, u32[]{:S(2)}, u32[]{:S(2)}) collective-permute-start(bf16[2,1,12,384]{3,2,1,0:T(8,128)(2,1)S(1)} %get-tuple-element.29), channel_id=1, source_target_pairs={{2,4},{4,2},{3,5},{5,3},{10,12},{12,10},{11,13},{13,11},{18,20},{2... | collective-permute-start | bytes 55304 | tf_op jit(solution)/shard_map/ppermute | solution.py:52
  38.1 5.3 %collective-permute-start.12 = (bf16[2,72,384]{2,1,0:T(8,128)(2,1)S(1)}, bf16[2,72,384]{2,1,0:T(8,128)(2,1)S(1)}, u32[]{:S(2)}, u32[]{:S(2)}) collective-permute-start(bf16[2,72,384]{2,1,0:T(8,128)(2,1)S(1)} %copy.16.refs_0_), channel_id=1, source_target_pairs={{0,8},{8,0},{16,24},{24,16},{1,9},{9,1},{17,25},{25,17},{2,10},{10... | collective-permute-start | bytes 331784 | tf_op jit(solution)/shard_map/ppermute | solution.py:36
  39.8 6.9 %collective-permute-start.13 = (bf16[2,72,384]{2,1,0:T(8,128)(2,1)S(1)}, bf16[2,72,384]{2,1,0:T(8,128)(2,1)S(1)}, u32[]{:S(2)}, u32[]{:S(2)}) collective-permute-start(bf16[2,72,384]{2,1,0:T(8,128)(2,1)S(1)} %copy.16.refs_0_), channel_id=1, source_target_pairs={{0,16},{8,24},{16,0},{24,8},{1,17},{9,25},{17,1},{25,9},{2,18},{10... | collective-permute-start | bytes 331784 | tf_op jit(solution)/shard_map/ppermute | solution.py:36
  40.8 5.9 %collective-permute-start.14 = (bf16[2,72,384]{2,1,0:T(8,128)(2,1)S(1)}, bf16[2,72,384]{2,1,0:T(8,128)(2,1)S(1)}, u32[]{:S(2)}, u32[]{:S(2)}) collective-permute-start(bf16[2,72,384]{2,1,0:T(8,128)(2,1)S(1)} %copy.16.refs_0_), channel_id=1, source_target_pairs={{0,24},{8,16},{16,8},{24,0},{1,25},{9,17},{17,9},{25,1},{2,26},{10... | collective-permute-start | bytes 331784 | tf_op jit(solution)/shard_map/ppermute | solution.py:36
  48.5 3.8 %collective-permute-start.15 = (bf16[2,40,128]{2,1,0:T(8,128)(2,1)S(1)}, bf16[2,40,128]{2,1,0:T(8,128)(2,1)S(1)}, u32[]{:S(2)}, u32[]{:S(2)}) collective-permute-start(bf16[2,40,128]{2,1,0:T(8,128)(2,1)S(1)} %get-tuple-element.26), channel_id=1, source_target_pairs={{0,8},{8,0},{16,24},{24,16},{1,9},{9,1},{17,25},{25,17},{2,10},{10... | collective-permute-start | bytes 61448 | tf_op jit(solution)/shard_map/ppermute | solution.py:36
  48.9 3.8 %collective-permute-start.16 = (bf16[2,40,128]{2,1,0:T(8,128)(2,1)S(1)}, bf16[2,40,128]{2,1,0:T(8,128)(2,1)S(1)}, u32[]{:S(2)}, u32[]{:S(2)}) collective-permute-start(bf16[2,40,128]{2,1,0:T(8,128)(2,1)S(1)} %get-tuple-element.27), channel_id=1, source_target_pairs={{0,16},{8,24},{16,0},{24,8},{1,17},{9,25},{17,1},{25,9},{2,18},{10... | collective-permute-start | bytes 61448 | tf_op jit(solution)/shard_map/ppermute | solution.py:36
  49.8 4.7 %collective-permute-start.17 = (bf16[2,40,128]{2,1,0:T(8,128)(2,1)S(1)}, bf16[2,40,128]{2,1,0:T(8,128)(2,1)S(1)}, u32[]{:S(2)}, u32[]{:S(2)}) collective-permute-start(bf16[2,40,128]{2,1,0:T(8,128)(2,1)S(1)} %get-tuple-element.28), channel_id=1, source_target_pairs={{0,24},{8,16},{16,8},{24,0},{1,25},{9,17},{17,9},{25,1},{2,26},{10... | collective-permute-start | bytes 61448 | tf_op jit(solution)/shard_map/ppermute | solution.py:36

commit v4 on v3

v4 whole, which is shorter than its diff:
```python
import functools
import math

import jax
import jax.numpy as jnp
from jax import lax
from jax.experimental import pallas as pl
from jax.experimental.pallas import tpu as pltpu
from jax.sharding import PartitionSpec as P

epsilon = 1e-06
f32 = jnp.float32
bf16 = jnp.bfloat16
lanes = 128


def is_power(count):
    return count & (count - 1) == 0


def sent_to(index, step, count):
    return index ^ step if is_power(count) else lax.rem(index + step, count)


def got_from(index, step, count):
    return index ^ step if is_power(count) else lax.rem(index + count - step, count)


def tm_exchange(blocks):
    count = len(blocks)
    got = [blocks[0]]
    for step in range(1, count):
        pairs = [
            (i, i ^ step if is_power(count) else (i + step) % count) for i in range(count)
        ]
        got.append(lax.ppermute(blocks[step], "tm", pairs))
    return got


def is_even(axis):
    return lax.rem(lax.axis_index(axis), 2) == 0


def halo_swaps(low_edge, high_edge, axis):
    count = lax.axis_size(axis)
    even = is_even(axis)
    got = []
    for start, value in ((0, (high_edge, low_edge)), (1, (low_edge, high_edge))):
        pairs = [(i, i + 1) for i in range(start, count - 1, 2)]
        if pairs:
            pairs = pairs + [(b, a) for a, b in pairs]
            got.append(lax.ppermute(jnp.where(even, *value), axis, pairs))
        else:
            got.append(None)
    return got


def low_and_high(axis, first, second):
    even = is_even(axis)
    if first is None:
        return None, None
    nothing = jnp.zeros_like(first)
    second = nothing if second is None else second
    return jnp.where(even, second, first), jnp.where(even, first, second)


def halo_edges(blocks, rows):
    count = blocks[0].shape[1]
    left = jnp.stack([block[:, :rows] for block in blocks])
    right = jnp.stack([block[:, count - rows :] for block in blocks])
    sides = halo_swaps(left, right, "col")
    low_side, high_side = low_and_high("col", *sides)
    if low_side is None:
        low_side = high_side = jnp.zeros_like(left)

    def strip(row):
        own = jnp.stack([block[:, row::rows] for block in blocks])
        return jnp.concatenate(
            [low_side[:, :, row : row + 1], own, high_side[:, :, row : row + 1]], axis=2
        )

    ends = halo_swaps(strip(0), strip(rows - 1), "row")
    return [[got for got in part if got is not None] for part in (sides, ends)]


def rms_parts(values, gain):
    inv_rms = lax.rsqrt(jnp.mean(values * values, axis=-1, keepdims=True) + epsilon)
    normed = values * inv_rms
    return inv_rms, normed, normed * gain


def silu_slope(values):
    sigmoid_val = jax.nn.sigmoid(values)
    return sigmoid_val * (1.0 + values * (1.0 - sigmoid_val))


def rms_back(cotangent, inv_rms, normed, gain):
    scaled_grad = cotangent * gain
    return inv_rms * (scaled_grad - normed * jnp.mean(normed * scaled_grad, axis=-1, keepdims=True))


def slot_matrix(slot, width, channels, wide):
    row = lax.broadcasted_iota(jnp.int32, (channels, wide), 0)
    col = lax.broadcasted_iota(jnp.int32, (channels, wide), 1)
    hit = (row == col + slot * width) & (col < width)
    return jnp.where(hit, 1.0, 0.0).astype(bf16)


def spread_matrix(slot, width, channels, wide):
    row = lax.broadcasted_iota(jnp.int32, (wide, channels), 0)
    col = lax.broadcasted_iota(jnp.int32, (wide, channels), 1)
    hit = (col == row + slot * width) & (row < width)
    return jnp.where(hit, 1.0, 0.0).astype(bf16)


def pack_kernel(peers, width, both_ref, gain_ref, *refs):
    out_refs, flat_ref = refs[:-1], refs[-1]
    me = lax.axis_index("tm")
    feat_ref, reward_ref = both_ref.at[0], both_ref.at[1]
    frames, channels = feat_ref.shape[0], feat_ref.shape[3]
    wide = out_refs[0].shape[2] - channels
    for frame in range(frames):
        act = rms_parts(join_cells(flat_ref.at[frame, 0], feat_ref, frame), gain_ref[...])[2]
        silu = (act * jax.nn.sigmoid(act)).astype(bf16)
        reward = join_cells(flat_ref.at[frame, 1], reward_ref, frame).astype(bf16)
        for step in range(peers):
            slot = sent_to(me, step, peers)
            piece = jnp.dot(
                silu, slot_matrix(slot, width, channels, wide), preferred_element_type=f32
            )
            out_refs[step][frame, :, :channels] = reward
            out_refs[step][frame, :, channels:] = piece.astype(bf16)


class Cells:
    def __init__(self, rows, cols):
        self.rows, self.cols = rows, cols
        self.left = rows * cols
        self.right = self.left + rows
        self.low = self.right + rows
        self.high = self.low + cols + 2

    def at(self, row, col):
        if row == 0:
            return self.low + col
        if row == self.rows + 1:
            return self.high + col
        if col == 0:
            return self.left + row - 1
        if col == self.cols + 1:
            return self.right + row - 1
        return (col - 1) * self.rows + row - 1


def lay_frames(peers, frames, cells, block_refs, side_refs, end_refs, cells_ref):
    me = lax.axis_index("tm")
    total = peers * frames
    tiles = cells_ref.shape[0]

    def lay(start, frame, values):
        for tile in range(tiles):
            piece = values[:, tile * lanes : (tile + 1) * lanes]
            place = pl.ds(start * total + frame, piece.shape[0], stride=total)
            cells_ref[tile, place, :] = piece.astype(f32)

    for step in range(peers):
        source = got_from(me, step, peers)
        for frame in range(frames):
            at = source * frames + frame
            lay(0, at, block_refs[step][frame])
            for axis, got_refs, low, high, count in (
                ("col", side_refs, cells.left, cells.right, cells.rows),
                ("row", end_refs, cells.low, cells.high, cells.cols + 2),
            ):
                got = [ref[step, frame].astype(f32) for ref in got_refs] + [None, None]
                values = low_and_high(axis, got[0], got[1])
                for start, value in zip((low, high), values):
                    if value is None:
                        value = jnp.zeros((count, tiles * lanes), f32)
                    lay(start, at, value)


def plane_row(cells, cells_ref, tile, row, first, count, total):
    return jnp.concatenate(
        [
            cells_ref[tile, pl.ds(cells.at(row, first + col) * total, total), :]
            for col in range(count)
        ],
        axis=0,
    )


def shifted(values, ahead):
    total = values.shape[1]
    if ahead == 0:
        return values
    frame = lax.broadcasted_iota(jnp.int32, values.shape, 1)
    moved = pltpu.roll(values, (-ahead) % total, 1)
    keep = frame < total - ahead if ahead > 0 else frame >= -ahead
    return jnp.where(keep, moved, 0.0)


def chunk_rows(rows, total):
    return max(r for r in range(1, rows + 1) if rows % r == 0 and (r == 1 or r * total <= 32))


def stacked_weights(kernel_ref, wide, order):
    width, channels = kernel_ref.shape[3:]
    pad = jnp.zeros((wide - width, channels), bf16)

    def block(a, b, c):
        value = kernel_ref[a, b, c]
        return jnp.concatenate([value, pad], axis=0) if wide > width else value

    return jnp.concatenate(
        [jnp.concatenate([block(*tap) for tap in column], axis=0) for column in order], axis=1
    )


def conv_ahead(cells, cells_ref, first, kernel_ref, plane_ref, parts_ref, sum_ref, total):
    rows, cols, channels = cells.rows, cells.cols, plane_ref.shape[2]
    wide = sum_ref.shape[0] * lanes
    wide_tiles = wide // lanes
    for row in range(rows + 2):
        for tile in range(channels // lanes):
            plane_ref[row, :, tile * lanes : (tile + 1) * lanes] = plane_row(
                cells, cells_ref, first + tile, row, 0, cols + 2, total
            ).astype(bf16)

    weights = stacked_weights(
        kernel_ref,
        wide,
        [[(2 - s, 2 - b, 2 - c) for s in range(3) for c in range(3)] for b in range(3)],
    )
    step = chunk_rows(rows, total)

    def chunk(start):
        left = jnp.concatenate(
            [plane_ref[pl.ds(start + b, step)].reshape(-1, channels) for b in range(3)], axis=1
        )
        parts = lax.dot_general(left, weights, (((1,), (1,)), ((), ())), preferred_element_type=f32)
        for tile in range(parts_ref.shape[0]):
            parts_ref[tile] = parts[:, tile * lanes : (tile + 1) * lanes]
        for row in range(step):
            for tile in range(wide_tiles):
                summed = None
                for s in range(3):
                    part = None
                    for c in range(3):
                        at = (row * (cols + 2) + c) * total
                        piece = parts_ref[(s * 3 + c) * wide_tiles + tile, at : at + cols * total, :]
                        part = piece if part is None else part + piece
                    part = shifted(part.reshape(cols, total, lanes), s)
                    summed = part if summed is None else summed + part
                for col in range(cols):
                    place = pl.ds((col * rows + start + row) * total, total)
                    sum_ref[tile, place, :] = summed[col]

    run_chunks(rows, step, chunk)


def run_chunks(rows, step, chunk):
    if step == rows:
        chunk(0)
    else:
        pl.loop(0, rows, step=step)(chunk)


def conv_behind(cells, cells_ref, first, kernel_ref, taps_ref, sum_ref, total):
    rows, cols = cells.rows, cells.cols
    channels = sum_ref.shape[0] * lanes
    wide_tiles = taps_ref.shape[2] // (3 * lanes)
    for row in range(rows + 2):
        for tile in range(wide_tiles):
            for c in range(3):
                at = (c * wide_tiles + tile) * lanes
                taps_ref[row, :, at : at + lanes] = plane_row(
                    cells, cells_ref, first + tile, row, c, cols, total
                ).astype(bf16)

    weights = stacked_weights(
        kernel_ref,
        wide_tiles * lanes,
        [[(a, b, c) for b in range(3) for c in range(3)] for a in range(3)],
    )
    step = chunk_rows(rows, total)

    def chunk(start):
        left = jnp.concatenate(
            [
                taps_ref[pl.ds(start + b, step)].reshape(-1, taps_ref.shape[2])
                for b in range(3)
            ],
            axis=1,
        )
        parts = jnp.dot(left, weights, preferred_element_type=f32)
        for tile in range(channels // lanes):
            summed = None
            for a in range(3):
                at = a * channels + tile * lanes
                part = parts[:, at : at + lanes].reshape(step * cols, total, lanes)
                part = shifted(part, a - 2)
                summed = part if summed is None else summed + part
            for row in range(step):
                for col in range(cols):
                    place = pl.ds((col * rows + start + row) * total, total)
                    sum_ref[tile, place, :] = summed[row * cols + col]

    run_chunks(rows, step, chunk)


def hand_out(peers, frames, total, sum_ref, out_refs, start):
    me = lax.axis_index("tm")
    for step in range(peers):
        target = sent_to(me, step, peers)
        for frame in range(frames):
            place = pl.ds(target * frames + frame, out_refs[step].shape[1], stride=total)
            for tile in range(sum_ref.shape[0]):
                at = start + tile * lanes
                out_refs[step][frame, :, at : at + lanes] = sum_ref[tile, place, :].astype(bf16)


def inner_kernel(peers, frames, cells, sides, behind, *refs):
    blocks, side_refs, refs = refs[:peers], refs[peers : peers + sides], refs[peers + sides :]
    total = peers * frames
    if behind:
        kernel_one, kernel_two, sum_one, sum_two, cells_ref, plane, parts, taps = refs
    else:
        kernel_two, sum_two, cells_ref, plane, parts = refs
    lay_frames(peers, frames, cells, blocks, side_refs, [], cells_ref)
    if behind:
        tiles = plane.shape[2] // lanes
        conv_behind(cells, cells_ref, tiles, kernel_one, taps, sum_one, total)
    conv_ahead(cells, cells_ref, 0, kernel_two, plane, parts, sum_two, total)


def outer_kernel(peers, frames, cells, ends, behind, *refs):
    end_refs, refs = refs[:ends], refs[ends:]
    count = 2 if behind else 1
    kernels, sums, outs = refs[:count], refs[count : 2 * count], refs[2 * count : 2 * count + peers]
    cells_ref, *kept = refs[2 * count + peers :]
    total = peers * frames
    me = lax.axis_index("tm")
    span = cells.cols + 2
    for step in range(peers):
        source = got_from(me, step, peers)
        for frame in range(frames):
            got = [ref[step, frame].astype(f32) for ref in end_refs] + [None, None]
            values = low_and_high("row", got[0], got[1])
            for place, value in enumerate(values):
                for tile in range(cells_ref.shape[0]):
                    at = place * span * total + source * frames + frame
                    cells_ref[tile, pl.ds(at, span, stride=total), :] = value[
                        :, tile * lanes : (tile + 1) * lanes
                    ]
    for kernel_ref, sum_ref, out_ref in zip(kernels, sums, kept):
        for tile in range(sum_ref.shape[0]):
            out_ref[tile] = sum_ref[tile]
    for place, row in ((0, 0), (1, cells.rows - 1)):
        if behind:
            outer_behind(cells, cells_ref, place, row, kernels[0], kept[0], total)
        outer_ahead(cells, cells_ref, place, row, kernels[-1], kept[-1], total)
    start = 0
    for sum_ref in kept:
        hand_out(peers, frames, total, sum_ref, outs, start)
        start += sum_ref.shape[0] * lanes


def add_row(cells, sum_ref, tile, row, values, total):
    for col in range(cells.cols):
        place = pl.ds((col * cells.rows + row) * total, total)
        sum_ref[tile, place, :] = sum_ref[tile, place, :] + values[col]


def end_row(cells, cells_ref, place, first, count, start, cols, total):
    base = (place * (cells.cols + 2) + start) * total
    return jnp.concatenate(
        [cells_ref[first + tile, base : base + cols * total, :] for tile in range(count)], axis=1
    ).astype(bf16)


def outer_behind(cells, cells_ref, place, row, kernel_ref, sum_ref, total):
    cols, channels = cells.cols, sum_ref.shape[0] * lanes
    tiles = channels // lanes
    wide_tiles = cells_ref.shape[0] - tiles
    b = 2 * place
    weights = stacked_weights(
        kernel_ref, wide_tiles * lanes, [[(a, b, c) for c in range(3)] for a in range(3)]
    )
    left = jnp.concatenate(
        [end_row(cells, cells_ref, place, tiles, wide_tiles, c, cols, total) for c in range(3)],
        axis=1,
    )
    parts = jnp.dot(left, weights, preferred_element_type=f32)
    for tile in range(tiles):
        summed = None
        for a in range(3):
            at = a * channels + tile * lanes
            part = shifted(parts[:, at : at + lanes].reshape(cols, total, lanes), a - 2)
            summed = part if summed is None else summed + part
        add_row(cells, sum_ref, tile, row, summed, total)


def outer_ahead(cells, cells_ref, place, row, kernel_ref, sum_ref, total):
    cols, channels = cells.cols, kernel_ref.shape[4]
    wide = sum_ref.shape[0] * lanes
    b = 2 * place
    weights = stacked_weights(
        kernel_ref, wide, [[(2 - s, 2 - b, 2 - c) for s in range(3) for c in range(3)]]
    )
    left = end_row(cells, cells_ref, place, 0, channels // lanes, 0, cols + 2, total)
    parts = lax.dot_general(left, weights, (((1,), (1,)), ((), ())), preferred_element_type=f32)
    for tile in range(wide // lanes):
        summed = None
        for s in range(3):
            part = None
            for c in range(3):
                at = (s * 3 + c) * wide + tile * lanes
                piece = parts[c * total : (c + cols) * total, at : at + lanes]
                part = piece if part is None else part + piece
            part = shifted(part.reshape(cols, total, lanes), s)
            summed = part if summed is None else summed + part
        add_row(cells, sum_ref, tile, row, summed, total)


def gathered(peers, frame, block_refs, start, width, channels):
    me = lax.axis_index("tm")
    wide = block_refs[0].shape[2] - start
    summed = None
    for step in range(peers):
        spread = spread_matrix(got_from(me, step, peers), width, channels, wide)
        part = jnp.dot(
            block_refs[step][frame, :, start:], spread, preferred_element_type=f32
        )
        summed = part if summed is None else summed + part
    return summed


def join_cells(flat_ref, in_ref, frame):
    rows = in_ref.shape[2]
    for col in range(in_ref.shape[1]):
        flat_ref[col * rows : (col + 1) * rows, :] = in_ref[frame, col].astype(f32)
    return flat_ref[...]


def split_cells(flat_ref, values, out_ref, frame):
    flat_ref[...] = values
    rows = out_ref.shape[2]
    for col in range(out_ref.shape[1]):
        out_ref[frame, col] = flat_ref[col * rows : (col + 1) * rows, :].astype(bf16)


def middle_kernel(peers, width, *refs):
    blocks = refs[:peers]
    gain_ref, bias_ref, out_ref = refs[peers:]
    frames, _, channels = out_ref.shape
    for frame in range(frames):
        hidden = blocks[0][frame, :, :channels].astype(f32)
        for step in range(1, peers):
            hidden = hidden + blocks[step][frame, :, :channels].astype(f32)
        hidden = hidden + bias_ref[...]
        back = gathered(peers, frame, blocks, channels, width, channels)
        inv, normed, act = rms_parts(hidden, gain_ref[...])
        out_ref[frame] = rms_back(back * silu_slope(act), inv, normed, gain_ref[...]).astype(bf16)


def final_kernel(peers, width, *refs):
    blocks = refs[:peers]
    feat_ref, reward_ref, gain_ref, out_ref, flat_ref = refs[peers:]
    frames, channels = out_ref.shape[0], out_ref.shape[3]
    for frame in range(frames):
        back = gathered(peers, frame, blocks, 0, width, channels)
        values = join_cells(flat_ref.at[frame, 0], feat_ref, frame)
        reward = join_cells(flat_ref.at[frame, 1], reward_ref, frame)
        inv, normed, act = rms_parts(values, gain_ref[...])
        result = rms_back(back * silu_slope(act), inv, normed, gain_ref[...])
        split_cells(flat_ref.at[frame, 2], result + reward, out_ref, frame)


def size_of(structs):
    return sum(math.prod(s.shape) * s.dtype.itemsize for s in structs)


def call(kernel, outs, scratch=(), flops=0, spare=2, covered=0, name=None):
    def run(*operands):
        held = size_of(outs) + size_of(operands)
        grant = 2 * held + size_of(scratch) + spare * 2**20
        return pl.pallas_call(
            kernel,
            out_shape=outs,
            scratch_shapes=list(scratch),
            cost_estimate=pl.CostEstimate(
                flops=flops + covered, bytes_accessed=held, transcendentals=0
            ),
            compiler_params=pltpu.CompilerParams(vmem_limit_bytes=min(grant, 60 * 2**20)),
            name=name,
        )(*operands)

    return run


def on_device(
    features, reward_grad, first_kernel, second_kernel, first_gain, second_gain, first_bias
):
    peers = lax.axis_size("tm")
    frames, rows, cols, channels = features.shape
    width = first_kernel.shape[3]
    wide = -(-width // lanes) * lanes
    total = peers * frames
    plane = (rows + 2) * (cols + 2)
    count = rows * cols
    struct = jax.ShapeDtypeStruct

    cells = Cells(rows, cols)
    by_col = (0, 2, 1, 3)
    held = features.transpose(by_col), reward_grad.transpose(by_col)
    ahead_scratch = [
        pltpu.VMEM((rows + 2, (cols + 2) * total, channels), bf16),
        pltpu.VMEM((9 * wide // lanes, chunk_rows(rows, total) * (cols + 2) * total, lanes), f32),
    ]
    flops = 2 * 27 * width * channels * total * count
    sum_shapes = [
        (channels // lanes, count * total, lanes),
        (wide // lanes, count * total, lanes),
    ]

    def convolved(blocks, kernels):
        behind = len(kernels) == 2
        shapes = sum_shapes[-len(kernels) :]
        tiles = blocks[0].shape[2] // lanes
        sides, ends = halo_edges(blocks, rows)
        taps = [pltpu.VMEM((rows + 2, cols * total, 3 * wide), bf16)] if behind else []
        sums = call(
            functools.partial(inner_kernel, peers, frames, cells, len(sides), behind),
            [struct(shape, f32) for shape in shapes],
            [pltpu.VMEM((tiles, plane * total, lanes), f32), *ahead_scratch, *taps],
            flops * len(kernels),
            spare=8,
            name="inner",
        )(*blocks, *sides, *kernels)
        return call(
            functools.partial(outer_kernel, peers, frames, cells, len(ends), behind),
            [struct((frames, count, sum(s[0] for s in shapes) * lanes), bf16)] * peers,
            [
                pltpu.VMEM((tiles, 2 * (cols + 2) * total, lanes), f32),
                *[pltpu.VMEM(shape, f32) for shape in shapes],
            ],
            flops * len(kernels) // 6,
            spare=8,
            name="outer",
        )(*ends, *kernels, *sums)

    packed = call(
        functools.partial(pack_kernel, peers, width),
        [struct((frames, count, channels + wide), bf16)] * peers,
        [pltpu.VMEM((frames, 2, count, channels), f32)],
        covered=4 * 10**9,
        name="pack",
    )(jnp.stack(held), first_gain)
    sums = convolved(tm_exchange(packed), [first_kernel, second_kernel])
    got = tm_exchange(sums)
    hidden_grad = call(
        functools.partial(middle_kernel, peers, width),
        [struct((frames, count, channels), bf16)],
        name="middle",
    )(*got, second_gain, first_bias)[0]
    backs = convolved(tm_exchange([hidden_grad] * peers), [first_kernel])
    got = tm_exchange(backs)
    result = call(
        functools.partial(final_kernel, peers, width),
        [struct(held[0].shape, bf16)],
        [pltpu.VMEM((frames, 3, count, channels), f32)],
        name="final",
    )(*got, *held, first_gain)[0]
    return result.transpose(by_col)


def solution(mesh):
    in_specs = (
        P("tm", "row", "col", None),
        P("tm", "row", "col", None),
        P(None, None, None, "tm", None),
        P(None, None, None, "tm", None),
        P(),
        P(),
        P(),
    )
    out_specs = P("tm", "row", "col", None)
    return jax.shard_map(
        on_device, mesh=mesh, in_specs=in_specs, out_specs=out_specs, check_vma=False
    )
```

time: 56.2 us -> 54.8 us (0.975)
  waiting for transfers between devices: 22.7 us -> 18.7 us
  local copies, waits for them, and re-layouts: 1.7 us -> 3.08 us
  other arithmetic: 0.41 us -> 1.66 us
  Pallas kernels: 7.28 us -> 8.39 us
  starting transfers between devices: 23.2 us -> 22.4 us
    ppermute x12, waiting for transfers between devices: 16.9 us -> 14.6 us  [tm_exchange(): got.append(lax.ppermute(blocks[step], 'tm', pairs))]
    unnamed x12 -> x18, local copies, waits for them, and re-layouts: 0.03 us -> 2.27 us
    ppermute x6, waiting for transfers between devices: 5.77 us -> 4.08 us  [halo_swaps(): got.append(lax.ppermute(jnp.where(even, *value), axis, pairs))]
    pallas_call x5 -> x7, Pallas kernels: 7.28 us -> 8.39 us  [run(): pl.pallas_call(kernel, out_shape=outs, scratch_shapes=list(scratch), cost...]
    another operation x0 -> x1, other arithmetic: none -> 0.95 us  [on_device(): jnp.stack(held)]
    ppermute x6, starting transfers between devices: 8.97 us -> 8.07 us  [halo_swaps(): got.append(lax.ppermute(jnp.where(even, *value), axis, pairs))]
    another operation x1 -> x8, local copies, waits for them, and re-layouts: 0.88 us -> 0.08 us  [halo_edges(): left = jnp.stack([block[:, :rows] for block in blocks])]
    slice x0 -> x19, local copies, waits for them, and re-layouts: none -> 0.73 us  [the longest x16 0.64 us: strip(): own = jnp.stack([block[:, row::rows] for block in blocks])]
  transfers between devices with their start and end apart: 18 -> 18, of which waited for: 15 -> 16; matrix products, arithmetic and copies ran while one was open for 1% -> 1% of each run, Pallas kernels for 0% -> 8%
where the time goes in v4:
time: 54.8 us; the launch traced here: 54.5 us
  starting transfers between devices  22.4 us (41%)
  waiting for transfers between devices  18.7 us (34%)
  Pallas kernels  8.39 us (15%)
  local copies, waits for them, and re-layouts  3.08 us (6%)
  other arithmetic  1.66 us (3%)
    ppermute x12, waiting for transfers between devices, tm_exchange(): got.append(lax.ppermute(blocks[step], 'tm', pairs))  14.6 us
    ppermute x12, starting transfers between devices, tm_exchange(): got.append(lax.ppermute(blocks[step], 'tm', pairs))  14.3 us
    pallas_call x7, Pallas kernels, run(): pl.pallas_call(kernel, out_shape=outs, scratch_shapes=list(scratch), cost...  8.39 us
    ppermute x6, starting transfers between devices, halo_swaps(): got.append(lax.ppermute(jnp.where(even, *value), axis, pairs))  8.07 us
    ppermute x6, waiting for transfers between devices, halo_swaps(): got.append(lax.ppermute(jnp.where(even, *value), axis, pairs))  4.08 us
    unnamed x18, local copies, waits for them, and re-layouts  2.27 us
  transfers between devices with their start and end apart: 18, of which 16 were waited for; matrix products, arithmetic and copies ran while one was open for 1% of the time, Pallas kernels for 8%

profile of v4, /device:TPU:8, one launch (start us, length us, event | category | flops | bytes accessed | tf_op | source)
XLA Modules:
  0.0 54.5 jit_solution(8918497581997978684)
XLA Ops:
  0.0 0.9 %pad_maximum_fusion.2.both_ref = bf16[2,2,10,4,384]{4,3,2,1,0:T(4,128)(2,1)S(1)} fusion(bf16[1,2,10,4,384]{4,3,2,1,0:T(4,128)(2,1)} %bitcast.55, bf16[1,2,10,4,384]{4,3,2,1,0:T(4,128)(2,1)} %bitcast.57), kind=kLoop, calls=%fused_computation.4 | loop fusion | flops 61440 | bytes 245760 | tf_op jit(solution)/shard_map/stack | solution.py:559
  1.0 0.7 %copy-done.7 = f32[384]{0:T(512)S(1)} copy-done((f32[384]{0:T(512)S(1)}, f32[384]{0:T(512)}, u32[]{:S(2)}) %copy-start.7) | copy-done | bytes 1560
  1.6 0.5 pack.1
  2.1 1.6 %collective-permute-start = (bf16[2,40,512]{2,1,0:T(8,128)(2,1)S(1)}, bf16[2,40,512]{2,1,0:T(8,128)(2,1)S(1)}, u32[]{:S(2)}, u32[]{:S(2)}) collective-permute-start(bf16[2,40,512]{2,1,0:T(8,128)(2,1)S(1)} %get-tuple-element.20), channel_id=1, source_target_pairs={{0,8},{8,0},{16,24},{24,16},{1,9},{9,1},{17,25},{25,17},{2,10},{10... | collective-permute-start | bytes 245768 | tf_op jit(solution)/shard_map/ppermute | solution.py:36
  3.7 1.5 %collective-permute-start.1 = (bf16[2,40,512]{2,1,0:T(8,128)(2,1)S(1)}, bf16[2,40,512]{2,1,0:T(8,128)(2,1)S(1)}, u32[]{:S(2)}, u32[]{:S(2)}) collective-permute-start(bf16[2,40,512]{2,1,0:T(8,128)(2,1)S(1)} %get-tuple-element.21), channel_id=1, source_target_pairs={{0,16},{8,24},{16,0},{24,8},{1,17},{9,25},{17,1},{25,9},{2,18},{10... | collective-permute-start | bytes 245768 | tf_op jit(solution)/shard_map/ppermute | solution.py:36
  5.2 0.5 collective-permute-start.2
  5.7 0.9 %collective-permute-done.refs_1_ = bf16[2,40,512]{2,1,0:T(8,128)(2,1)S(1)} collective-permute-done((bf16[2,40,512]{2,1,0:T(8,128)(2,1)S(1)}, bf16[2,40,512]{2,1,0:T(8,128)(2,1)S(1)}, u32[]{:S(2)}, u32[]{:S(2)}) %collective-permute-start) | collective-permute-done | bytes 81952 | tf_op jit(solution)/shard_map/ppermute | solution.py:36
  6.6 2.4 %collective-permute-done.1.refs_2_ = bf16[2,40,512]{2,1,0:T(8,128)(2,1)S(1)} collective-permute-done((bf16[2,40,512]{2,1,0:T(8,128)(2,1)S(1)}, bf16[2,40,512]{2,1,0:T(8,128)(2,1)S(1)}, u32[]{:S(2)}, u32[]{:S(2)}) %collective-permute-start.1) | collective-permute-done | bytes 81952 | tf_op jit(solution)/shard_map/ppermute | solution.py:36
  9.0 1.5 %collective-permute-done.2.refs_3_ = bf16[2,40,512]{2,1,0:T(8,128)(2,1)S(1)} collective-permute-done((bf16[2,40,512]{2,1,0:T(8,128)(2,1)S(1)}, bf16[2,40,512]{2,1,0:T(8,128)(2,1)S(1)}, u32[]{:S(2)}, u32[]{:S(2)}) %collective-permute-start.2) | collective-permute-done | bytes 81952 | tf_op jit(solution)/shard_map/ppermute | solution.py:36
  10.6 0.1 collective-permute-start.3
  11.0 0.9 %collective-permute-done.3.refs_4_ = bf16[4,2,4,512]{3,2,1,0:T(4,128)(2,1)S(1)} collective-permute-done((bf16[4,2,4,512]{3,2,1,0:T(4,128)(2,1)S(1)}, bf16[4,2,4,512]{3,2,1,0:T(4,128)(2,1)S(1)}, u32[]{:S(2)}, u32[]{:S(2)}) %collective-permute-start.3) | collective-permute-done | bytes 32800 | tf_op jit(solution)/shard_map/ppermute | solution.py:52
  12.0 0.2 broadcast_select_fusion
  12.1 0.2 broadcast_select_fusion.1
  12.3 0.5 collective-permute-start.4
  12.8 4.6 %collective-permute-start.5 = (bf16[4,2,12,512]{3,2,1,0:T(8,128)(2,1)S(1)}, bf16[4,2,12,512]{3,2,1,0:T(8,128)(2,1)S(1)}, u32[]{:S(2)}, u32[]{:S(2)}) collective-permute-start(bf16[4,2,12,512]{3,2,1,0:T(8,128)(2,1)S(1)} %broadcast_select_fusion), channel_id=1, source_target_pairs={{2,4},{4,2},{3,5},{5,3},{10,12},{12,10},{11,13},{13,11},{18,20},{2... | collective-permute-start | bytes 294920 | tf_op jit(solution)/shard_map/ppermute | solution.py:52
  17.4 1.5 %copy-done.1 = bf16[3,3,3,96,384]{4,3,2,1,0:T(8,128)(2,1)S(1)} copy-done((bf16[3,3,3,96,384]{4,3,2,1,0:T(8,128)(2,1)S(1)}, bf16[3,3,3,96,384]{4,3,2,1,0:T(8,128)(2,1)}, u32[]{:S(2)}) %copy-start.1) | copy-done | bytes 1990680
  19.0 2.8 %inner.2 = (f32[3,320,128]{2,1,0:T(8,128)S(1)}, f32[1,320,128]{2,1,0:T(8,128)S(1)}) custom-call(bf16[2,40,512]{2,1,0:T(8,128)(2,1)S(1)} %get-tuple-element.19.refs_0_, bf16[2,40,512]{2,1,0:T(8,128)(2,1)S(1)} %collective-permute-done.refs_1_, bf16[2,40,512]{2,1,0:T(8,128)(2,1)S(1)} %collective-permute-done.1.refs_2_, ...), custom_call_target="tpu_custom_call" | custom-call | flops 1274019840 | bytes 4997120 | tf_op jit(solution)/shard_map/inner/pallas_call | solution.py:488
  21.8 1.3 %outer.2 = (bf16[2,40,512]{2,1,0:T(8,128)(2,1)S(1)}, bf16[2,40,512]{2,1,0:T(8,128)(2,1)S(1)}, bf16[2,40,512]{2,1,0:T(8,128)(2,1)S(1)}, bf16[2,40,512]{2,1,0:T(8,128)(2,1)S(1)}) custom-call(bf16[4,2,12,512]{3,2,1,0:T(8,128)(2,1)S(1)} %collective-permute-done.4.refs_0_, bf16[4,2,12,512]{3,2,1,0:T(8,128)(2,1)S(1)} %collective-permute-done.5.refs_1_, ...), custom_call_target="tpu_custom_call" | custom-call | flops 212336640 | bytes 5160960 | tf_op jit(solution)/shard_map/outer/pallas_call | solution.py:488
  23.1 0.6 %collective-permute-start.6 = (bf16[2,40,512]{2,1,0:T(8,128)(2,1)S(1)}, bf16[2,40,512]{2,1,0:T(8,128)(2,1)S(1)}, u32[]{:S(2)}, u32[]{:S(2)}) collective-permute-start(bf16[2,40,512]{2,1,0:T(8,128)(2,1)S(1)} %get-tuple-element.26), channel_id=1, source_target_pairs={{0,8},{8,0},{16,24},{24,16},{1,9},{9,1},{17,25},{25,17},{2,10},{10... | collective-permute-start | bytes 245768 | tf_op jit(solution)/shard_map/ppermute | solution.py:36
  23.7 0.7 %collective-permute-start.7 = (bf16[2,40,512]{2,1,0:T(8,128)(2,1)S(1)}, bf16[2,40,512]{2,1,0:T(8,128)(2,1)S(1)}, u32[]{:S(2)}, u32[]{:S(2)}) collective-permute-start(bf16[2,40,512]{2,1,0:T(8,128)(2,1)S(1)} %get-tuple-element.27), channel_id=1, source_target_pairs={{0,16},{8,24},{16,0},{24,8},{1,17},{9,25},{17,1},{25,9},{2,18},{10... | collective-permute-start | bytes 245768 | tf_op jit(solution)/shard_map/ppermute | solution.py:36
  24.5 2.2 %collective-permute-start.8 = (bf16[2,40,512]{2,1,0:T(8,128)(2,1)S(1)}, bf16[2,40,512]{2,1,0:T(8,128)(2,1)S(1)}, u32[]{:S(2)}, u32[]{:S(2)}) collective-permute-start(bf16[2,40,512]{2,1,0:T(8,128)(2,1)S(1)} %get-tuple-element.28), channel_id=1, source_target_pairs={{0,24},{8,16},{16,8},{24,0},{1,25},{9,17},{17,9},{25,1},{2,26},{10... | collective-permute-start | bytes 245768 | tf_op jit(solution)/shard_map/ppermute | solution.py:36
  26.7 1.8 %collective-permute-done.6.refs_1_ = bf16[2,40,512]{2,1,0:T(8,128)(2,1)S(1)} collective-permute-done((bf16[2,40,512]{2,1,0:T(8,128)(2,1)S(1)}, bf16[2,40,512]{2,1,0:T(8,128)(2,1)S(1)}, u32[]{:S(2)}, u32[]{:S(2)}) %collective-permute-start.6) | collective-permute-done | bytes 81952 | tf_op jit(solution)/shard_map/ppermute | solution.py:36
  28.4 0.5 collective-permute-done.7.refs_2_
  28.9 0.9 %collective-permute-done.8.refs_3_ = bf16[2,40,512]{2,1,0:T(8,128)(2,1)S(1)} collective-permute-done((bf16[2,40,512]{2,1,0:T(8,128)(2,1)S(1)}, bf16[2,40,512]{2,1,0:T(8,128)(2,1)S(1)}, u32[]{:S(2)}, u32[]{:S(2)}) %collective-permute-start.8) | collective-permute-done | bytes 81952 | tf_op jit(solution)/shard_map/ppermute | solution.py:36
  29.8 0.4 middle.1.refs_0_
  30.2 2.3 %collective-permute-start.11 = (bf16[2,40,384]{2,1,0:T(8,128)(2,1)S(1)}, bf16[2,40,384]{2,1,0:T(8,128)(2,1)S(1)}, u32[]{:S(2)}, u32[]{:S(2)}) collective-permute-start(bf16[2,40,384]{2,1,0:T(8,128)(2,1)S(1)} %middle.1.refs_0_), channel_id=1, source_target_pairs={{0,24},{8,16},{16,8},{24,0},{1,25},{9,17},{17,9},{25,1},{2,26},{10... | collective-permute-start | bytes 184328 | tf_op jit(solution)/shard_map/ppermute | solution.py:36
  32.5 0.6 %collective-permute-start.10 = (bf16[2,40,384]{2,1,0:T(8,128)(2,1)S(1)}, bf16[2,40,384]{2,1,0:T(8,128)(2,1)S(1)}, u32[]{:S(2)}, u32[]{:S(2)}) collective-permute-start(bf16[2,40,384]{2,1,0:T(8,128)(2,1)S(1)} %middle.1.refs_0_), channel_id=1, source_target_pairs={{0,16},{8,24},{16,0},{24,8},{1,17},{9,25},{17,1},{25,9},{2,18},{10... | collective-permute-start | bytes 184328 | tf_op jit(solution)/shard_map/ppermute | solution.py:36
  33.1 0.7 %collective-permute-start.9 = (bf16[2,40,384]{2,1,0:T(8,128)(2,1)S(1)}, bf16[2,40,384]{2,1,0:T(8,128)(2,1)S(1)}, u32[]{:S(2)}, u32[]{:S(2)}) collective-permute-start(bf16[2,40,384]{2,1,0:T(8,128)(2,1)S(1)} %middle.1.refs_0_), channel_id=1, source_target_pairs={{0,8},{8,0},{16,24},{24,16},{1,9},{9,1},{17,25},{25,17},{2,10},{10... | collective-permute-start | bytes 184328 | tf_op jit(solution)/shard_map/ppermute | solution.py:36
  33.8 1.6 %collective-permute-done.11.refs_3_ = bf16[2,40,384]{2,1,0:T(8,128)(2,1)S(1)} collective-permute-done((bf16[2,40,384]{2,1,0:T(8,128)(2,1)S(1)}, bf16[2,40,384]{2,1,0:T(8,128)(2,1)S(1)}, u32[]{:S(2)}, u32[]{:S(2)}) %collective-permute-start.11) | collective-permute-done | bytes 61472 | tf_op jit(solution)/shard_map/ppermute | solution.py:36
  35.4 1.4 %collective-permute-done.10.refs_2_ = bf16[2,40,384]{2,1,0:T(8,128)(2,1)S(1)} collective-permute-done((bf16[2,40,384]{2,1,0:T(8,128)(2,1)S(1)}, bf16[2,40,384]{2,1,0:T(8,128)(2,1)S(1)}, u32[]{:S(2)}, u32[]{:S(2)}) %collective-permute-start.10) | collective-permute-done | bytes 61472 | tf_op jit(solution)/shard_map/ppermute | solution.py:36
  36.8 0.6 %collective-permute-done.9.refs_1_ = bf16[2,40,384]{2,1,0:T(8,128)(2,1)S(1)} collective-permute-done((bf16[2,40,384]{2,1,0:T(8,128)(2,1)S(1)}, bf16[2,40,384]{2,1,0:T(8,128)(2,1)S(1)}, u32[]{:S(2)}, u32[]{:S(2)}) %collective-permute-start.9) | collective-permute-done | bytes 61472 | tf_op jit(solution)/shard_map/ppermute | solution.py:36
  37.4 0.1 collective-permute-start.12
  37.8 0.8 %collective-permute-done.12.refs_4_ = bf16[4,2,4,384]{3,2,1,0:T(4,128)(2,1)S(1)} collective-permute-done((bf16[4,2,4,384]{3,2,1,0:T(4,128)(2,1)S(1)}, bf16[4,2,4,384]{3,2,1,0:T(4,128)(2,1)S(1)}, u32[]{:S(2)}, u32[]{:S(2)}) %collective-permute-start.12) | collective-permute-done | bytes 24608 | tf_op jit(solution)/shard_map/ppermute | solution.py:52
  38.7 0.1 broadcast_select_fusion.2
  38.9 0.1 broadcast_select_fusion.3
  39.0 0.1 collective-permute-start.13
  39.1 2.7 %collective-permute-start.14 = (bf16[4,2,12,384]{3,2,1,0:T(8,128)(2,1)S(1)}, bf16[4,2,12,384]{3,2,1,0:T(8,128)(2,1)S(1)}, u32[]{:S(2)}, u32[]{:S(2)}) collective-permute-start(bf16[4,2,12,384]{3,2,1,0:T(8,128)(2,1)S(1)} %broadcast_select_fusion.2), channel_id=1, source_target_pairs={{2,4},{4,2},{3,5},{5,3},{10,12},{12,10},{11,13},{13,11},{18,20},{2... | collective-permute-start | bytes 221192 | tf_op jit(solution)/shard_map/ppermute | solution.py:52
  41.9 1.6 %inner.3.refs_3_ = f32[1,320,128]{2,1,0:T(8,128)S(1)} custom-call(bf16[2,40,384]{2,1,0:T(8,128)(2,1)S(1)} %middle.1.refs_0_, bf16[2,40,384]{2,1,0:T(8,128)(2,1)S(1)} %collective-permute-done.9.refs_1_, bf16[2,40,384]{2,1,0:T(8,128)(2,1)S(1)} %collective-permute-done.10.refs_2_, bf16[2,40,384]{2,1,0:T(8,128)(2,1)S(1)} %collective-permute-done.11.refs_3_, ...), custom_call_target="tpu_custom_call" | custom-call | flops 637009920 | bytes 2424832 | tf_op jit(solution)/shard_map/inner/pallas_call | solution.py:488
  43.5 0.5 collective-permute-done.13.refs_0_
  44.0 1.9 %collective-permute-done.14.refs_1_ = bf16[4,2,12,384]{3,2,1,0:T(8,128)(2,1)S(1)} collective-permute-done((bf16[4,2,12,384]{3,2,1,0:T(8,128)(2,1)S(1)}, bf16[4,2,12,384]{3,2,1,0:T(8,128)(2,1)S(1)}, u32[]{:S(2)}, u32[]{:S(2)}) %collective-permute-start.14) | collective-permute-done | bytes 73760 | tf_op jit(solution)/shard_map/ppermute | solution.py:52
  45.9 0.8 %outer.3 = (bf16[2,40,128]{2,1,0:T(8,128)(2,1)S(1)}, bf16[2,40,128]{2,1,0:T(8,128)(2,1)S(1)}, bf16[2,40,128]{2,1,0:T(8,128)(2,1)S(1)}, bf16[2,40,128]{2,1,0:T(8,128)(2,1)S(1)}) custom-call(bf16[4,2,12,384]{3,2,1,0:T(8,128)(2,1)S(1)} %collective-permute-done.13.refs_0_, bf16[4,2,12,384]{3,2,1,0:T(8,128)(2,1)S(1)} %collective-permute-done.14.refs_1_, ...), custom_call_target="tpu_custom_call" | custom-call | flops 106168320 | bytes 2383872 | tf_op jit(solution)/shard_map/outer/pallas_call | solution.py:488
  46.7 0.8 %collective-permute-start.15 = (bf16[2,40,128]{2,1,0:T(8,128)(2,1)S(1)}, bf16[2,40,128]{2,1,0:T(8,128)(2,1)S(1)}, u32[]{:S(2)}, u32[]{:S(2)}) collective-permute-start(bf16[2,40,128]{2,1,0:T(8,128)(2,1)S(1)} %get-tuple-element.30), channel_id=1, source_target_pairs={{0,8},{8,0},{16,24},{24,16},{1,9},{9,1},{17,25},{25,17},{2,10},{10... | collective-permute-start | bytes 61448 | tf_op jit(solution)/shard_map/ppermute | solution.py:36
  47.5 1.3 %collective-permute-start.16 = (bf16[2,40,128]{2,1,0:T(8,128)(2,1)S(1)}, bf16[2,40,128]{2,1,0:T(8,128)(2,1)S(1)}, u32[]{:S(2)}, u32[]{:S(2)}) collective-permute-start(bf16[2,40,128]{2,1,0:T(8,128)(2,1)S(1)} %get-tuple-element.31), channel_id=1, source_target_pairs={{0,16},{8,24},{16,0},{24,8},{1,17},{9,25},{17,1},{25,9},{2,18},{10... | collective-permute-start | bytes 61448 | tf_op jit(solution)/shard_map/ppermute | solution.py:36
  48.8 1.5 %collective-permute-start.17 = (bf16[2,40,128]{2,1,0:T(8,128)(2,1)S(1)}, bf16[2,40,128]{2,1,0:T(8,128)(2,1)S(1)}, u32[]{:S(2)}, u32[]{:S(2)}) collective-permute-start(bf16[2,40,128]{2,1,0:T(8,128)(2,1)S(1)} %get-tuple-element.32), channel_id=1, source_target_pairs={{0,24},{8,16},{16,8},{24,0},{1,25},{9,17},{17,9},{25,1},{2,26},{10... | collective-permute-start | bytes 61448 | tf_op jit(solution)/shard_map/ppermute | solution.py:36
  50.3 0.5 collective-permute-done.15.refs_1_
  50.7 0.7 %collective-permute-done.16.refs_2_ = bf16[2,40,128]{2,1,0:T(8,128)(2,1)S(1)} collective-permute-done((bf16[2,40,128]{2,1,0:T(8,128)(2,1)S(1)}, bf16[2,40,128]{2,1,0:T(8,128)(2,1)S(1)}, u32[]{:S(2)}, u32[]{:S(2)}) %collective-permute-start.16) | collective-permute-done | bytes 20512 | tf_op jit(solution)/shard_map/ppermute | solution.py:36
  51.5 2.0 %collective-permute-done.17.refs_3_ = bf16[2,40,128]{2,1,0:T(8,128)(2,1)S(1)} collective-permute-done((bf16[2,40,128]{2,1,0:T(8,128)(2,1)S(1)}, bf16[2,40,128]{2,1,0:T(8,128)(2,1)S(1)}, u32[]{:S(2)}, u32[]{:S(2)}) %collective-permute-start.17) | collective-permute-done | bytes 20512 | tf_op jit(solution)/shard_map/ppermute | solution.py:36
  53.5 1.0 %final.1 = bf16[2,10,4,384]{3,2,1,0:T(4,128)(2,1)} custom-call(bf16[2,40,128]{2,1,0:T(8,128)(2,1)S(1)} %get-tuple-element.29.refs_0_, bf16[2,40,128]{2,1,0:T(8,128)(2,1)S(1)} %collective-permute-done.15.refs_1_, bf16[2,40,128]{2,1,0:T(8,128)(2,1)S(1)} %collective-permute-done.16.refs_2_, bf16[2,40,128]{2,1,0:T(8,128)(2,1)S(1)} %collective-permute-done.17.refs_3_, ...), custom_call_target="tpu_custom_call" | custom-call | bytes 267776 | tf_op jit(solution)/shard_map/final/pallas_call | solution.py:488
  (49 shorter events, 1.0 us)
Async XLA Ops:
  0.9 0.7 %copy-start.7 = (f32[384]{0:T(512)S(1)}, f32[384]{0:T(512)}, u32[]{:S(2)}) copy-start(f32[384]{0:T(512)} %refs_6_.3) | copy-start | bytes 4612
  2.1 15.3 %copy-start = (bf16[3,3,3,96,384]{4,3,2,1,0:T(8,128)(2,1)S(1)}, bf16[3,3,3,96,384]{4,3,2,1,0:T(8,128)(2,1)}, u32[]{:S(2)}) copy-start(bf16[3,3,3,96,384]{4,3,2,1,0:T(8,128)(2,1)} %refs_2_.3) | copy-start | bytes 5971972
  2.1 4.5 %collective-permute-start = (bf16[2,40,512]{2,1,0:T(8,128)(2,1)S(1)}, bf16[2,40,512]{2,1,0:T(8,128)(2,1)S(1)}, u32[]{:S(2)}, u32[]{:S(2)}) collective-permute-start(bf16[2,40,512]{2,1,0:T(8,128)(2,1)S(1)} %get-tuple-element.20), channel_id=1, source_target_pairs={{0,8},{8,0},{16,24},{24,16},{1,9},{9,1},{17,25},{25,17},{2,10},{10... | collective-permute-start | bytes 245768 | tf_op jit(solution)/shard_map/ppermute | solution.py:36
  3.7 5.3 %collective-permute-start.1 = (bf16[2,40,512]{2,1,0:T(8,128)(2,1)S(1)}, bf16[2,40,512]{2,1,0:T(8,128)(2,1)S(1)}, u32[]{:S(2)}, u32[]{:S(2)}) collective-permute-start(bf16[2,40,512]{2,1,0:T(8,128)(2,1)S(1)} %get-tuple-element.21), channel_id=1, source_target_pairs={{0,16},{8,24},{16,0},{24,8},{1,17},{9,25},{17,1},{25,9},{2,18},{10... | collective-permute-start | bytes 245768 | tf_op jit(solution)/shard_map/ppermute | solution.py:36
  5.2 5.3 %collective-permute-start.2 = (bf16[2,40,512]{2,1,0:T(8,128)(2,1)S(1)}, bf16[2,40,512]{2,1,0:T(8,128)(2,1)S(1)}, u32[]{:S(2)}, u32[]{:S(2)}) collective-permute-start(bf16[2,40,512]{2,1,0:T(8,128)(2,1)S(1)} %get-tuple-element.22), channel_id=1, source_target_pairs={{0,24},{8,16},{16,8},{24,0},{1,25},{9,17},{17,9},{25,1},{2,26},{10... | collective-permute-start | bytes 245768 | tf_op jit(solution)/shard_map/ppermute | solution.py:36
  10.6 1.3 %collective-permute-start.3 = (bf16[4,2,4,512]{3,2,1,0:T(4,128)(2,1)S(1)}, bf16[4,2,4,512]{3,2,1,0:T(4,128)(2,1)S(1)}, u32[]{:S(2)}, u32[]{:S(2)}) collective-permute-start(bf16[4,2,4,512]{3,2,1,0:T(4,128)(2,1)S(1)} %maximum_select_fusion), channel_id=1, source_target_pairs={{0,1},{1,0},{2,3},{3,2},{4,5},{5,4},{6,7},{7,6},{8,9},{9,8},{10,11... | collective-permute-start | bytes 98312 | tf_op jit(solution)/shard_map/ppermute | solution.py:52
  12.3 9.5 %collective-permute-start.4 = (bf16[4,2,12,512]{3,2,1,0:T(8,128)(2,1)S(1)}, bf16[4,2,12,512]{3,2,1,0:T(8,128)(2,1)S(1)}, u32[]{:S(2)}, u32[]{:S(2)}) collective-permute-start(bf16[4,2,12,512]{3,2,1,0:T(8,128)(2,1)S(1)} %broadcast_select_fusion.1), channel_id=1, source_target_pairs={{0,2},{4,6},{2,0},{6,4},{1,3},{5,7},{3,1},{7,5},{8,10},{12,14},{10... | collective-permute-start | bytes 294920 | tf_op jit(solution)/shard_map/ppermute | solution.py:52
  12.8 9.0 %collective-permute-start.5 = (bf16[4,2,12,512]{3,2,1,0:T(8,128)(2,1)S(1)}, bf16[4,2,12,512]{3,2,1,0:T(8,128)(2,1)S(1)}, u32[]{:S(2)}, u32[]{:S(2)}) collective-permute-start(bf16[4,2,12,512]{3,2,1,0:T(8,128)(2,1)S(1)} %broadcast_select_fusion), channel_id=1, source_target_pairs={{2,4},{4,2},{3,5},{5,3},{10,12},{12,10},{11,13},{13,11},{18,20},{2... | collective-permute-start | bytes 294920 | tf_op jit(solution)/shard_map/ppermute | solution.py:52
  17.4 1.6 %copy-start.1 = (bf16[3,3,3,96,384]{4,3,2,1,0:T(8,128)(2,1)S(1)}, bf16[3,3,3,96,384]{4,3,2,1,0:T(8,128)(2,1)}, u32[]{:S(2)}) copy-start(bf16[3,3,3,96,384]{4,3,2,1,0:T(8,128)(2,1)} %refs_3_.1) | copy-start | bytes 5971972
  19.0 2.8 %copy-start.2 = (bf16[3,3,3,96,384]{4,3,2,1,0:T(8,128)(2,1)S(1)}, bf16[3,3,3,96,384]{4,3,2,1,0:T(8,128)(2,1)}, u32[]{:S(2)}) copy-start(bf16[3,3,3,96,384]{4,3,2,1,0:T(8,128)(2,1)} %refs_3_.1) | copy-start | bytes 5971972
  21.8 8.0 %copy-start.5 = (f32[384]{0:T(512)S(1)}, f32[384]{0:T(512)}, u32[]{:S(2)}) copy-start(f32[384]{0:T(512)} %refs_4_.1) | copy-start | bytes 4612
  21.8 8.0 %copy-start.6 = (f32[384]{0:T(512)S(1)}, f32[384]{0:T(512)}, u32[]{:S(2)}) copy-start(f32[384]{0:T(512)} %refs_5_.4) | copy-start | bytes 4612
  23.1 5.3 %collective-permute-start.6 = (bf16[2,40,512]{2,1,0:T(8,128)(2,1)S(1)}, bf16[2,40,512]{2,1,0:T(8,128)(2,1)S(1)}, u32[]{:S(2)}, u32[]{:S(2)}) collective-permute-start(bf16[2,40,512]{2,1,0:T(8,128)(2,1)S(1)} %get-tuple-element.26), channel_id=1, source_target_pairs={{0,8},{8,0},{16,24},{24,16},{1,9},{9,1},{17,25},{25,17},{2,10},{10... | collective-permute-start | bytes 245768 | tf_op jit(solution)/shard_map/ppermute | solution.py:36
  23.7 5.2 %collective-permute-start.7 = (bf16[2,40,512]{2,1,0:T(8,128)(2,1)S(1)}, bf16[2,40,512]{2,1,0:T(8,128)(2,1)S(1)}, u32[]{:S(2)}, u32[]{:S(2)}) collective-permute-start(bf16[2,40,512]{2,1,0:T(8,128)(2,1)S(1)} %get-tuple-element.27), channel_id=1, source_target_pairs={{0,16},{8,24},{16,0},{24,8},{1,17},{9,25},{17,1},{25,9},{2,18},{10... | collective-permute-start | bytes 245768 | tf_op jit(solution)/shard_map/ppermute | solution.py:36
  24.5 5.3 %collective-permute-start.8 = (bf16[2,40,512]{2,1,0:T(8,128)(2,1)S(1)}, bf16[2,40,512]{2,1,0:T(8,128)(2,1)S(1)}, u32[]{:S(2)}, u32[]{:S(2)}) collective-permute-start(bf16[2,40,512]{2,1,0:T(8,128)(2,1)S(1)} %get-tuple-element.28), channel_id=1, source_target_pairs={{0,24},{8,16},{16,8},{24,0},{1,25},{9,17},{17,9},{25,1},{2,26},{10... | collective-permute-start | bytes 245768 | tf_op jit(solution)/shard_map/ppermute | solution.py:36
  30.2 5.2 %collective-permute-start.11 = (bf16[2,40,384]{2,1,0:T(8,128)(2,1)S(1)}, bf16[2,40,384]{2,1,0:T(8,128)(2,1)S(1)}, u32[]{:S(2)}, u32[]{:S(2)}) collective-permute-start(bf16[2,40,384]{2,1,0:T(8,128)(2,1)S(1)} %middle.1.refs_0_), channel_id=1, source_target_pairs={{0,24},{8,16},{16,8},{24,0},{1,25},{9,17},{17,9},{25,1},{2,26},{10... | collective-permute-start | bytes 184328 | tf_op jit(solution)/shard_map/ppermute | solution.py:36
  32.5 4.3 %collective-permute-start.10 = (bf16[2,40,384]{2,1,0:T(8,128)(2,1)S(1)}, bf16[2,40,384]{2,1,0:T(8,128)(2,1)S(1)}, u32[]{:S(2)}, u32[]{:S(2)}) collective-permute-start(bf16[2,40,384]{2,1,0:T(8,128)(2,1)S(1)} %middle.1.refs_0_), channel_id=1, source_target_pairs={{0,16},{8,24},{16,0},{24,8},{1,17},{9,25},{17,1},{25,9},{2,18},{10... | collective-permute-start | bytes 184328 | tf_op jit(solution)/shard_map/ppermute | solution.py:36
  33.1 4.2 %collective-permute-start.9 = (bf16[2,40,384]{2,1,0:T(8,128)(2,1)S(1)}, bf16[2,40,384]{2,1,0:T(8,128)(2,1)S(1)}, u32[]{:S(2)}, u32[]{:S(2)}) collective-permute-start(bf16[2,40,384]{2,1,0:T(8,128)(2,1)S(1)} %middle.1.refs_0_), channel_id=1, source_target_pairs={{0,8},{8,0},{16,24},{24,16},{1,9},{9,1},{17,25},{25,17},{2,10},{10... | collective-permute-start | bytes 184328 | tf_op jit(solution)/shard_map/ppermute | solution.py:36
  37.4 1.3 %collective-permute-start.12 = (bf16[4,2,4,384]{3,2,1,0:T(4,128)(2,1)S(1)}, bf16[4,2,4,384]{3,2,1,0:T(4,128)(2,1)S(1)}, u32[]{:S(2)}, u32[]{:S(2)}) collective-permute-start(bf16[4,2,4,384]{3,2,1,0:T(4,128)(2,1)S(1)} %maximum_select_fusion.1), channel_id=1, source_target_pairs={{0,1},{1,0},{2,3},{3,2},{4,5},{5,4},{6,7},{7,6},{8,9},{9,8},{10,11... | collective-permute-start | bytes 73736 | tf_op jit(solution)/shard_map/ppermute | solution.py:52
  39.0 14.5 %copy-start.3 = (bf16[2,4,10,384]{3,1,2,0:T(4,128)(2,1)S(1)}, bf16[2,4,10,384]{3,1,2,0:T(4,128)(2,1)}, u32[]{:S(2)}) copy-start(bf16[2,4,10,384]{3,1,2,0:T(4,128)(2,1)} %param.8) | copy-start | bytes 184324
  39.0 14.5 %copy-start.4 = (bf16[2,4,10,384]{3,1,2,0:T(4,128)(2,1)S(1)}, bf16[2,4,10,384]{3,1,2,0:T(4,128)(2,1)}, u32[]{:S(2)}) copy-start(bf16[2,4,10,384]{3,1,2,0:T(4,128)(2,1)} %param.7) | copy-start | bytes 184324
  39.0 14.4 %copy-start.8 = (f32[384]{0:T(512)S(1)}, f32[384]{0:T(512)}, u32[]{:S(2)}) copy-start(f32[384]{0:T(512)} %refs_6_.3) | copy-start | bytes 4612
  39.0 4.9 %collective-permute-start.13 = (bf16[4,2,12,384]{3,2,1,0:T(8,128)(2,1)S(1)}, bf16[4,2,12,384]{3,2,1,0:T(8,128)(2,1)S(1)}, u32[]{:S(2)}, u32[]{:S(2)}) collective-permute-start(bf16[4,2,12,384]{3,2,1,0:T(8,128)(2,1)S(1)} %broadcast_select_fusion.3), channel_id=1, source_target_pairs={{0,2},{4,6},{2,0},{6,4},{1,3},{5,7},{3,1},{7,5},{8,10},{12,14},{10... | collective-permute-start | bytes 221192 | tf_op jit(solution)/shard_map/ppermute | solution.py:52
  39.1 6.8 %collective-permute-start.14 = (bf16[4,2,12,384]{3,2,1,0:T(8,128)(2,1)S(1)}, bf16[4,2,12,384]{3,2,1,0:T(8,128)(2,1)S(1)}, u32[]{:S(2)}, u32[]{:S(2)}) collective-permute-start(bf16[4,2,12,384]{3,2,1,0:T(8,128)(2,1)S(1)} %broadcast_select_fusion.2), channel_id=1, source_target_pairs={{2,4},{4,2},{3,5},{5,3},{10,12},{12,10},{11,13},{13,11},{18,20},{2... | collective-permute-start | bytes 221192 | tf_op jit(solution)/shard_map/ppermute | solution.py:52
  46.7 4.0 %collective-permute-start.15 = (bf16[2,40,128]{2,1,0:T(8,128)(2,1)S(1)}, bf16[2,40,128]{2,1,0:T(8,128)(2,1)S(1)}, u32[]{:S(2)}, u32[]{:S(2)}) collective-permute-start(bf16[2,40,128]{2,1,0:T(8,128)(2,1)S(1)} %get-tuple-element.30), channel_id=1, source_target_pairs={{0,8},{8,0},{16,24},{24,16},{1,9},{9,1},{17,25},{25,17},{2,10},{10... | collective-permute-start | bytes 61448 | tf_op jit(solution)/shard_map/ppermute | solution.py:36
  47.5 4.0 %collective-permute-start.16 = (bf16[2,40,128]{2,1,0:T(8,128)(2,1)S(1)}, bf16[2,40,128]{2,1,0:T(8,128)(2,1)S(1)}, u32[]{:S(2)}, u32[]{:S(2)}) collective-permute-start(bf16[2,40,128]{2,1,0:T(8,128)(2,1)S(1)} %get-tuple-element.31), channel_id=1, source_target_pairs={{0,16},{8,24},{16,0},{24,8},{1,17},{9,25},{17,1},{25,9},{2,18},{10... | collective-permute-start | bytes 61448 | tf_op jit(solution)/shard_map/ppermute | solution.py:36
  48.8 4.7 %collective-permute-start.17 = (bf16[2,40,128]{2,1,0:T(8,128)(2,1)S(1)}, bf16[2,40,128]{2,1,0:T(8,128)(2,1)S(1)}, u32[]{:S(2)}, u32[]{:S(2)}) collective-permute-start(bf16[2,40,128]{2,1,0:T(8,128)(2,1)S(1)} %get-tuple-element.32), channel_id=1, source_target_pairs={{0,24},{8,16},{16,8},{24,0},{1,25},{9,17},{17,9},{25,1},{2,26},{10... | collective-permute-start | bytes 61448 | tf_op jit(solution)/shard_map/ppermute | solution.py:36

commit v5 on v4

--- a/solution.py
+++ b/solution.py
@@ -481,7 +481,7 @@
     return sum(math.prod(s.shape) * s.dtype.itemsize for s in structs)
 
 
-def call(kernel, outs, scratch=(), flops=0, spare=2, covered=0, name=None):
+def call(kernel, outs, scratch=(), flops=0, spare=2, covered=0):
     def run(*operands):
         held = size_of(outs) + size_of(operands)
         grant = 2 * held + size_of(scratch) + spare * 2**20
@@ -493,13 +493,12 @@
                 flops=flops + covered, bytes_accessed=held, transcendentals=0
             ),
             compiler_params=pltpu.CompilerParams(vmem_limit_bytes=min(grant, 60 * 2**20)),
-            name=name,
         )(*operands)
 
     return run
 
 
-def on_device(
+def steps(
     features, reward_grad, first_kernel, second_kernel, first_gain, second_gain, first_bias
 ):
     peers = lax.axis_size("tm")
@@ -536,7 +535,6 @@
             [pltpu.VMEM((tiles, plane * total, lanes), f32), *ahead_scratch, *taps],
             flops * len(kernels),
             spare=8,
-            name="inner",
         )(*blocks, *sides, *kernels)
         return call(
             functools.partial(outer_kernel, peers, frames, cells, len(ends), behind),
@@ -547,7 +545,6 @@
             ],
             flops * len(kernels) // 6,
             spare=8,
-            name="outer",
         )(*ends, *kernels, *sums)
 
     packed = call(
@@ -555,14 +552,11 @@
         [struct((frames, count, channels + wide), bf16)] * peers,
         [pltpu.VMEM((frames, 2, count, channels), f32)],
         covered=4 * 10**9,
-        name="pack",
     )(jnp.stack(held), first_gain)
     sums = convolved(tm_exchange(packed), [first_kernel, second_kernel])
     got = tm_exchange(sums)
     hidden_grad = call(
-        functools.partial(middle_kernel, peers, width),
-        [struct((frames, count, channels), bf16)],
-        name="middle",
+        functools.partial(middle_kernel, peers, width), [struct((frames, count, channels), bf16)]
     )(*got, second_gain, first_bias)[0]
     backs = convolved(tm_exchange([hidden_grad] * peers), [first_kernel])
     got = tm_exchange(backs)
@@ -570,7 +564,6 @@
         functools.partial(final_kernel, peers, width),
         [struct(held[0].shape, bf16)],
         [pltpu.VMEM((frames, 3, count, channels), f32)],
-        name="final",
     )(*got, *held, first_gain)[0]
     return result.transpose(by_col)
 
@@ -586,6 +579,4 @@
         P(),
     )
     out_specs = P("tm", "row", "col", None)
-    return jax.shard_map(
-        on_device, mesh=mesh, in_specs=in_specs, out_specs=out_specs, check_vma=False
-    )
+    return jax.shard_map(steps, mesh=mesh, in_specs=in_specs, out_specs=out_specs, check_vma=False)

time: 54.8 us -> 54.8 us (level)
  no operation moved by 1% of the time
where the time goes in v5:
time: 54.8 us; the launch traced here: 54.5 us
  starting transfers between devices  22.4 us (41%)
  waiting for transfers between devices  18.7 us (34%)
  Pallas kernels  8.39 us (15%)
  local copies, waits for them, and re-layouts  3.08 us (6%)
  other arithmetic  1.66 us (3%)
    ppermute x12, waiting for transfers between devices, tm_exchange(): got.append(lax.ppermute(blocks[step], 'tm', pairs))  14.6 us
    ppermute x12, starting transfers between devices, tm_exchange(): got.append(lax.ppermute(blocks[step], 'tm', pairs))  14.3 us
    pallas_call x7, Pallas kernels, run(): pl.pallas_call(kernel, out_shape=outs, scratch_shapes=list(scratch), cost...  8.39 us
    ppermute x6, starting transfers between devices, halo_swaps(): got.append(lax.ppermute(jnp.where(even, *value), axis, pairs))  8.07 us
    ppermute x6, waiting for transfers between devices, halo_swaps(): got.append(lax.ppermute(jnp.where(even, *value), axis, pairs))  4.08 us
    unnamed x18, local copies, waits for them, and re-layouts  2.27 us
  transfers between devices with their start and end apart: 18, of which 16 were waited for; matrix products, arithmetic and copies ran while one was open for 1% of the time, Pallas kernels for 8%

profile of v5, /device:TPU:8, one launch (start us, length us, event | category | flops | bytes accessed | tf_op | source)
XLA Modules:
  0.0 54.5 jit_solution(8918497581997978684)
XLA Ops:
  0.0 0.9 %pad_maximum_fusion.2.both_ref = bf16[2,2,10,4,384]{4,3,2,1,0:T(4,128)(2,1)S(1)} fusion(bf16[1,2,10,4,384]{4,3,2,1,0:T(4,128)(2,1)} %bitcast.55, bf16[1,2,10,4,384]{4,3,2,1,0:T(4,128)(2,1)} %bitcast.57), kind=kLoop, calls=%fused_computation.4 | loop fusion | flops 61440 | bytes 245760 | tf_op jit(solution)/shard_map/stack | solution.py:555
  1.0 0.7 %copy-done.7 = f32[384]{0:T(512)S(1)} copy-done((f32[384]{0:T(512)S(1)}, f32[384]{0:T(512)}, u32[]{:S(2)}) %copy-start.7) | copy-done | bytes 1560
  1.6 0.5 shard_map.73
  2.1 1.6 %collective-permute-start = (bf16[2,40,512]{2,1,0:T(8,128)(2,1)S(1)}, bf16[2,40,512]{2,1,0:T(8,128)(2,1)S(1)}, u32[]{:S(2)}, u32[]{:S(2)}) collective-permute-start(bf16[2,40,512]{2,1,0:T(8,128)(2,1)S(1)} %get-tuple-element.20), channel_id=1, source_target_pairs={{0,8},{8,0},{16,24},{24,16},{1,9},{9,1},{17,25},{25,17},{2,10},{10... | collective-permute-start | bytes 245768 | tf_op jit(solution)/shard_map/ppermute | solution.py:36
  3.7 1.5 %collective-permute-start.1 = (bf16[2,40,512]{2,1,0:T(8,128)(2,1)S(1)}, bf16[2,40,512]{2,1,0:T(8,128)(2,1)S(1)}, u32[]{:S(2)}, u32[]{:S(2)}) collective-permute-start(bf16[2,40,512]{2,1,0:T(8,128)(2,1)S(1)} %get-tuple-element.21), channel_id=1, source_target_pairs={{0,16},{8,24},{16,0},{24,8},{1,17},{9,25},{17,1},{25,9},{2,18},{10... | collective-permute-start | bytes 245768 | tf_op jit(solution)/shard_map/ppermute | solution.py:36
  5.2 0.5 collective-permute-start.2
  5.7 0.9 %collective-permute-done.refs_1_ = bf16[2,40,512]{2,1,0:T(8,128)(2,1)S(1)} collective-permute-done((bf16[2,40,512]{2,1,0:T(8,128)(2,1)S(1)}, bf16[2,40,512]{2,1,0:T(8,128)(2,1)S(1)}, u32[]{:S(2)}, u32[]{:S(2)}) %collective-permute-start) | collective-permute-done | bytes 81952 | tf_op jit(solution)/shard_map/ppermute | solution.py:36
  6.6 2.4 %collective-permute-done.1.refs_2_ = bf16[2,40,512]{2,1,0:T(8,128)(2,1)S(1)} collective-permute-done((bf16[2,40,512]{2,1,0:T(8,128)(2,1)S(1)}, bf16[2,40,512]{2,1,0:T(8,128)(2,1)S(1)}, u32[]{:S(2)}, u32[]{:S(2)}) %collective-permute-start.1) | collective-permute-done | bytes 81952 | tf_op jit(solution)/shard_map/ppermute | solution.py:36
  9.0 1.5 %collective-permute-done.2.refs_3_ = bf16[2,40,512]{2,1,0:T(8,128)(2,1)S(1)} collective-permute-done((bf16[2,40,512]{2,1,0:T(8,128)(2,1)S(1)}, bf16[2,40,512]{2,1,0:T(8,128)(2,1)S(1)}, u32[]{:S(2)}, u32[]{:S(2)}) %collective-permute-start.2) | collective-permute-done | bytes 81952 | tf_op jit(solution)/shard_map/ppermute | solution.py:36
  10.6 0.1 collective-permute-start.3
  11.0 0.9 %collective-permute-done.3.refs_4_ = bf16[4,2,4,512]{3,2,1,0:T(4,128)(2,1)S(1)} collective-permute-done((bf16[4,2,4,512]{3,2,1,0:T(4,128)(2,1)S(1)}, bf16[4,2,4,512]{3,2,1,0:T(4,128)(2,1)S(1)}, u32[]{:S(2)}, u32[]{:S(2)}) %collective-permute-start.3) | collective-permute-done | bytes 32800 | tf_op jit(solution)/shard_map/ppermute | solution.py:52
  12.0 0.2 broadcast_select_fusion
  12.1 0.2 broadcast_select_fusion.1
  12.3 0.5 collective-permute-start.4
  12.8 4.6 %collective-permute-start.5 = (bf16[4,2,12,512]{3,2,1,0:T(8,128)(2,1)S(1)}, bf16[4,2,12,512]{3,2,1,0:T(8,128)(2,1)S(1)}, u32[]{:S(2)}, u32[]{:S(2)}) collective-permute-start(bf16[4,2,12,512]{3,2,1,0:T(8,128)(2,1)S(1)} %broadcast_select_fusion), channel_id=1, source_target_pairs={{2,4},{4,2},{3,5},{5,3},{10,12},{12,10},{11,13},{13,11},{18,20},{2... | collective-permute-start | bytes 294920 | tf_op jit(solution)/shard_map/ppermute | solution.py:52
  17.4 1.5 %copy-done.1 = bf16[3,3,3,96,384]{4,3,2,1,0:T(8,128)(2,1)S(1)} copy-done((bf16[3,3,3,96,384]{4,3,2,1,0:T(8,128)(2,1)S(1)}, bf16[3,3,3,96,384]{4,3,2,1,0:T(8,128)(2,1)}, u32[]{:S(2)}) %copy-start.1) | copy-done | bytes 1990680
  19.0 2.8 %shard_map.74 = (f32[3,320,128]{2,1,0:T(8,128)S(1)}, f32[1,320,128]{2,1,0:T(8,128)S(1)}) custom-call(bf16[2,40,512]{2,1,0:T(8,128)(2,1)S(1)} %get-tuple-element.19.refs_0_, bf16[2,40,512]{2,1,0:T(8,128)(2,1)S(1)} %collective-permute-done.refs_1_, bf16[2,40,512]{2,1,0:T(8,128)(2,1)S(1)} %collective-permute-done.1.refs_2_, ...), custom_call_target="tpu_custom_call" | custom-call | flops 1274019840 | bytes 4997120 | tf_op jit(solution)/shard_map/pallas_call | solution.py:488
  21.8 1.3 %shard_map.75 = (bf16[2,40,512]{2,1,0:T(8,128)(2,1)S(1)}, bf16[2,40,512]{2,1,0:T(8,128)(2,1)S(1)}, bf16[2,40,512]{2,1,0:T(8,128)(2,1)S(1)}, bf16[2,40,512]{2,1,0:T(8,128)(2,1)S(1)}) custom-call(bf16[4,2,12,512]{3,2,1,0:T(8,128)(2,1)S(1)} %collective-permute-done.4.refs_0_, bf16[4,2,12,512]{3,2,1,0:T(8,128)(2,1)S(1)} %collective-permute-done.5.refs_1_, ...), custom_call_target="tpu_custom_call" | custom-call | flops 212336640 | bytes 5160960 | tf_op jit(solution)/shard_map/pallas_call | solution.py:488
  23.1 0.6 %collective-permute-start.6 = (bf16[2,40,512]{2,1,0:T(8,128)(2,1)S(1)}, bf16[2,40,512]{2,1,0:T(8,128)(2,1)S(1)}, u32[]{:S(2)}, u32[]{:S(2)}) collective-permute-start(bf16[2,40,512]{2,1,0:T(8,128)(2,1)S(1)} %get-tuple-element.26), channel_id=1, source_target_pairs={{0,8},{8,0},{16,24},{24,16},{1,9},{9,1},{17,25},{25,17},{2,10},{10... | collective-permute-start | bytes 245768 | tf_op jit(solution)/shard_map/ppermute | solution.py:36
  23.7 0.7 %collective-permute-start.7 = (bf16[2,40,512]{2,1,0:T(8,128)(2,1)S(1)}, bf16[2,40,512]{2,1,0:T(8,128)(2,1)S(1)}, u32[]{:S(2)}, u32[]{:S(2)}) collective-permute-start(bf16[2,40,512]{2,1,0:T(8,128)(2,1)S(1)} %get-tuple-element.27), channel_id=1, source_target_pairs={{0,16},{8,24},{16,0},{24,8},{1,17},{9,25},{17,1},{25,9},{2,18},{10... | collective-permute-start | bytes 245768 | tf_op jit(solution)/shard_map/ppermute | solution.py:36
  24.5 2.2 %collective-permute-start.8 = (bf16[2,40,512]{2,1,0:T(8,128)(2,1)S(1)}, bf16[2,40,512]{2,1,0:T(8,128)(2,1)S(1)}, u32[]{:S(2)}, u32[]{:S(2)}) collective-permute-start(bf16[2,40,512]{2,1,0:T(8,128)(2,1)S(1)} %get-tuple-element.28), channel_id=1, source_target_pairs={{0,24},{8,16},{16,8},{24,0},{1,25},{9,17},{17,9},{25,1},{2,26},{10... | collective-permute-start | bytes 245768 | tf_op jit(solution)/shard_map/ppermute | solution.py:36
  26.7 1.8 %collective-permute-done.6.refs_1_ = bf16[2,40,512]{2,1,0:T(8,128)(2,1)S(1)} collective-permute-done((bf16[2,40,512]{2,1,0:T(8,128)(2,1)S(1)}, bf16[2,40,512]{2,1,0:T(8,128)(2,1)S(1)}, u32[]{:S(2)}, u32[]{:S(2)}) %collective-permute-start.6) | collective-permute-done | bytes 81952 | tf_op jit(solution)/shard_map/ppermute | solution.py:36
  28.4 0.5 collective-permute-done.7.refs_2_
  28.9 0.9 %collective-permute-done.8.refs_3_ = bf16[2,40,512]{2,1,0:T(8,128)(2,1)S(1)} collective-permute-done((bf16[2,40,512]{2,1,0:T(8,128)(2,1)S(1)}, bf16[2,40,512]{2,1,0:T(8,128)(2,1)S(1)}, u32[]{:S(2)}, u32[]{:S(2)}) %collective-permute-start.8) | collective-permute-done | bytes 81952 | tf_op jit(solution)/shard_map/ppermute | solution.py:36
  29.8 0.4 shard_map.76.refs_0_
  30.2 2.3 %collective-permute-start.11 = (bf16[2,40,384]{2,1,0:T(8,128)(2,1)S(1)}, bf16[2,40,384]{2,1,0:T(8,128)(2,1)S(1)}, u32[]{:S(2)}, u32[]{:S(2)}) collective-permute-start(bf16[2,40,384]{2,1,0:T(8,128)(2,1)S(1)} %shard_map.76.refs_0_), channel_id=1, source_target_pairs={{0,24},{8,16},{16,8},{24,0},{1,25},{9,17},{17,9},{25,1},{2,26},{10... | collective-permute-start | bytes 184328 | tf_op jit(solution)/shard_map/ppermute | solution.py:36
  32.5 0.6 %collective-permute-start.10 = (bf16[2,40,384]{2,1,0:T(8,128)(2,1)S(1)}, bf16[2,40,384]{2,1,0:T(8,128)(2,1)S(1)}, u32[]{:S(2)}, u32[]{:S(2)}) collective-permute-start(bf16[2,40,384]{2,1,0:T(8,128)(2,1)S(1)} %shard_map.76.refs_0_), channel_id=1, source_target_pairs={{0,16},{8,24},{16,0},{24,8},{1,17},{9,25},{17,1},{25,9},{2,18},{10... | collective-permute-start | bytes 184328 | tf_op jit(solution)/shard_map/ppermute | solution.py:36
  33.1 0.7 %collective-permute-start.9 = (bf16[2,40,384]{2,1,0:T(8,128)(2,1)S(1)}, bf16[2,40,384]{2,1,0:T(8,128)(2,1)S(1)}, u32[]{:S(2)}, u32[]{:S(2)}) collective-permute-start(bf16[2,40,384]{2,1,0:T(8,128)(2,1)S(1)} %shard_map.76.refs_0_), channel_id=1, source_target_pairs={{0,8},{8,0},{16,24},{24,16},{1,9},{9,1},{17,25},{25,17},{2,10},{10... | collective-permute-start | bytes 184328 | tf_op jit(solution)/shard_map/ppermute | solution.py:36
  33.8 1.6 %collective-permute-done.11.refs_3_ = bf16[2,40,384]{2,1,0:T(8,128)(2,1)S(1)} collective-permute-done((bf16[2,40,384]{2,1,0:T(8,128)(2,1)S(1)}, bf16[2,40,384]{2,1,0:T(8,128)(2,1)S(1)}, u32[]{:S(2)}, u32[]{:S(2)}) %collective-permute-start.11) | collective-permute-done | bytes 61472 | tf_op jit(solution)/shard_map/ppermute | solution.py:36
  35.4 1.4 %collective-permute-done.10.refs_2_ = bf16[2,40,384]{2,1,0:T(8,128)(2,1)S(1)} collective-permute-done((bf16[2,40,384]{2,1,0:T(8,128)(2,1)S(1)}, bf16[2,40,384]{2,1,0:T(8,128)(2,1)S(1)}, u32[]{:S(2)}, u32[]{:S(2)}) %collective-permute-start.10) | collective-permute-done | bytes 61472 | tf_op jit(solution)/shard_map/ppermute | solution.py:36
  36.8 0.6 %collective-permute-done.9.refs_1_ = bf16[2,40,384]{2,1,0:T(8,128)(2,1)S(1)} collective-permute-done((bf16[2,40,384]{2,1,0:T(8,128)(2,1)S(1)}, bf16[2,40,384]{2,1,0:T(8,128)(2,1)S(1)}, u32[]{:S(2)}, u32[]{:S(2)}) %collective-permute-start.9) | collective-permute-done | bytes 61472 | tf_op jit(solution)/shard_map/ppermute | solution.py:36
  37.4 0.1 collective-permute-start.12
  37.8 0.8 %collective-permute-done.12.refs_4_ = bf16[4,2,4,384]{3,2,1,0:T(4,128)(2,1)S(1)} collective-permute-done((bf16[4,2,4,384]{3,2,1,0:T(4,128)(2,1)S(1)}, bf16[4,2,4,384]{3,2,1,0:T(4,128)(2,1)S(1)}, u32[]{:S(2)}, u32[]{:S(2)}) %collective-permute-start.12) | collective-permute-done | bytes 24608 | tf_op jit(solution)/shard_map/ppermute | solution.py:52
  38.7 0.1 broadcast_select_fusion.2
  38.9 0.1 broadcast_select_fusion.3
  39.0 0.1 collective-permute-start.13
  39.1 2.7 %collective-permute-start.14 = (bf16[4,2,12,384]{3,2,1,0:T(8,128)(2,1)S(1)}, bf16[4,2,12,384]{3,2,1,0:T(8,128)(2,1)S(1)}, u32[]{:S(2)}, u32[]{:S(2)}) collective-permute-start(bf16[4,2,12,384]{3,2,1,0:T(8,128)(2,1)S(1)} %broadcast_select_fusion.2), channel_id=1, source_target_pairs={{2,4},{4,2},{3,5},{5,3},{10,12},{12,10},{11,13},{13,11},{18,20},{2... | collective-permute-start | bytes 221192 | tf_op jit(solution)/shard_map/ppermute | solution.py:52
  41.9 1.6 %shard_map.77.refs_3_ = f32[1,320,128]{2,1,0:T(8,128)S(1)} custom-call(bf16[2,40,384]{2,1,0:T(8,128)(2,1)S(1)} %shard_map.76.refs_0_, bf16[2,40,384]{2,1,0:T(8,128)(2,1)S(1)} %collective-permute-done.9.refs_1_, bf16[2,40,384]{2,1,0:T(8,128)(2,1)S(1)} %collective-permute-done.10.refs_2_, bf16[2,40,384]{2,1,0:T(8,128)(2,1)S(1)} %collective-permute-done.11.refs_3_, ...), custom_call_target="tpu_custom_call" | custom-call | flops 637009920 | bytes 2424832 | tf_op jit(solution)/shard_map/pallas_call | solution.py:488
  43.5 0.5 collective-permute-done.13.refs_0_
  44.0 1.9 %collective-permute-done.14.refs_1_ = bf16[4,2,12,384]{3,2,1,0:T(8,128)(2,1)S(1)} collective-permute-done((bf16[4,2,12,384]{3,2,1,0:T(8,128)(2,1)S(1)}, bf16[4,2,12,384]{3,2,1,0:T(8,128)(2,1)S(1)}, u32[]{:S(2)}, u32[]{:S(2)}) %collective-permute-start.14) | collective-permute-done | bytes 73760 | tf_op jit(solution)/shard_map/ppermute | solution.py:52
  45.9 0.8 %shard_map.78 = (bf16[2,40,128]{2,1,0:T(8,128)(2,1)S(1)}, bf16[2,40,128]{2,1,0:T(8,128)(2,1)S(1)}, bf16[2,40,128]{2,1,0:T(8,128)(2,1)S(1)}, bf16[2,40,128]{2,1,0:T(8,128)(2,1)S(1)}) custom-call(bf16[4,2,12,384]{3,2,1,0:T(8,128)(2,1)S(1)} %collective-permute-done.13.refs_0_, bf16[4,2,12,384]{3,2,1,0:T(8,128)(2,1)S(1)} %collective-permute-done.14.refs_1_, ...), custom_call_target="tpu_custom_call" | custom-call | flops 106168320 | bytes 2383872 | tf_op jit(solution)/shard_map/pallas_call | solution.py:488
  46.7 0.8 %collective-permute-start.15 = (bf16[2,40,128]{2,1,0:T(8,128)(2,1)S(1)}, bf16[2,40,128]{2,1,0:T(8,128)(2,1)S(1)}, u32[]{:S(2)}, u32[]{:S(2)}) collective-permute-start(bf16[2,40,128]{2,1,0:T(8,128)(2,1)S(1)} %get-tuple-element.30), channel_id=1, source_target_pairs={{0,8},{8,0},{16,24},{24,16},{1,9},{9,1},{17,25},{25,17},{2,10},{10... | collective-permute-start | bytes 61448 | tf_op jit(solution)/shard_map/ppermute | solution.py:36
  47.5 1.3 %collective-permute-start.16 = (bf16[2,40,128]{2,1,0:T(8,128)(2,1)S(1)}, bf16[2,40,128]{2,1,0:T(8,128)(2,1)S(1)}, u32[]{:S(2)}, u32[]{:S(2)}) collective-permute-start(bf16[2,40,128]{2,1,0:T(8,128)(2,1)S(1)} %get-tuple-element.31), channel_id=1, source_target_pairs={{0,16},{8,24},{16,0},{24,8},{1,17},{9,25},{17,1},{25,9},{2,18},{10... | collective-permute-start | bytes 61448 | tf_op jit(solution)/shard_map/ppermute | solution.py:36
  48.8 1.5 %collective-permute-start.17 = (bf16[2,40,128]{2,1,0:T(8,128)(2,1)S(1)}, bf16[2,40,128]{2,1,0:T(8,128)(2,1)S(1)}, u32[]{:S(2)}, u32[]{:S(2)}) collective-permute-start(bf16[2,40,128]{2,1,0:T(8,128)(2,1)S(1)} %get-tuple-element.32), channel_id=1, source_target_pairs={{0,24},{8,16},{16,8},{24,0},{1,25},{9,17},{17,9},{25,1},{2,26},{10... | collective-permute-start | bytes 61448 | tf_op jit(solution)/shard_map/ppermute | solution.py:36
  50.3 0.5 collective-permute-done.15.refs_1_
  50.7 0.7 %collective-permute-done.16.refs_2_ = bf16[2,40,128]{2,1,0:T(8,128)(2,1)S(1)} collective-permute-done((bf16[2,40,128]{2,1,0:T(8,128)(2,1)S(1)}, bf16[2,40,128]{2,1,0:T(8,128)(2,1)S(1)}, u32[]{:S(2)}, u32[]{:S(2)}) %collective-permute-start.16) | collective-permute-done | bytes 20512 | tf_op jit(solution)/shard_map/ppermute | solution.py:36
  51.5 2.0 %collective-permute-done.17.refs_3_ = bf16[2,40,128]{2,1,0:T(8,128)(2,1)S(1)} collective-permute-done((bf16[2,40,128]{2,1,0:T(8,128)(2,1)S(1)}, bf16[2,40,128]{2,1,0:T(8,128)(2,1)S(1)}, u32[]{:S(2)}, u32[]{:S(2)}) %collective-permute-start.17) | collective-permute-done | bytes 20512 | tf_op jit(solution)/shard_map/ppermute | solution.py:36
  53.5 1.0 %shard_map.79 = bf16[2,10,4,384]{3,2,1,0:T(4,128)(2,1)} custom-call(bf16[2,40,128]{2,1,0:T(8,128)(2,1)S(1)} %get-tuple-element.29.refs_0_, bf16[2,40,128]{2,1,0:T(8,128)(2,1)S(1)} %collective-permute-done.15.refs_1_, bf16[2,40,128]{2,1,0:T(8,128)(2,1)S(1)} %collective-permute-done.16.refs_2_, bf16[2,40,128]{2,1,0:T(8,128)(2,1)S(1)} %collective-permute-done.17.refs_3_, ...), custom_call_target="tpu_custom_call" | custom-call | bytes 267776 | tf_op jit(solution)/shard_map/pallas_call | solution.py:488
  (49 shorter events, 1.0 us)
Async XLA Ops:
  0.9 0.7 %copy-start.7 = (f32[384]{0:T(512)S(1)}, f32[384]{0:T(512)}, u32[]{:S(2)}) copy-start(f32[384]{0:T(512)} %refs_6_.3) | copy-start | bytes 4612
  2.1 15.3 %copy-start = (bf16[3,3,3,96,384]{4,3,2,1,0:T(8,128)(2,1)S(1)}, bf16[3,3,3,96,384]{4,3,2,1,0:T(8,128)(2,1)}, u32[]{:S(2)}) copy-start(bf16[3,3,3,96,384]{4,3,2,1,0:T(8,128)(2,1)} %refs_2_.3) | copy-start | bytes 5971972
  2.1 4.5 %collective-permute-start = (bf16[2,40,512]{2,1,0:T(8,128)(2,1)S(1)}, bf16[2,40,512]{2,1,0:T(8,128)(2,1)S(1)}, u32[]{:S(2)}, u32[]{:S(2)}) collective-permute-start(bf16[2,40,512]{2,1,0:T(8,128)(2,1)S(1)} %get-tuple-element.20), channel_id=1, source_target_pairs={{0,8},{8,0},{16,24},{24,16},{1,9},{9,1},{17,25},{25,17},{2,10},{10... | collective-permute-start | bytes 245768 | tf_op jit(solution)/shard_map/ppermute | solution.py:36
  3.7 5.3 %collective-permute-start.1 = (bf16[2,40,512]{2,1,0:T(8,128)(2,1)S(1)}, bf16[2,40,512]{2,1,0:T(8,128)(2,1)S(1)}, u32[]{:S(2)}, u32[]{:S(2)}) collective-permute-start(bf16[2,40,512]{2,1,0:T(8,128)(2,1)S(1)} %get-tuple-element.21), channel_id=1, source_target_pairs={{0,16},{8,24},{16,0},{24,8},{1,17},{9,25},{17,1},{25,9},{2,18},{10... | collective-permute-start | bytes 245768 | tf_op jit(solution)/shard_map/ppermute | solution.py:36
  5.2 5.3 %collective-permute-start.2 = (bf16[2,40,512]{2,1,0:T(8,128)(2,1)S(1)}, bf16[2,40,512]{2,1,0:T(8,128)(2,1)S(1)}, u32[]{:S(2)}, u32[]{:S(2)}) collective-permute-start(bf16[2,40,512]{2,1,0:T(8,128)(2,1)S(1)} %get-tuple-element.22), channel_id=1, source_target_pairs={{0,24},{8,16},{16,8},{24,0},{1,25},{9,17},{17,9},{25,1},{2,26},{10... | collective-permute-start | bytes 245768 | tf_op jit(solution)/shard_map/ppermute | solution.py:36
  10.6 1.3 %collective-permute-start.3 = (bf16[4,2,4,512]{3,2,1,0:T(4,128)(2,1)S(1)}, bf16[4,2,4,512]{3,2,1,0:T(4,128)(2,1)S(1)}, u32[]{:S(2)}, u32[]{:S(2)}) collective-permute-start(bf16[4,2,4,512]{3,2,1,0:T(4,128)(2,1)S(1)} %maximum_select_fusion), channel_id=1, source_target_pairs={{0,1},{1,0},{2,3},{3,2},{4,5},{5,4},{6,7},{7,6},{8,9},{9,8},{10,11... | collective-permute-start | bytes 98312 | tf_op jit(solution)/shard_map/ppermute | solution.py:52
  12.3 9.5 %collective-permute-start.4 = (bf16[4,2,12,512]{3,2,1,0:T(8,128)(2,1)S(1)}, bf16[4,2,12,512]{3,2,1,0:T(8,128)(2,1)S(1)}, u32[]{:S(2)}, u32[]{:S(2)}) collective-permute-start(bf16[4,2,12,512]{3,2,1,0:T(8,128)(2,1)S(1)} %broadcast_select_fusion.1), channel_id=1, source_target_pairs={{0,2},{4,6},{2,0},{6,4},{1,3},{5,7},{3,1},{7,5},{8,10},{12,14},{10... | collective-permute-start | bytes 294920 | tf_op jit(solution)/shard_map/ppermute | solution.py:52
  12.8 9.0 %collective-permute-start.5 = (bf16[4,2,12,512]{3,2,1,0:T(8,128)(2,1)S(1)}, bf16[4,2,12,512]{3,2,1,0:T(8,128)(2,1)S(1)}, u32[]{:S(2)}, u32[]{:S(2)}) collective-permute-start(bf16[4,2,12,512]{3,2,1,0:T(8,128)(2,1)S(1)} %broadcast_select_fusion), channel_id=1, source_target_pairs={{2,4},{4,2},{3,5},{5,3},{10,12},{12,10},{11,13},{13,11},{18,20},{2... | collective-permute-start | bytes 294920 | tf_op jit(solution)/shard_map/ppermute | solution.py:52
  17.4 1.6 %copy-start.1 = (bf16[3,3,3,96,384]{4,3,2,1,0:T(8,128)(2,1)S(1)}, bf16[3,3,3,96,384]{4,3,2,1,0:T(8,128)(2,1)}, u32[]{:S(2)}) copy-start(bf16[3,3,3,96,384]{4,3,2,1,0:T(8,128)(2,1)} %refs_3_.1) | copy-start | bytes 5971972
  19.0 2.8 %copy-start.2 = (bf16[3,3,3,96,384]{4,3,2,1,0:T(8,128)(2,1)S(1)}, bf16[3,3,3,96,384]{4,3,2,1,0:T(8,128)(2,1)}, u32[]{:S(2)}) copy-start(bf16[3,3,3,96,384]{4,3,2,1,0:T(8,128)(2,1)} %refs_3_.1) | copy-start | bytes 5971972
  21.8 8.0 %copy-start.5 = (f32[384]{0:T(512)S(1)}, f32[384]{0:T(512)}, u32[]{:S(2)}) copy-start(f32[384]{0:T(512)} %refs_4_.1) | copy-start | bytes 4612
  21.8 8.0 %copy-start.6 = (f32[384]{0:T(512)S(1)}, f32[384]{0:T(512)}, u32[]{:S(2)}) copy-start(f32[384]{0:T(512)} %refs_5_.4) | copy-start | bytes 4612
  23.1 5.3 %collective-permute-start.6 = (bf16[2,40,512]{2,1,0:T(8,128)(2,1)S(1)}, bf16[2,40,512]{2,1,0:T(8,128)(2,1)S(1)}, u32[]{:S(2)}, u32[]{:S(2)}) collective-permute-start(bf16[2,40,512]{2,1,0:T(8,128)(2,1)S(1)} %get-tuple-element.26), channel_id=1, source_target_pairs={{0,8},{8,0},{16,24},{24,16},{1,9},{9,1},{17,25},{25,17},{2,10},{10... | collective-permute-start | bytes 245768 | tf_op jit(solution)/shard_map/ppermute | solution.py:36
  23.7 5.2 %collective-permute-start.7 = (bf16[2,40,512]{2,1,0:T(8,128)(2,1)S(1)}, bf16[2,40,512]{2,1,0:T(8,128)(2,1)S(1)}, u32[]{:S(2)}, u32[]{:S(2)}) collective-permute-start(bf16[2,40,512]{2,1,0:T(8,128)(2,1)S(1)} %get-tuple-element.27), channel_id=1, source_target_pairs={{0,16},{8,24},{16,0},{24,8},{1,17},{9,25},{17,1},{25,9},{2,18},{10... | collective-permute-start | bytes 245768 | tf_op jit(solution)/shard_map/ppermute | solution.py:36
  24.5 5.3 %collective-permute-start.8 = (bf16[2,40,512]{2,1,0:T(8,128)(2,1)S(1)}, bf16[2,40,512]{2,1,0:T(8,128)(2,1)S(1)}, u32[]{:S(2)}, u32[]{:S(2)}) collective-permute-start(bf16[2,40,512]{2,1,0:T(8,128)(2,1)S(1)} %get-tuple-element.28), channel_id=1, source_target_pairs={{0,24},{8,16},{16,8},{24,0},{1,25},{9,17},{17,9},{25,1},{2,26},{10... | collective-permute-start | bytes 245768 | tf_op jit(solution)/shard_map/ppermute | solution.py:36
  30.2 5.2 %collective-permute-start.11 = (bf16[2,40,384]{2,1,0:T(8,128)(2,1)S(1)}, bf16[2,40,384]{2,1,0:T(8,128)(2,1)S(1)}, u32[]{:S(2)}, u32[]{:S(2)}) collective-permute-start(bf16[2,40,384]{2,1,0:T(8,128)(2,1)S(1)} %shard_map.76.refs_0_), channel_id=1, source_target_pairs={{0,24},{8,16},{16,8},{24,0},{1,25},{9,17},{17,9},{25,1},{2,26},{10... | collective-permute-start | bytes 184328 | tf_op jit(solution)/shard_map/ppermute | solution.py:36
  32.5 4.3 %collective-permute-start.10 = (bf16[2,40,384]{2,1,0:T(8,128)(2,1)S(1)}, bf16[2,40,384]{2,1,0:T(8,128)(2,1)S(1)}, u32[]{:S(2)}, u32[]{:S(2)}) collective-permute-start(bf16[2,40,384]{2,1,0:T(8,128)(2,1)S(1)} %shard_map.76.refs_0_), channel_id=1, source_target_pairs={{0,16},{8,24},{16,0},{24,8},{1,17},{9,25},{17,1},{25,9},{2,18},{10... | collective-permute-start | bytes 184328 | tf_op jit(solution)/shard_map/ppermute | solution.py:36
  33.1 4.2 %collective-permute-start.9 = (bf16[2,40,384]{2,1,0:T(8,128)(2,1)S(1)}, bf16[2,40,384]{2,1,0:T(8,128)(2,1)S(1)}, u32[]{:S(2)}, u32[]{:S(2)}) collective-permute-start(bf16[2,40,384]{2,1,0:T(8,128)(2,1)S(1)} %shard_map.76.refs_0_), channel_id=1, source_target_pairs={{0,8},{8,0},{16,24},{24,16},{1,9},{9,1},{17,25},{25,17},{2,10},{10... | collective-permute-start | bytes 184328 | tf_op jit(solution)/shard_map/ppermute | solution.py:36
  37.4 1.3 %collective-permute-start.12 = (bf16[4,2,4,384]{3,2,1,0:T(4,128)(2,1)S(1)}, bf16[4,2,4,384]{3,2,1,0:T(4,128)(2,1)S(1)}, u32[]{:S(2)}, u32[]{:S(2)}) collective-permute-start(bf16[4,2,4,384]{3,2,1,0:T(4,128)(2,1)S(1)} %maximum_select_fusion.1), channel_id=1, source_target_pairs={{0,1},{1,0},{2,3},{3,2},{4,5},{5,4},{6,7},{7,6},{8,9},{9,8},{10,11... | collective-permute-start | bytes 73736 | tf_op jit(solution)/shard_map/ppermute | solution.py:52
  39.0 14.5 %copy-start.3 = (bf16[2,4,10,384]{3,1,2,0:T(4,128)(2,1)S(1)}, bf16[2,4,10,384]{3,1,2,0:T(4,128)(2,1)}, u32[]{:S(2)}) copy-start(bf16[2,4,10,384]{3,1,2,0:T(4,128)(2,1)} %param.8) | copy-start | bytes 184324
  39.0 14.5 %copy-start.4 = (bf16[2,4,10,384]{3,1,2,0:T(4,128)(2,1)S(1)}, bf16[2,4,10,384]{3,1,2,0:T(4,128)(2,1)}, u32[]{:S(2)}) copy-start(bf16[2,4,10,384]{3,1,2,0:T(4,128)(2,1)} %param.7) | copy-start | bytes 184324
  39.0 14.4 %copy-start.8 = (f32[384]{0:T(512)S(1)}, f32[384]{0:T(512)}, u32[]{:S(2)}) copy-start(f32[384]{0:T(512)} %refs_6_.3) | copy-start | bytes 4612
  39.0 4.9 %collective-permute-start.13 = (bf16[4,2,12,384]{3,2,1,0:T(8,128)(2,1)S(1)}, bf16[4,2,12,384]{3,2,1,0:T(8,128)(2,1)S(1)}, u32[]{:S(2)}, u32[]{:S(2)}) collective-permute-start(bf16[4,2,12,384]{3,2,1,0:T(8,128)(2,1)S(1)} %broadcast_select_fusion.3), channel_id=1, source_target_pairs={{0,2},{4,6},{2,0},{6,4},{1,3},{5,7},{3,1},{7,5},{8,10},{12,14},{10... | collective-permute-start | bytes 221192 | tf_op jit(solution)/shard_map/ppermute | solution.py:52
  39.1 6.8 %collective-permute-start.14 = (bf16[4,2,12,384]{3,2,1,0:T(8,128)(2,1)S(1)}, bf16[4,2,12,384]{3,2,1,0:T(8,128)(2,1)S(1)}, u32[]{:S(2)}, u32[]{:S(2)}) collective-permute-start(bf16[4,2,12,384]{3,2,1,0:T(8,128)(2,1)S(1)} %broadcast_select_fusion.2), channel_id=1, source_target_pairs={{2,4},{4,2},{3,5},{5,3},{10,12},{12,10},{11,13},{13,11},{18,20},{2... | collective-permute-start | bytes 221192 | tf_op jit(solution)/shard_map/ppermute | solution.py:52
  46.7 4.0 %collective-permute-start.15 = (bf16[2,40,128]{2,1,0:T(8,128)(2,1)S(1)}, bf16[2,40,128]{2,1,0:T(8,128)(2,1)S(1)}, u32[]{:S(2)}, u32[]{:S(2)}) collective-permute-start(bf16[2,40,128]{2,1,0:T(8,128)(2,1)S(1)} %get-tuple-element.30), channel_id=1, source_target_pairs={{0,8},{8,0},{16,24},{24,16},{1,9},{9,1},{17,25},{25,17},{2,10},{10... | collective-permute-start | bytes 61448 | tf_op jit(solution)/shard_map/ppermute | solution.py:36
  47.5 4.0 %collective-permute-start.16 = (bf16[2,40,128]{2,1,0:T(8,128)(2,1)S(1)}, bf16[2,40,128]{2,1,0:T(8,128)(2,1)S(1)}, u32[]{:S(2)}, u32[]{:S(2)}) collective-permute-start(bf16[2,40,128]{2,1,0:T(8,128)(2,1)S(1)} %get-tuple-element.31), channel_id=1, source_target_pairs={{0,16},{8,24},{16,0},{24,8},{1,17},{9,25},{17,1},{25,9},{2,18},{10... | collective-permute-start | bytes 61448 | tf_op jit(solution)/shard_map/ppermute | solution.py:36
  48.8 4.7 %collective-permute-start.17 = (bf16[2,40,128]{2,1,0:T(8,128)(2,1)S(1)}, bf16[2,40,128]{2,1,0:T(8,128)(2,1)S(1)}, u32[]{:S(2)}, u32[]{:S(2)}) collective-permute-start(bf16[2,40,128]{2,1,0:T(8,128)(2,1)S(1)} %get-tuple-element.32), channel_id=1, source_target_pairs={{0,24},{8,16},{16,8},{24,0},{1,25},{9,17},{17,9},{25,1},{2,26},{10... | collective-permute-start | bytes 61448 | tf_op jit(solution)/shard_map/ppermute | solution.py:36
